TPU v7x, 512 devices: a whole 4x4x16 slice. The times are simulated.
512 devices in a mesh: section: 8 (over x, core), dp: 16 (over z), tensor: 4 (over y).
Axes of the slice: x: 4, y: 4, z: 16, core: 2. Of those that a mesh axis runs over, the one named last changes fastest.
Arguments:
- arrived: bfloat16 [16384, 8192], P(('section', 'dp'), 'tensor'), may hold values from -10 to 10
- cot_later: bfloat16 [16384, 8192], P(('section', 'dp'), 'tensor'), may hold values from -6 to 6
- q_base: bfloat16 [2, 16384, 8192], P(None, ('section', 'dp'), 'tensor'), may hold values from -121 to 121
- k_base: bfloat16 [2, 16384, 1024], P(None, ('section', 'dp'), 'tensor'), may hold values from -7 to 7
- v_base: bfloat16 [2, 16384, 1024], P(None, ('section', 'dp'), 'tensor'), may hold values from -6 to 6
- gains: float32 [16, 8192], P('section', 'tensor'), may hold values from 0.5 to 1.5
- parents: int32 [16384], P(('section', 'dp')), may hold values from -1 to 126, as said below
- a_query: bfloat16 [16, 8192, 128], P('section', ('tensor', 'dp')), may hold values from -0.0625 to 0.0625
- b_query: bfloat16 [16, 128, 8192], P('section', 'dp', 'tensor'), may hold values from -0.5 to 0.5
- a_out: bfloat16 [16, 8192, 128], P('section', ('tensor', 'dp')), may hold values from -0.0625 to 0.0625
- b_out: bfloat16 [16, 128, 8192], P('section', 'dp', 'tensor'), may hold values from -0.5 to 0.5
Outputs:
- section_out: bfloat16 [16384, 8192], P(('section', 'dp'), 'tensor')
- cot_send: bfloat16 [16384, 8192], P(('section', 'dp'), 'tensor')
- grad_a_query: float32 [16, 8192, 128], P('section', ('tensor', 'dp'))
- grad_b_query: float32 [16, 128, 8192], P('section', 'dp', 'tensor')
- grad_a_out: float32 [16, 8192, 128], P('section', ('tensor', 'dp'))
- grad_b_out: float32 [16, 128, 8192], P('section', 'dp', 'tensor')
Inputs may be any that keep to these rules, and one draw needn't show every extreme that they name: `parents`: within each block of 128 tokens the first token's parent is -1 and every other token's parent is an earlier index of the same block, at most 12 before it.
All inputs are finite; a program needn't handle non-finite values.
Results may differ from a plain program's by a relative error of at most 0.04.
Values may be sent and summed in bfloat16 or wider, within the bound.
No kernel may reach another device: no remote copies, remote signals or barrier semaphores. Data moves between devices by JAX's collectives and lax.ppermute only.
A program may use at most 64 MiB of HBM per device.

v0:
```python
import jax
import jax.numpy as jnp
from jax import lax
from jax.sharding import PartitionSpec as P

D = 8192
HEAD_DIM = 128


EPSILON = 1e-05


def from_behind(value, axis, steps):
    count = lax.axis_size(axis)
    pairs = [(source, (source + steps) % count) for source in range(count)]
    return lax.ppermute(value, axis, pairs)


def contract_rows(left, right):
    return lax.dot_general(
        left, right, (((0,), (0,)), ((), ())), preferred_element_type=jnp.float32
    )


def contract_cols(left, right):
    return lax.dot_general(
        left, right, (((1,), (1,)), ((), ())), preferred_element_type=jnp.float32
    )


def tree_mask(parent_links):
    token_count = parent_links.shape[0]
    position = jnp.arange(token_count, dtype=jnp.int32)
    linked = (position[:, None] == position[None, :]) | (parent_links[:, None] == position[None, :])
    reached = linked.astype(jnp.bfloat16)
    for doubling in range(max(1, (token_count - 1).bit_length())):
        reached = jnp.minimum(
            jnp.dot(reached, reached, preferred_element_type=jnp.float32), 1.0
        ).astype(jnp.bfloat16)
    return reached > 0.5


def attend(queries, key_rows, value_rows, allowed):
    token_count = queries.shape[0]
    groups = key_rows.shape[1] // HEAD_DIM
    query_heads = queries.reshape(token_count, groups, -1, HEAD_DIM)
    key_heads = key_rows.reshape(token_count, groups, HEAD_DIM)
    value_heads = value_rows.reshape(token_count, groups, HEAD_DIM)
    scores = jnp.einsum(
        "tgjd,ugd->gjtu", query_heads, key_heads, preferred_element_type=jnp.float32
    ) * HEAD_DIM ** (-0.5)
    scores = jnp.where(allowed[None, None], scores, -1e30)
    highest = jnp.max(scores, axis=-1, keepdims=True)
    weights = jnp.exp(scores - highest)
    probability = weights / jnp.sum(weights, axis=-1, keepdims=True)
    mixed_out = jnp.einsum(
        "gjtu,ugd->tgjd",
        probability.astype(jnp.bfloat16),
        value_heads,
        preferred_element_type=jnp.float32,
    )
    return (probability, mixed_out.reshape(token_count, -1).astype(jnp.bfloat16))


def attend_back(back_mixed, probability, key_rows, value_rows):
    token_count = back_mixed.shape[0]
    groups = key_rows.shape[1] // HEAD_DIM
    back_heads = back_mixed.reshape(token_count, groups, -1, HEAD_DIM)
    key_heads = key_rows.reshape(token_count, groups, HEAD_DIM)
    value_heads = value_rows.reshape(token_count, groups, HEAD_DIM)
    back_prob = jnp.einsum(
        "tgjd,ugd->gjtu", back_heads, value_heads, preferred_element_type=jnp.float32
    )
    back_scores = probability * (
        back_prob - jnp.sum(probability * back_prob, axis=-1, keepdims=True)
    )
    back_query = jnp.einsum(
        "gjtu,ugd->tgjd",
        back_scores.astype(jnp.bfloat16),
        key_heads,
        preferred_element_type=jnp.float32,
    ) * HEAD_DIM ** (-0.5)
    return back_query.reshape(token_count, -1).astype(jnp.bfloat16)


def forward_layer(hidden, gain_row, adapter_set, query_base, key_rows, value_rows, allowed):
    down_query, up_query, down_output, up_output = adapter_set
    local_squares = jnp.sum(hidden * hidden, axis=1)
    unscaled = (hidden * gain_row[None, :]).astype(jnp.bfloat16)
    local_projection = jnp.dot(unscaled, down_query, preferred_element_type=jnp.float32)
    square_total = lax.psum(local_squares, "tensor")
    projected = lax.psum(local_projection.astype(jnp.bfloat16), "tensor").astype(jnp.float32)
    scale_rows = lax.rsqrt(square_total / D + EPSILON)
    rank_query = (scale_rows[:, None] * projected).astype(jnp.bfloat16)
    normed = (hidden * scale_rows[:, None] * gain_row[None, :]).astype(jnp.bfloat16)
    queries = (
        query_base.astype(jnp.float32)
        + jnp.dot(rank_query, up_query, preferred_element_type=jnp.float32)
    ).astype(jnp.bfloat16)
    probability, attended = attend(queries, key_rows, value_rows, allowed)
    rank_output = lax.psum(
        jnp.dot(attended, down_output, preferred_element_type=jnp.float32).astype(jnp.bfloat16),
        "tensor",
    )
    hidden_next = hidden + jnp.dot(rank_output, up_output, preferred_element_type=jnp.float32)
    return (
        hidden_next,
        (hidden, scale_rows, normed, projected, rank_query, probability, attended, rank_output),
    )


def backward_layer(gradient, kept_values, gain_row, adapter_set, key_rows, value_rows):
    hidden, scale_rows, normed, projected, rank_query, probability, attended, rank_output = (
        kept_values
    )
    down_query, up_query, down_output, up_output = adapter_set
    grad_bf = gradient.astype(jnp.bfloat16)
    term_b_out = contract_rows(rank_output, grad_bf)
    back_rank_output = lax.psum(contract_cols(grad_bf, up_output).astype(jnp.bfloat16), "tensor")
    term_a_out = contract_rows(attended, back_rank_output)
    back_attended = contract_cols(back_rank_output, down_output).astype(jnp.bfloat16)
    back_query = attend_back(back_attended, probability, key_rows, value_rows)
    term_b_query = contract_rows(rank_query, back_query)
    back_rank_query = lax.psum(contract_cols(back_query, up_query).astype(jnp.bfloat16), "tensor")
    term_a_query = contract_rows(normed, back_rank_query)
    gained = gain_row[None, :] * contract_cols(back_rank_query, down_query)
    along_norm = jnp.sum(back_rank_query.astype(jnp.float32) * projected, axis=1) / D
    gradient_next = (
        gradient + scale_rows[:, None] * gained - hidden * (scale_rows**3 * along_norm)[:, None]
    )
    return (gradient_next, (term_a_query, term_b_query, term_a_out, term_b_out))


def fetch_layer(a_query, b_query, a_out, b_out, layer_index):
    return (
        lax.all_gather(a_query[layer_index], "dp", axis=0, tiled=True),
        lax.all_gather(b_query[layer_index], "dp", axis=0, tiled=True),
        lax.all_gather(a_out[layer_index], "dp", axis=0, tiled=True),
        lax.all_gather(b_out[layer_index], "dp", axis=0, tiled=True),
    )


def on_device(
    arrived, cot_later, q_base, k_base, v_base, gains, parents, a_query, b_query, a_out, b_out
):
    layer_count = q_base.shape[0]
    current = from_behind(arrived, "section", 1)
    returned = from_behind(cot_later, "section", -1)
    allowed = tree_mask(parents)
    adapter_sets = [
        fetch_layer(a_query, b_query, a_out, b_out, layer_index)
        for layer_index in range(layer_count)
    ]
    hidden = current.astype(jnp.float32)
    kept_list = []
    for layer_index in range(layer_count):
        hidden, kept_values = forward_layer(
            hidden,
            gains[layer_index],
            adapter_sets[layer_index],
            q_base[layer_index],
            k_base[layer_index],
            v_base[layer_index],
            allowed,
        )
        kept_list.append(kept_values)
    section_out = hidden.astype(jnp.bfloat16)
    gradient = returned.astype(jnp.float32)
    partials = [None] * layer_count
    for layer_index in reversed(range(layer_count)):
        gradient, partials[layer_index] = backward_layer(
            gradient,
            kept_list[layer_index],
            gains[layer_index],
            adapter_sets[layer_index],
            k_base[layer_index],
            v_base[layer_index],
        )
    stacked = [
        jnp.stack([partials[layer_index][member] for layer_index in range(layer_count)])
        for member in range(4)
    ]
    finals = (
        lax.psum_scatter(
            stacked[0].astype(jnp.bfloat16), "dp", scatter_dimension=1, tiled=True
        ).astype(jnp.float32),
        lax.psum_scatter(
            stacked[1].astype(jnp.bfloat16), "dp", scatter_dimension=1, tiled=True
        ).astype(jnp.float32),
        lax.psum_scatter(
            stacked[2].astype(jnp.bfloat16), "dp", scatter_dimension=1, tiled=True
        ).astype(jnp.float32),
        lax.psum_scatter(
            stacked[3].astype(jnp.bfloat16), "dp", scatter_dimension=1, tiled=True
        ).astype(jnp.float32),
    )
    return (section_out, gradient.astype(jnp.bfloat16), finals[0], finals[1], finals[2], finals[3])


def solution(mesh):
    in_specs = (
        P(("section", "dp"), "tensor"),
        P(("section", "dp"), "tensor"),
        P(None, ("section", "dp"), "tensor"),
        P(None, ("section", "dp"), "tensor"),
        P(None, ("section", "dp"), "tensor"),
        P("section", "tensor"),
        P(("section", "dp")),
        P("section", ("tensor", "dp"), None),
        P("section", "dp", "tensor"),
        P("section", ("tensor", "dp"), None),
        P("section", "dp", "tensor"),
    )
    out_specs = (
        P(("section", "dp"), "tensor"),
        P(("section", "dp"), "tensor"),
        P("section", ("tensor", "dp"), None),
        P("section", "dp", "tensor"),
        P("section", ("tensor", "dp"), None),
        P("section", "dp", "tensor"),
    )
    return jax.shard_map(
        on_device, mesh=mesh, in_specs=in_specs, out_specs=out_specs, check_vma=False
    )
```

profile of v0, /device:TPU:4, one launch (start us, length us, event | category | flops | bytes accessed | tf_op | source)
XLA Modules:
  0.0 786.0 jit_solution(3158077006203157411)
XLA Ops:
  7.2 1.7 collective-permute-start.1
  9.0 1.2 fusion.33
  14.8 41.1 %all-gather.7 = bf16[1,128,2048]{2,1,0:T(8,128)(2,1)} all-gather(bf16[1,8,2048]{2,1,0:T(8,128)(2,1)S(1)} %get-tuple-element.16), channel_id=9, replica_groups=mesh['section'=8,'dp'=16,'tensor'=4] {'dp'}, dimensions={1}, use_global_device_ids=true | all-gather | bytes 557056 | tf_op jit(solution)/shard_map/all_gather | solution.py:139
  55.9 31.7 %all-gather.6 = bf16[1,2048,128]{2,1,0:T(8,128)(2,1)} all-gather(bf16[1,128,128]{2,1,0:T(8,128)(2,1)S(1)} %get-tuple-element.14), channel_id=8, replica_groups=mesh['section'=8,'dp'=16,'tensor'=4] {'dp'}, dimensions={1}, use_global_device_ids=true | all-gather | bytes 557056 | tf_op jit(solution)/shard_map/all_gather | solution.py:138
  87.6 30.3 %all-gather.5 = bf16[1,128,2048]{2,1,0:T(8,128)(2,1)S(1)} all-gather(bf16[1,8,2048]{2,1,0:T(8,128)(2,1)S(1)} %get-tuple-element.20), channel_id=7, replica_groups=mesh['section'=8,'dp'=16,'tensor'=4] {'dp'}, dimensions={1}, use_global_device_ids=true | all-gather | bytes 557056 | tf_op jit(solution)/shard_map/all_gather | solution.py:137
  117.9 29.8 %all-gather.4 = bf16[1,2048,128]{2,1,0:T(8,128)(2,1)S(1)} all-gather(bf16[1,128,128]{2,1,0:T(8,128)(2,1)S(1)} %get-tuple-element.18), channel_id=6, replica_groups=mesh['section'=8,'dp'=16,'tensor'=4] {'dp'}, dimensions={1}, use_global_device_ids=true | all-gather | bytes 557056 | tf_op jit(solution)/shard_map/all_gather | solution.py:136
  147.7 29.8 %all-gather.3 = bf16[1,128,2048]{2,1,0:T(8,128)(2,1)S(1)} all-gather(bf16[1,8,2048]{2,1,0:T(8,128)(2,1)S(1)} %get-tuple-element.17), channel_id=5, replica_groups=mesh['section'=8,'dp'=16,'tensor'=4] {'dp'}, dimensions={1}, use_global_device_ids=true | all-gather | bytes 557056 | tf_op jit(solution)/shard_map/all_gather | solution.py:139
  177.5 30.8 %all-gather.2 = bf16[1,2048,128]{2,1,0:T(8,128)(2,1)S(1)} all-gather(bf16[1,128,128]{2,1,0:T(8,128)(2,1)S(1)} %get-tuple-element.15), channel_id=4, replica_groups=mesh['section'=8,'dp'=16,'tensor'=4] {'dp'}, dimensions={1}, use_global_device_ids=true | all-gather | bytes 557056 | tf_op jit(solution)/shard_map/all_gather | solution.py:138
  208.2 28.9 %all-gather.1 = bf16[1,128,2048]{2,1,0:T(8,128)(2,1)S(1)} all-gather(bf16[1,8,2048]{2,1,0:T(8,128)(2,1)S(1)} %get-tuple-element.21), channel_id=3, replica_groups=mesh['section'=8,'dp'=16,'tensor'=4] {'dp'}, dimensions={1}, use_global_device_ids=true | all-gather | bytes 557056 | tf_op jit(solution)/shard_map/all_gather | solution.py:137
  237.1 33.1 %all-gather = bf16[1,2048,128]{2,1,0:T(8,128)(2,1)} all-gather(bf16[1,128,128]{2,1,0:T(8,128)(2,1)S(1)} %get-tuple-element.19), channel_id=2, replica_groups=mesh['section'=8,'dp'=16,'tensor'=4] {'dp'}, dimensions={1}, use_global_device_ids=true | all-gather | bytes 557056 | tf_op jit(solution)/shard_map/all_gather | solution.py:136
  272.5 10.7 %psum.70 = f32[128]{0:T(128)S(1)} all-reduce(f32[128]{0:T(128)S(1)} %fusion.40), channel_id=1, replica_groups=mesh['section'=8,'dp'=16,'tensor'=4] {'tensor'}, use_global_device_ids=true, to_apply=%region_1.0 | all-reduce | flops 128 | bytes 1024 | tf_op jit(solution)/shard_map/psum | solution.py:91
  283.7 1.3 convolution_convert_fusion.19
  285.1 14.4 %psum.71 = bf16[128,128]{1,0:T(8,128)(2,1)S(1)} all-reduce(bf16[128,128]{1,0:T(8,128)(2,1)S(1)} %convolution_convert_fusion.19), channel_id=1, replica_groups=mesh['section'=8,'dp'=16,'tensor'=4] {'tensor'}, use_global_device_ids=true, to_apply=%region_2.0 | all-reduce | flops 16384 | bytes 65536 | tf_op jit(solution)/shard_map/psum | solution.py:92
  299.5 1.4 fusion.31
  301.0 1.5 fusion.122
  302.5 1.5 convolution_convert_fusion.11
  304.9 16.2 %psum.72 = bf16[128,128]{1,0:T(8,128)(2,1)S(1)} all-reduce(bf16[128,128]{1,0:T(8,128)(2,1)S(1)} %convolution_convert_fusion.18), channel_id=1, replica_groups=mesh['section'=8,'dp'=16,'tensor'=4] {'tensor'}, use_global_device_ids=true, to_apply=%region_5.6 | all-reduce | flops 16384 | bytes 65536 | tf_op jit(solution)/shard_map/psum | solution.py:101
  321.4 7.8 psum.73
  329.3 0.9 convolution_convert_fusion.17
  330.3 2.0 convolution_convert_fusion.15
  332.4 50.9 %all-reduce.7.cloned.1.call-done = (bf16[128,128]{1,0:T(8,128)(2,1)}, bf16[128,128]{1,0:T(8,128)(2,1)}) async-done(((bf16[128,128]{1,0:T(8,128)(2,1)}, bf16[128,128]{1,0:T(8,128)(2,1)}), (bf16[128,128]{1,0:T(8,128)(2,1)}, bf16[128,128]{1,0:T(8,128)(2,1)})) %all-reduce.7.cloned.1.call-update) | async-done | bytes 65552 | tf_op jit(solution)/shard_map/psum | solution.py:92
  383.3 1.4 fusion.30
  385.8 1.1 fusion.28
  386.9 2.6 fusion.125
  389.5 1.6 convolution_convert_fusion.10
  391.0 1.0 convolution_convert_fusion.16
  392.0 1.1 fusion.15
  395.5 16.0 %psum.77 = bf16[128,128]{1,0:T(8,128)(2,1)S(1)} all-reduce(bf16[128,128]{1,0:T(8,128)(2,1)S(1)} %convolution_convert_fusion.14), channel_id=1, replica_groups=mesh['section'=8,'dp'=16,'tensor'=4] {'tensor'}, use_global_device_ids=true, to_apply=%region_14.15 | all-reduce | flops 16384 | bytes 65536 | tf_op jit(solution)/shard_map/psum | solution.py:124
  412.1 1.6 multiply_subtract_fusion
  414.0 14.8 %psum.78 = bf16[128,128]{1,0:T(8,128)(2,1)S(1)} all-reduce(bf16[128,128]{1,0:T(8,128)(2,1)S(1)} %convolution_convert_fusion.13), channel_id=1, replica_groups=mesh['section'=8,'dp'=16,'tensor'=4] {'tensor'}, use_global_device_ids=true, to_apply=%region_16.17 | all-reduce | flops 16384 | bytes 65536 | tf_op jit(solution)/shard_map/psum | solution.py:119
  428.8 2.2 fusion.14
  433.7 1.0 convolution_convert_fusion.12
  434.8 2.1 pad_maximum_fusion.2
  439.5 1.1 copy.86
  440.6 1.4 copy.96
  442.4 48.7 %all-reduce.5.cloned.1.call-done = (bf16[128,128]{1,0:T(8,128)(2,1)}, bf16[128,128]{1,0:T(8,128)(2,1)}) async-done(((bf16[128,128]{1,0:T(8,128)(2,1)}, bf16[128,128]{1,0:T(8,128)(2,1)}), (bf16[128,128]{1,0:T(8,128)(2,1)}, bf16[128,128]{1,0:T(8,128)(2,1)})) %all-reduce.5.cloned.1.call-update) | async-done | bytes 65552 | tf_op jit(solution)/shard_map/psum | solution.py:101
  491.1 1.4 fusion.17
  492.6 1.1 copy.88
  493.7 1.4 copy.97
  496.2 1.1 pad_maximum_fusion
  498.4 1.1 fusion.8
  499.5 1.2 fusion.9
  500.6 64.2 %reduce-scatter.11.cloned.1.call-done = bf16[2,128,128]{2,1,0:T(8,128)(2,1)} async-done(((bf16[2,2048,128]{2,1,0:T(8,128)(2,1)}), bf16[2,128,128]{2,1,0:T(8,128)(2,1)}) %reduce-scatter.11.cloned.1.call-update) | async-done | bytes 65552 | tf_op jit(solution)/shard_map/reduce_scatter | solution.py:190
  564.8 1.5 convert_element_type.236
  566.3 69.5 %reduce-scatter.13.cloned.1.call-done = bf16[8,4096]{1,0:T(8,128)(2,1)} async-done(((bf16[128,4096]{1,0:T(8,128)(2,1)}), bf16[8,4096]{1,0:T(8,128)(2,1)}) %reduce-scatter.13.cloned.1.call-update) | async-done | bytes 65552
  637.4 69.3 %reduce-scatter.15.cloned.1.call-done = bf16[8,4096]{1,0:T(8,128)(2,1)} async-done(((bf16[128,4096]{1,0:T(8,128)(2,1)}), bf16[8,4096]{1,0:T(8,128)(2,1)}) %reduce-scatter.15.cloned.1.call-update) | async-done | bytes 65552
  708.2 69.4 %reduce-scatter.9.cloned.1.call-done = bf16[2,128,128]{2,1,0:T(8,128)(2,1)} async-done(((bf16[2,2048,128]{2,1,0:T(8,128)(2,1)}), bf16[2,128,128]{2,1,0:T(8,128)(2,1)}) %reduce-scatter.9.cloned.1.call-update) | async-done | bytes 65552 | tf_op jit(solution)/shard_map/reduce_scatter | solution.py:184
  777.7 1.5 convert_element_type.234
  (133 shorter events, 24.2 us)
Async XLA Ops:
  7.2 376.1 %all-reduce.7.cloned.1.call-start = ((), (), s32[]{:S(2)}) async-start(), calls=%async_computation.9 | async-start | bytes 131072 | tf_op jit(solution)/shard_map/psum | solution.py:92
  7.2 265.0 %collective-permute-start = (bf16[128,2048]{1,0:T(8,128)(2,1)}, bf16[128,2048]{1,0:T(8,128)(2,1)S(1)}, u32[]{:S(2)}, u32[]{:S(2)}) collective-permute-start(bf16[128,2048]{1,0:T(8,128)(2,1)} %param.11), channel_id=1, source_target_pairs={{0,64},{64,128},{128,192},{192,256},{256,320},{320,384},{384,448},... | collective-permute-start | bytes 1572872 | tf_op jit(solution)/shard_map/ppermute | solution.py:16
  7.2 323.0 %collective-permute-start.1 = (bf16[128,2048]{1,0:T(8,128)(2,1)}, bf16[128,2048]{1,0:T(8,128)(2,1)}, u32[]{:S(2)}, u32[]{:S(2)}) collective-permute-start(bf16[128,2048]{1,0:T(8,128)(2,1)} %param.12), channel_id=1, source_target_pairs={{0,448},{64,0},{128,64},{192,128},{256,192},{320,256},{384,320},{4... | collective-permute-start | bytes 1572872 | tf_op jit(solution)/shard_map/ppermute | solution.py:16
  10.4 0.9 copy-start.22
  11.3 0.8 copy-start.23
  12.1 0.8 copy-start.24
  12.1 0.9 copy-start.25
  12.9 0.9 copy-start.20
  13.9 0.9 copy-start.21
  147.7 181.6 %copy-start.4 = (bf16[1,2048,128]{2,1,0:T(8,128)(2,1)}, bf16[1,2048,128]{2,1,0:T(8,128)(2,1)S(1)}, u32[]{:S(2)}) copy-start(bf16[1,2048,128]{2,1,0:T(8,128)(2,1)S(1)} %all-gather.4) | copy-start | bytes 1572868
  208.2 95.8 %copy-start.2 = (bf16[1,2048,128]{2,1,0:T(8,128)(2,1)}, bf16[1,2048,128]{2,1,0:T(8,128)(2,1)S(1)}, u32[]{:S(2)}) copy-start(bf16[1,2048,128]{2,1,0:T(8,128)(2,1)S(1)} %all-gather.2) | copy-start | bytes 1572868
  237.1 62.4 %copy-start = (bf16[1,128,2048]{2,1,0:T(8,128)(2,1)}, bf16[1,128,2048]{2,1,0:T(8,128)(2,1)S(1)}, u32[]{:S(2)}) copy-start(bf16[1,128,2048]{2,1,0:T(8,128)(2,1)S(1)} %all-gather.1) | copy-start | bytes 1572868
  271.5 0.7 copy-start.27
  283.2 0.5 copy-start.28
  302.5 1.5 copy-start.34
  304.0 0.8 copy-start.9
  329.3 3.1 copy-start.30
  329.3 1.0 copy-start.6
  332.3 158.8 %all-reduce.5.cloned.1.call-start = ((), (), s32[]{:S(2)}) async-start(), calls=%async_computation.8 | async-start | bytes 131072 | tf_op jit(solution)/shard_map/psum | solution.py:101
  384.7 1.1 copy-start.5
  384.7 1.1 copy-start.19
  392.0 1.1 copy-start.14
  392.0 1.6 copy-start.33
  393.1 0.9 copy-start.26
  394.7 0.8 copy-start.10
  395.5 16.0 %copy-start.17 = (bf16[128,128]{1,0:T(8,128)(2,1)S(1)}, bf16[128,128]{1,0:T(8,128)(2,1)}, u32[]{:S(2)}) copy-start(bf16[128,128]{1,0:T(8,128)(2,1)} %get-tuple-element.8) | copy-start | bytes 98308
  411.5 0.6 copy-start.31
  428.8 2.2 copy-start.3
  431.0 1.2 copy-start.32
  431.3 0.9 copy-start.35
  432.6 1.1 copy-start.1
  432.9 0.8 copy-start.12
  433.7 1.0 copy-start.15
  434.7 130.1 %reduce-scatter.11.cloned.1.call-start = ((), (), s32[]{:S(2)}) async-start(), calls=%async_computation.5 | async-start | bytes 1114112 | tf_op jit(solution)/shard_map/reduce_scatter | solution.py:190
  436.9 1.0 copy-start.11
  436.9 198.9 %reduce-scatter.13.cloned.1.call-start = ((), (), s32[]{:S(2)}) async-start(), calls=%async_computation.6 | async-start | bytes 1114112
  437.9 1.0 copy-start.13
  442.0 264.7 %reduce-scatter.15.cloned.1.call-start = ((), (), s32[]{:S(2)}) async-start(), calls=%async_computation.7 | async-start | bytes 1114112
  495.1 0.8 copy-start.16
  495.1 282.6 %reduce-scatter.9.cloned.1.call-start = ((), (), s32[]{:S(2)}) async-start(), calls=%async_computation.4 | async-start | bytes 1114112 | tf_op jit(solution)/shard_map/reduce_scatter | solution.py:184
  497.3 1.0 copy-start.7
  497.3 0.7 copy-start.29
  497.4 1.0 copy-start.18
  498.4 1.1 copy-start.8
Sparse Core Ops, SparseCore 0:
  332.4 50.8 all-reduce.6
  434.8 56.2 all-reduce.4
  493.9 70.8 reduce-scatter.10
  567.7 68.0 reduce-scatter.12
  638.5 68.1 reduce-scatter.14
  709.6 68.0 reduce-scatter.8
where the time goes:
time: 788 us; the launch traced here: 786 us
  waiting for transfers between devices  372 us (47%)
  blocking collectives  335 us (43%)
  matrix products  32.4 us (4%)
  local copies, waits for them, and re-layouts  21 us (3%)
  between operations  14.6 us (2%)
  other arithmetic  8.18 us (1%)
    unnamed x8, waiting for transfers between devices  139 us
    all_gather x2, blocking collectives, fetch_layer(): lax.all_gather(b_out[layer_index], 'dp', axis=0, tiled=True)  70.9 us
    reduce_scatter x1, waiting for transfers between devices, on_device(): lax.psum_scatter(stacked[0].astype(jnp.bfloat16), 'dp', scatter_dimension...  69.4 us
    reduce_scatter x1, waiting for transfers between devices, on_device(): lax.psum_scatter(stacked[2].astype(jnp.bfloat16), 'dp', scatter_dimension...  64.2 us
    all_gather x2, blocking collectives, fetch_layer(): lax.all_gather(a_query[layer_index], 'dp', axis=0, tiled=True)  62.9 us
    all_gather x2, blocking collectives, fetch_layer(): lax.all_gather(a_out[layer_index], 'dp', axis=0, tiled=True)  62.5 us
    all_gather x2, blocking collectives, fetch_layer(): lax.all_gather(b_query[layer_index], 'dp', axis=0, tiled=True)  59.2 us
    psum x1, waiting for transfers between devices, forward_layer(): lax.psum(local_projection.astype(jnp.bfloat16), 'tensor')  50.9 us
  transfers between devices with their start and end apart: 8, of which 6 were waited for; matrix products, arithmetic and copies ran while one was open for 4% of the time, Pallas kernels for 0%

commit v1 on v0

v1 whole, which is shorter than its diff:
```python
import functools

import jax
import jax.numpy as jnp
from jax import lax
from jax.experimental import pallas as pl
from jax.experimental.pallas import tpu as pltpu
from jax.sharding import PartitionSpec as P

D = 8192
HEAD_DIM = 128
EPSILON = 1e-05
F32 = jnp.float32
BF16 = jnp.bfloat16
VMEM_LIMIT = 12 << 20
A_OUT0, B_OUT0, A_QUERY1, B_OUT1, B_QUERY1, A_OUT1 = range(6)


def from_behind(value, axis, steps):
    count = lax.axis_size(axis)
    pairs = [(source, (source + steps) % count) for source in range(count)]
    return lax.ppermute(value, axis, pairs)


def dot(left, right):
    return jnp.dot(left, right, preferred_element_type=F32)


def dot_rows(left, right):
    return lax.dot_general(left, right, (((0,), (0,)), ((), ())), preferred_element_type=F32)


def dot_cols(left, right):
    return lax.dot_general(left, right, (((1,), (1,)), ((), ())), preferred_element_type=F32)


def row_sum(value):
    return jnp.sum(value, axis=1, keepdims=True)


def kernel_call(body, out_shape, operands, flops=4e8):
    size = sum(x.size * x.dtype.itemsize for x in (*operands, *out_shape))
    return pl.pallas_call(
        body,
        out_shape=out_shape,
        in_specs=[pl.BlockSpec(memory_space=pltpu.VMEM)] * len(operands),
        out_specs=[pl.BlockSpec(memory_space=pltpu.VMEM)] * len(out_shape),
        compiler_params=pltpu.CompilerParams(vmem_limit_bytes=VMEM_LIMIT),
        cost_estimate=pl.CostEstimate(flops=int(flops), bytes_accessed=size, transcendentals=0),
    )(*operands)


def shape(dims, dtype):
    return jax.ShapeDtypeStruct(dims, dtype)


def pack_up(block):
    rows, width = block.shape
    return block.reshape(rows, width // 128, 128).transpose(1, 0, 2).reshape(-1, 128)


def unpack_up(block, rows):
    tiles = block.shape[0] // rows
    return block.reshape(tiles, rows, 128).transpose(1, 0, 2).reshape(rows, tiles * 128)


def read_down(stack_ref, member):
    value = stack_ref[:, member]
    return value.reshape(-1, 128)


def read_up(stack_ref, member):
    count, _, length, _ = stack_ref.shape
    rows = 128 // count
    columns = []
    for pair in range(length // (2 * rows)):
        slab = stack_ref[:, member, pair * 2 * rows : (pair + 1) * 2 * rows, :].astype(F32)
        for half in range(2):
            columns.append(
                slab[:, half * rows : (half + 1) * rows, :].reshape(128, 128).astype(BF16)
            )
    return jnp.concatenate(columns, axis=1)


def write_down(stack_ref, member, value):
    count = stack_ref.shape[0]
    stack_ref[:, member] = value.astype(BF16).reshape(count, -1, 128)


def write_up(stack_ref, member, value):
    count, _, length, _ = stack_ref.shape
    rows = 128 // count
    for pair in range(length // (2 * rows)):
        halves = [
            value[:, (2 * pair + half) * 128 : (2 * pair + half + 1) * 128].reshape(
                count, rows, 128
            )
            for half in range(2)
        ]
        stack_ref[:, member, pair * 2 * rows : (pair + 1) * 2 * rows, :] = jnp.concatenate(
            halves, axis=1
        ).astype(BF16)


def to_column(row):
    lane = lax.broadcasted_iota(jnp.int32, (128, 128), 1)
    line = lax.broadcasted_iota(jnp.int32, (128, 128), 0)
    return row_sum(jnp.where(lane == line, jnp.broadcast_to(row, (128, 128)), 0.0))


def mask_body(parent_ref, mask_ref):
    lane = lax.broadcasted_iota(jnp.int32, (128, 128), 1)
    line = lax.broadcasted_iota(jnp.int32, (128, 128), 0)
    linked = (lane == line) | (parent_ref[...] == lane)
    reached = jnp.where(linked, 1.0, 0.0).astype(BF16)
    for _ in range(7):
        reached = jnp.minimum(dot(reached, reached), 1.0).astype(BF16)
    mask_ref[...] = reached.astype(F32)


def first_body(hidden_ref, gain_ref, down_ref, sent_ref):
    hidden = hidden_ref[...].astype(F32)
    projected = dot((hidden * gain_ref[...]).astype(BF16), down_ref[...])
    ones = jnp.ones((8, hidden.shape[1]), F32)
    squares = lax.dot_general(
        ones,
        hidden * hidden,
        (((1,), (1,)), ((), ())),
        preferred_element_type=F32,
        precision=lax.Precision.HIGHEST,
    )
    for peer in range(sent_ref.shape[0]):
        sent_ref[peer, :128, :] = projected
        sent_ref[peer, 128:, :] = squares


def softmax_of(queries, keys, mask):
    scores = jnp.where(mask > 0.5, dot_cols(queries, keys) * HEAD_DIM ** (-0.5), -1e30)
    weights = jnp.exp(scores - jnp.max(scores, axis=1, keepdims=True))
    return weights / row_sum(weights)


def columns_of(index):
    return slice(index * HEAD_DIM, (index + 1) * HEAD_DIM)


def forward0_body(
    came_ref,
    up_ref,
    query_ref,
    key_ref,
    value_ref,
    mask_ref,
    attended_ref,
    probability_ref,
    rank_ref,
    small_ref,
):
    total = came_ref[0]
    for peer in range(1, came_ref.shape[0]):
        total = total + came_ref[peer]
    projected = total[:128]
    squares = to_column(total[128:129])
    scale = lax.rsqrt(squares / D + EPSILON)
    rank_query = (scale * projected).astype(BF16)
    rank_ref[...] = rank_query
    small_ref[0] = projected
    small_ref[1] = jnp.broadcast_to(scale, (128, 128))
    small_ref[2] = jnp.broadcast_to(squares, (128, 128))
    mask = mask_ref[...]
    heads = query_ref.shape[1] // HEAD_DIM
    groups = key_ref.shape[1] // HEAD_DIM
    for head in range(heads):
        at, shared = columns_of(head), columns_of(head // (heads // groups))
        queries = (query_ref[:, at].astype(F32) + dot(rank_query, up_ref[:, at])).astype(BF16)
        probability = softmax_of(queries, key_ref[:, shared], mask)
        probability_ref[head] = probability
        attended_ref[:, at] = dot(probability.astype(BF16), value_ref[:, shared]).astype(BF16)


def second_body(attended_ref, hidden_ref, cot_ref, gain_ref, stack_ref, sent_ref, kept_ref):
    hidden, gain = hidden_ref[...], gain_ref[...]
    up0 = read_up(stack_ref, B_OUT0)
    down1 = read_down(stack_ref, A_QUERY1)
    cot = cot_ref[...]
    sent_ref[:128, :] = dot(attended_ref[...], read_down(stack_ref, A_OUT0)).astype(BF16)
    sent_ref[128:256, :] = dot((hidden.astype(F32) * gain).astype(BF16), down1).astype(BF16)
    sent_ref[256:384, :] = dot((up0.astype(F32) * gain).astype(BF16), down1).astype(BF16)
    sent_ref[384:512, :] = dot_cols(cot, read_up(stack_ref, B_OUT1)).astype(BF16)
    sent_ref[512:640, :] = dot_cols(hidden, up0).astype(BF16)
    sent_ref[640:, :] = dot_cols(up0, up0).astype(BF16)
    kept_ref[...] = dot_cols(cot, up0).astype(BF16)


def layer1_body(
    came_ref,
    small0_ref,
    kept_ref,
    stack_ref,
    query_ref,
    key_ref,
    value_ref,
    mask_ref,
    sent_ref,
    attended_ref,
    back_query_ref,
    ranks_ref,
    small_ref,
):
    def total(start):
        value = came_ref[0, start : start + 128, :].astype(F32)
        for peer in range(1, came_ref.shape[0]):
            value = value + came_ref[peer, start : start + 128, :].astype(F32)
        return value

    rank_output0 = total(0).astype(BF16)
    wide0 = rank_output0.astype(F32)
    cross = total(256)
    projected = total(128) + dot(rank_output0, cross.astype(BF16))
    back_rank_output = total(384).astype(BF16)
    hidden_up = total(512)
    gram = total(640)
    gram_high = gram.astype(BF16)
    gram_low = (gram - gram_high.astype(F32)).astype(BF16)
    output_gram = dot(rank_output0, gram_high) + dot(rank_output0, gram_low)
    squares = small0_ref[2, :, :1] + row_sum(wide0 * (2.0 * hidden_up + output_gram))
    scale = lax.rsqrt(jnp.maximum(squares, 0.0) / D + EPSILON)
    rank_query = (scale * projected).astype(BF16)
    ranks_ref[0] = rank_output0
    ranks_ref[1] = rank_query
    ranks_ref[2] = back_rank_output
    small_ref[0] = projected
    small_ref[1] = jnp.broadcast_to(scale, (128, 128))
    small_ref[2] = cross
    small_ref[3] = hidden_up + output_gram
    mask = mask_ref[...]
    up_query = read_up(stack_ref, B_QUERY1)
    down_output = read_down(stack_ref, A_OUT1)
    heads = query_ref.shape[1] // HEAD_DIM
    groups = key_ref.shape[1] // HEAD_DIM
    for head in range(heads):
        at, shared = columns_of(head), columns_of(head // (heads // groups))
        keys, values = key_ref[:, shared], value_ref[:, shared]
        queries = (query_ref[:, at].astype(F32) + dot(rank_query, up_query[:, at])).astype(BF16)
        probability = softmax_of(queries, keys, mask)
        attended_ref[:, at] = dot(probability.astype(BF16), values).astype(BF16)
        back_query_ref[:, at] = score_back(
            dot_cols(back_rank_output, down_output[at, :]).astype(BF16), probability, keys, values
        )
    rank_output = dot(attended_ref[...], down_output).astype(BF16)
    back_rank = dot_cols(back_query_ref[...], up_query).astype(BF16)
    for peer in range(sent_ref.shape[0]):
        sent_ref[peer, :128, :] = rank_output
        sent_ref[peer, 128:256, :] = back_rank
        sent_ref[peer, 256:, :] = kept_ref[...]


def score_back(back_attended, probability, keys, values):
    back_probability = dot_cols(back_attended, values)
    back_scores = probability * (back_probability - row_sum(probability * back_probability))
    return (dot(back_scores.astype(BF16), keys) * HEAD_DIM ** (-0.5)).astype(BF16)


def middle_body(
    came_ref,
    ranks_ref,
    small_ref,
    hidden_ref,
    cot_ref,
    gain_ref,
    stack_ref,
    attended0_ref,
    attended1_ref,
    back_query_ref,
    out_ref,
    gradient_ref,
    back_rank_ref,
    terms_ref,
):
    def total(start):
        value = came_ref[0, start : start + 128, :].astype(F32)
        for peer in range(1, came_ref.shape[0]):
            value = value + came_ref[peer, start : start + 128, :].astype(F32)
        return value

    rank_output1 = total(0).astype(BF16)
    back_rank = total(128).astype(BF16)
    gain = gain_ref[...]
    rank_output0, rank_query = ranks_ref[0], ranks_ref[1]
    scale = small_ref[1, :, :1]
    along = row_sum(back_rank.astype(F32) * small_ref[0]) / D
    pull = scale * scale * scale * along
    back_output0 = (
        total(256) + scale * dot_cols(back_rank, small_ref[2].astype(BF16)) - pull * small_ref[3]
    ).astype(BF16)
    back_rank_ref[...] = back_output0
    write_down(terms_ref, A_OUT0, dot_rows(attended0_ref[...], back_output0))
    write_down(terms_ref, A_OUT1, dot_rows(attended1_ref[...], ranks_ref[2]))
    write_up(terms_ref, B_QUERY1, dot_rows(rank_query, back_query_ref[...]))
    cot = cot_ref[...]
    write_up(terms_ref, B_OUT1, dot_rows(rank_output1, cot))
    hidden = hidden_ref[...].astype(F32) + dot(rank_output0, read_up(stack_ref, B_OUT0))
    normed = (hidden * scale * gain).astype(BF16)
    write_down(terms_ref, A_QUERY1, dot_rows(normed, back_rank))
    gained = gain * dot_cols(back_rank, read_down(stack_ref, A_QUERY1))
    gradient = cot.astype(F32) + scale * gained - hidden * pull
    gradient_ref[...] = gradient
    write_up(terms_ref, B_OUT0, dot_rows(rank_output0, gradient.astype(BF16)))
    out_ref[...] = (hidden + dot(rank_output1, read_up(stack_ref, B_OUT1))).astype(BF16)


def backward0_body(
    back_rank_ref,
    stack_ref,
    probability_ref,
    key_ref,
    value_ref,
    up_ref,
    back_query_ref,
    sent_ref,
):
    back_output = back_rank_ref[...]
    down_output = read_down(stack_ref, A_OUT0)
    heads = probability_ref.shape[0]
    groups = key_ref.shape[1] // HEAD_DIM
    for head in range(heads):
        at, shared = columns_of(head), columns_of(head // (heads // groups))
        back_query_ref[:, at] = score_back(
            dot_cols(back_output, down_output[at, :]).astype(BF16),
            probability_ref[head],
            key_ref[:, shared],
            value_ref[:, shared],
        )
    back_rank = dot_cols(back_query_ref[...], up_ref[...]).astype(BF16)
    for peer in range(sent_ref.shape[0]):
        sent_ref[peer] = back_rank


def last_body(
    came_ref,
    small_ref,
    rank_ref,
    back_query_ref,
    hidden_ref,
    gradient_ref,
    gain_ref,
    down_ref,
    cot_ref,
    terms_ref,
):
    value = came_ref[0].astype(F32)
    for peer in range(1, came_ref.shape[0]):
        value = value + came_ref[peer].astype(F32)
    back_rank = value.astype(BF16)
    gain = gain_ref[...]
    scale = small_ref[1, :, :1]
    hidden = hidden_ref[...].astype(F32)
    write_down(terms_ref, 0, dot_rows((hidden * scale * gain).astype(BF16), back_rank))
    write_up(terms_ref, 1, dot_rows(rank_ref[...], back_query_ref[...]))
    along = row_sum(back_rank.astype(F32) * small_ref[0]) / D
    gained = gain * dot_cols(back_rank, down_ref[...])
    cot_ref[...] = (
        gradient_ref[...] + scale * gained - hidden * (scale * scale * scale * along)
    ).astype(BF16)


def swap(value, axis):
    return lax.all_to_all(value, axis, 0, 0, tiled=True)


def on_device(
    arrived, cot_later, q_base, k_base, v_base, gains, parents, a_query, b_query, a_out, b_out
):
    ways = lax.axis_size("tensor")
    count = lax.axis_size("dp")
    rows = b_query.shape[1]
    width = arrived.shape[1]
    heads = width // HEAD_DIM
    block = shape((128, width), BF16)
    hidden = from_behind(arrived, "section", 1)
    shard = jnp.stack(
        [a_out[0], pack_up(b_out[0]), a_query[1], pack_up(b_out[1]), pack_up(b_query[1]), a_out[1]]
    )
    stack = lax.all_gather(shard, "dp", axis=0, tiled=False)
    cot = from_behind(cot_later, "section", -1)
    down0 = lax.all_gather(a_query[0], "dp", axis=0, tiled=True)
    gain0, gain1 = gains[0:1], gains[1:2]

    (mask,) = kernel_call(mask_body, [shape((128, 128), F32)], (parents.reshape(128, 1),), 3e7)
    (sent,) = kernel_call(
        first_body, [shape((ways, 136, 128), F32)], (hidden, gain0, down0), 1e8
    )
    came = swap(sent, "tensor")
    up_block, _ = lax.optimization_barrier((b_query[0], sent))
    up0 = lax.all_gather(up_block, "dp", axis=0, tiled=True)
    attended0, probability, rank_query0, small0 = kernel_call(
        forward0_body,
        [
            block,
            shape((heads, 128, 128), F32),
            shape((128, 128), BF16),
            shape((3, 128, 128), F32),
        ],
        (came, up0, q_base[0], k_base[0], v_base[0], mask),
    )
    sent, kept = kernel_call(
        second_body,
        [shape((768, 128), BF16), shape((128, 128), BF16)],
        (attended0, hidden, cot, gain1, stack),
        5e8,
    )
    came = lax.all_gather(sent, "tensor", axis=0, tiled=False)
    sent, attended1, back_query1, ranks, small1 = kernel_call(
        layer1_body,
        [
            shape((ways, 384, 128), BF16),
            block,
            block,
            shape((3, 128, 128), BF16),
            shape((4, 128, 128), F32),
        ],
        (came, small0, kept, stack, q_base[1], k_base[1], v_base[1], mask),
        8e8,
    )
    came = swap(sent, "tensor")
    section_out, gradient, back_rank_output0, terms = kernel_call(
        middle_body,
        [block, shape((128, width), F32), shape((128, 128), BF16), shape(stack.shape, BF16)],
        (
            came, ranks, small1, hidden, cot, gain1, stack, attended0, attended1, back_query1,
        ),
        6e8,
    )
    reduced = lax.psum_scatter(terms, "dp", scatter_dimension=0, tiled=False)
    back_query0, sent = kernel_call(
        backward0_body,
        [block, shape((ways, 128, 128), BF16)],
        (back_rank_output0, stack, probability, k_base[0], v_base[0], up0),
    )
    came = swap(sent, "tensor")
    cot_send, last_terms = kernel_call(
        last_body,
        [block, shape((count, 2, stack.shape[2], 128), BF16)],
        (came, small0, rank_query0, back_query0, hidden, gradient, gain0, down0),
    )
    last = jnp.sum(swap(last_terms, "dp").astype(F32), axis=0)
    reduced = reduced.astype(F32)
    return (
        section_out,
        cot_send,
        jnp.stack([last[0], reduced[A_QUERY1]]),
        jnp.stack([unpack_up(last[1], rows), unpack_up(reduced[B_QUERY1], rows)]),
        jnp.stack([reduced[A_OUT0], reduced[A_OUT1]]),
        jnp.stack([unpack_up(reduced[B_OUT0], rows), unpack_up(reduced[B_OUT1], rows)]),
    )


def solution(mesh):
    in_specs = (
        P(("section", "dp"), "tensor"),
        P(("section", "dp"), "tensor"),
        P(None, ("section", "dp"), "tensor"),
        P(None, ("section", "dp"), "tensor"),
        P(None, ("section", "dp"), "tensor"),
        P("section", "tensor"),
        P(("section", "dp")),
        P("section", ("tensor", "dp"), None),
        P("section", "dp", "tensor"),
        P("section", ("tensor", "dp"), None),
        P("section", "dp", "tensor"),
    )
    out_specs = (
        P(("section", "dp"), "tensor"),
        P(("section", "dp"), "tensor"),
        P("section", ("tensor", "dp"), None),
        P("section", "dp", "tensor"),
        P("section", ("tensor", "dp"), None),
        P("section", "dp", "tensor"),
    )
    return jax.shard_map(
        on_device, mesh=mesh, in_specs=in_specs, out_specs=out_specs, check_vma=False
    )
```

time: 788 us -> 273 us (0.35)
  the two profiles are of different devices: /device:TPU:4 before, /device:TPU:32 now
where the time goes in v1:
time: 273 us; the launch traced here: 272 us
  blocking collectives  163 us (60%)
  Pallas kernels  30 us (11%)
  waiting for transfers between devices  27.1 us (10%)
  local copies, waits for them, and re-layouts  26.6 us (10%)
  between operations  14.2 us (5%)
  starting transfers between devices  7.52 us (3%)
  other arithmetic  3.77 us (1%)
    all_to_all x3, blocking collectives, swap(): return lax.all_to_all(value, axis, 0, 0, tiled=True)  77.3 us
    all_gather x1, blocking collectives, on_device(): down0 = lax.all_gather(a_query[0], 'dp', axis=0, tiled=True)  39.1 us
    all_gather x1, blocking collectives, on_device(): up0 = lax.all_gather(up_block, 'dp', axis=0, tiled=True)  32 us
    pallas_call x8, Pallas kernels, kernel_call(): pl.pallas_call(body, out_shape=out_shape, in_specs=[pl.BlockSpec(memory_s...  30 us
    reduce_scatter x1, waiting for transfers between devices, on_device(): reduced = lax.psum_scatter(terms, 'dp', scatter_dimension=0, tiled=False)  27 us
    unnamed x63, local copies, waits for them, and re-layouts  20.6 us
    all_gather x1, blocking collectives, on_device(): came = lax.all_gather(sent, 'tensor', axis=0, tiled=False)  14.2 us
  transfers between devices with their start and end apart: 5, of which 1 were waited for; matrix products, arithmetic and copies ran while one was open for 2% of the time, Pallas kernels for 6%

profile of v1, /device:TPU:32, one launch (start us, length us, event | category | flops | bytes accessed | tf_op | source)
XLA Modules:
  0.0 271.7 jit_solution(1631777671510491540)
XLA Ops:
  7.2 0.8 slice_dynamic-update-slice_fusion.2
  8.1 0.8 bitcast_dynamic-update-slice_fusion.2
  8.8 0.8 slice_dynamic-update-slice_fusion.1
  9.6 0.8 bitcast_dynamic-update-slice_fusion.1
  10.4 0.8 bitcast_dynamic-update-slice_fusion
  11.1 0.8 slice_dynamic-update-slice_fusion
  11.9 0.7 copy-done.26
  12.7 2.9 %collective-permute-start.1 = (bf16[128,2048]{1,0:T(8,128)(2,1)}, bf16[128,2048]{1,0:T(8,128)(2,1)S(1)}, u32[]{:S(2)}, u32[]{:S(2)}) collective-permute-start(bf16[128,2048]{1,0:T(8,128)(2,1)} %param.12), channel_id=1, source_target_pairs={{0,448},{64,0},{128,64},{192,128},{256,192},{320,256},{384,320},{4... | collective-permute-start | bytes 1572872 | tf_op jit(solution)/shard_map/ppermute | solution.py:22
  15.6 0.8 slice_bitcast_fusion.13
  16.4 2.1 slice_bitcast_fusion
  18.4 0.8 fusion
  19.2 0.8 copy.18.parent_ref
  20.0 1.0 shard_map.155.mask_ref
  21.0 39.1 %all-gather = bf16[1,2048,128]{2,1,0:T(8,128)(2,1)S(1)} all-gather(bf16[1,128,128]{2,1,0:T(8,128)(2,1)S(1)} %get-tuple-element.61), channel_id=2, replica_groups=mesh['section'=8,'dp'=16,'tensor'=4] {'dp'}, dimensions={1}, use_global_device_ids=true | all-gather | bytes 557056 | tf_op jit(solution)/shard_map/all_gather | solution.py:386
  60.1 0.7 slice_bitcast_fusion.9
  60.9 1.8 shard_map.154
  62.7 4.5 %all-to-all-start = ((f32[4,136,128]{2,1,0:T(8,128)}), f32[4,136,128]{2,1,0:T(8,128)S(1)}, u32[]{:S(2)}, u32[]{:S(2)}) async-start(f32[4,136,128]{2,1,0:T(8,128)} %shard_map.154), calls=%async_computation | async-start | bytes 557056 | tf_op jit(solution)/shard_map/all_to_all | solution.py:368
  67.2 32.0 %all_gather.19.up_ref = bf16[128,2048]{1,0:T(8,128)(2,1)S(1)} all-gather(bf16[8,2048]{1,0:T(8,128)(2,1)S(1)} %slice_bitcast_fusion.13), channel_id=1, replica_groups=mesh['section'=8,'dp'=16,'tensor'=4] {'dp'}, dimensions={0}, use_global_device_ids=true | all-gather | bytes 557056 | tf_op jit(solution)/shard_map/all_gather | solution.py:395
  99.3 6.9 %shard_map.156 = (bf16[128,2048]{1,0:T(8,128)(2,1)S(1)}, f32[16,128,128]{2,1,0:T(8,128)S(1)}, bf16[128,128]{1,0:T(8,128)(2,1)S(1)}, f32[3,128,128]{2,1,0:T(8,128)S(1)}) custom-call(f32[4,136,128]{2,1,0:T(8,128)S(1)} %all-to-all-done.came_ref, bf16[128,2048]{1,0:T(8,128)(2,1)S(1)} %all_gather.19.up_ref, bf16[128,2048]{1,0:T(8,128)(2,1)S(1)} %get-tuple-element.47.query_ref, ...), custom_call_target="tpu_custom_call" | custom-call | flops 400000000 | bytes 3325952 | tf_op jit(solution)/shard_map/pallas_call | solution.py:43
  106.2 0.8 copy-done.14
  107.0 1.0 copy-done.18
  108.6 0.8 copy-done.11
  109.4 1.9 copy-done
  111.3 1.0 copy-done.3
  112.3 1.0 copy-done.12
  113.4 1.0 copy-done.15
  114.4 1.1 shard_map.157
  115.5 14.2 %all-gather.2 = bf16[3072,128]{1,0:T(8,128)(2,1)S(1)} all-gather(bf16[768,128]{1,0:T(8,128)(2,1)S(1)} %get-tuple-element.28), channel_id=4, replica_groups=mesh['section'=8,'dp'=16,'tensor'=4] {'tensor'}, dimensions={0}, use_global_device_ids=true | all-gather | bytes 983040 | tf_op jit(solution)/shard_map/all_gather | solution.py:412
  129.7 1.0 copy-done.17
  130.8 0.8 copy-done.22
  131.6 0.8 copy-done.23
  132.4 11.0 %shard_map.158 = (bf16[4,384,128]{2,1,0:T(8,128)(2,1)S(1)}, bf16[128,2048]{1,0:T(8,128)(2,1)S(1)}, bf16[128,2048]{1,0:T(8,128)(2,1)S(1)}, bf16[3,128,128]{2,1,0:T(8,128)(2,1)S(1)}, f32[4,128,128]{2,1,0:T(8,128)S(1)}) custom-call(bf16[4,768,128]{2,1,0:T(8,128)(2,1)S(1)} %bitcast.72, f32[3,128,128]{2,1,0:T(8,128)S(1)} %get-tuple-element.29.small0_ref.small_ref, ...), custom_call_target="tpu_custom_call" | custom-call | flops 800000000 | bytes 6684672 | tf_op jit(solution)/shard_map/pallas_call | solution.py:43
  143.5 10.6 %all_to_all.20.came_ref = bf16[4,384,128]{2,1,0:T(8,128)(2,1)S(1)} all-to-all(bf16[4,384,128]{2,1,0:T(8,128)(2,1)S(1)} %get-tuple-element.31), channel_id=1, replica_groups=mesh['section'=8,'dp'=16,'tensor'=4] {'tensor'}, dimensions={0} | all-to-all | bytes 786432 | tf_op jit(solution)/shard_map/all_to_all | solution.py:368
  154.1 2.5 shard_map.159
  156.6 1.6 copy-done.10
  158.3 1.0 copy-done.20
  159.3 1.1 copy-done.7
  160.4 1.2 copy-done.19
  161.6 4.1 %shard_map.160 = (bf16[128,2048]{1,0:T(8,128)(2,1)S(1)}, bf16[4,128,128]{2,1,0:T(8,128)(2,1)S(1)}) custom-call(bf16[128,128]{1,0:T(8,128)(2,1)S(1)} %get-tuple-element.37.back_rank_ref, bf16[16,6,128,128]{3,2,1,0:T(8,128)(2,1)S(1)} %bitcast.69, f32[16,128,128]{2,1,0:T(8,128)S(1)} %copy-done.19, bf16[128,256]{1,0:T(8,128)(2,1)S(1)} %get-tuple-element.64.key_ref, ...), custom_call_target="tpu_custom_call" | custom-call | flops 400000000 | bytes 5537792 | tf_op jit(solution)/shard_map/pallas_call | solution.py:43
  165.7 8.4 %all_to_all.21.came_ref = bf16[4,128,128]{2,1,0:T(8,128)(2,1)S(1)} all-to-all(bf16[4,128,128]{2,1,0:T(8,128)(2,1)S(1)} %get-tuple-element.39), channel_id=1, replica_groups=mesh['section'=8,'dp'=16,'tensor'=4] {'tensor'}, dimensions={0} | all-to-all | bytes 262144 | tf_op jit(solution)/shard_map/all_to_all | solution.py:368
  174.1 1.5 shard_map.161
  175.6 58.4 %all_to_all.22 = bf16[16,2,128,128]{3,2,1,0:T(8,128)(2,1)S(1)} all-to-all(bf16[16,2,128,128]{3,2,1,0:T(8,128)(2,1)S(1)} %get-tuple-element.44), channel_id=1, replica_groups=mesh['section'=8,'dp'=16,'tensor'=4] {'dp'}, dimensions={0} | all-to-all | bytes 2097152 | tf_op jit(solution)/shard_map/all_to_all | solution.py:368
  234.2 27.0 %reduce-scatter.2.cloned.1.call-done = bf16[1,6,128,128]{3,2,1,0:T(8,128)(2,1)} async-done(((bf16[16,6,128,128]{3,2,1,0:T(8,128)(2,1)}), bf16[1,6,128,128]{3,2,1,0:T(8,128)(2,1)}) %reduce-scatter.2.cloned.1.call-update) | async-done | bytes 196624 | tf_op jit(solution)/shard_map/reduce_scatter | solution.py:434
  261.2 1.0 convert_element_type.8
  262.2 0.7 pad_maximum_fusion.3
  262.8 0.7 pad_maximum_fusion.1
  263.5 0.7 pad_maximum_fusion
  264.2 0.7 pad_maximum_fusion.2
  (55 shorter events, 1.1 us)
Async XLA Ops:
  7.2 52.9 %copy-start.27 = (bf16[2,128,256]{2,1,0:T(8,128)(2,1)S(1)}, bf16[2,128,256]{2,1,0:T(8,128)(2,1)}, u32[]{:S(2)}) copy-start(bf16[2,128,256]{2,1,0:T(8,128)(2,1)} %param.15) | copy-start | bytes 393220
  7.2 52.9 %copy-start.28 = (bf16[2,128,256]{2,1,0:T(8,128)(2,1)S(1)}, bf16[2,128,256]{2,1,0:T(8,128)(2,1)}, u32[]{:S(2)}) copy-start(bf16[2,128,256]{2,1,0:T(8,128)(2,1)} %param.14) | copy-start | bytes 393220
  7.2 102.2 %all-gather.5.cloned.1.call-start = ((), (), s32[]{:S(2)}) async-start(), calls=%async_computation.6 | async-start | bytes 3342336 | tf_op jit(solution)/shard_map/all_gather | solution.py:384
  11.9 0.7 copy-start.26
  12.6 48.2 %collective-permute-start = (bf16[128,2048]{1,0:T(8,128)(2,1)}, bf16[128,2048]{1,0:T(8,128)(2,1)S(1)}, u32[]{:S(2)}, u32[]{:S(2)}) collective-permute-start(bf16[128,2048]{1,0:T(8,128)(2,1)} %param.11), channel_id=1, source_target_pairs={{0,64},{64,128},{128,192},{192,256},{256,320},{320,384},{384,448},... | collective-permute-start | bytes 1572872 | tf_op jit(solution)/shard_map/ppermute | solution.py:22
  12.7 95.9 %collective-permute-start.1 = (bf16[128,2048]{1,0:T(8,128)(2,1)}, bf16[128,2048]{1,0:T(8,128)(2,1)S(1)}, u32[]{:S(2)}, u32[]{:S(2)}) collective-permute-start(bf16[128,2048]{1,0:T(8,128)(2,1)} %param.12), channel_id=1, source_target_pairs={{0,448},{64,0},{128,64},{192,128},{256,192},{320,256},{384,320},{4... | collective-permute-start | bytes 1572872 | tf_op jit(solution)/shard_map/ppermute | solution.py:22
  60.1 0.8 copy-start.8
  60.8 48.6 %copy-start.2 = (bf16[128,2048]{1,0:T(8,128)(2,1)}, bf16[128,2048]{1,0:T(8,128)(2,1)S(1)}, u32[]{:S(2)}) copy-start(bf16[128,2048]{1,0:T(8,128)(2,1)S(1)} %collective-permute-done.hidden_ref) | copy-start | bytes 1572868
  62.7 36.5 %all-to-all-start = ((f32[4,136,128]{2,1,0:T(8,128)}), f32[4,136,128]{2,1,0:T(8,128)S(1)}, u32[]{:S(2)}, u32[]{:S(2)}) async-start(f32[4,136,128]{2,1,0:T(8,128)} %shard_map.154), calls=%async_computation | async-start | bytes 557056 | tf_op jit(solution)/shard_map/all_to_all | solution.py:368
  67.2 193.9 %reduce-scatter.2.cloned.1.call-start = ((), (), s32[]{:S(2)}) async-start(), calls=%async_computation.5 | async-start | bytes 3342336 | tf_op jit(solution)/shard_map/reduce_scatter | solution.py:434
  99.2 10.1 %copy-start.6 = (bf16[128,2048]{1,0:T(8,128)(2,1)}, bf16[128,2048]{1,0:T(8,128)(2,1)S(1)}, u32[]{:S(2)}) copy-start(bf16[128,2048]{1,0:T(8,128)(2,1)S(1)} %all_gather.19.up_ref) | copy-start | bytes 1572868
  106.2 0.8 copy-start.14
  107.0 1.0 copy-start.18
  108.0 0.6 copy-start.24
  108.6 0.8 copy-start.11
  109.4 1.9 copy-start
  111.3 1.0 copy-start.3
  112.3 1.0 copy-start.12
  113.4 1.0 copy-start.15
  114.4 15.3 %copy-start.1 = (bf16[96,128,128]{2,1,0:T(8,128)(2,1)S(1)}, bf16[96,128,128]{2,1,0:T(8,128)(2,1)}, u32[]{:S(2)}) copy-start(bf16[96,128,128]{2,1,0:T(8,128)(2,1)} %all-gather.5.cloned.1.call-done) | copy-start | bytes 9437188
  115.5 38.6 %copy-start.4 = (bf16[128,2048]{1,0:T(8,128)(2,1)S(1)}, bf16[128,2048]{1,0:T(8,128)(2,1)}, u32[]{:S(2)}) copy-start(bf16[128,2048]{1,0:T(8,128)(2,1)} %copy-done.2) | copy-start | bytes 1572868
  115.5 38.6 %copy-start.13 = (bf16[128,2048]{1,0:T(8,128)(2,1)S(1)}, bf16[128,2048]{1,0:T(8,128)(2,1)}, u32[]{:S(2)}) copy-start(bf16[128,2048]{1,0:T(8,128)(2,1)} %copy-done.11) | copy-start | bytes 1572868
  115.5 38.6 %copy-start.16 = (bf16[128,2048]{1,0:T(8,128)(2,1)S(1)}, bf16[128,2048]{1,0:T(8,128)(2,1)}, u32[]{:S(2)}) copy-start(bf16[128,2048]{1,0:T(8,128)(2,1)} %copy-done.14) | copy-start | bytes 1572868
  129.7 1.0 copy-start.17
  130.8 0.8 copy-start.22
  131.6 0.8 copy-start.23
  156.6 1.7 copy-start.10
  158.3 1.0 copy-start.20
  159.3 14.8 %copy-start.25 = (bf16[128,128]{1,0:T(8,128)(2,1)S(1)}, bf16[128,128]{1,0:T(8,128)(2,1)}, u32[]{:S(2)}) copy-start(bf16[128,128]{1,0:T(8,128)(2,1)} %copy-done.24) | copy-start | bytes 98308
  159.3 14.8 %copy-start.5 = (bf16[128,2048]{1,0:T(8,128)(2,1)S(1)}, bf16[128,2048]{1,0:T(8,128)(2,1)}, u32[]{:S(2)}) copy-start(bf16[128,2048]{1,0:T(8,128)(2,1)} %copy-done.2) | copy-start | bytes 1572868
  159.3 1.1 copy-start.7
  160.4 1.2 copy-start.19
  161.6 12.4 %copy-start.9 = (bf16[1,2048,128]{2,1,0:T(8,128)(2,1)S(1)}, bf16[1,2048,128]{2,1,0:T(8,128)(2,1)}, u32[]{:S(2)}) copy-start(bf16[1,2048,128]{2,1,0:T(8,128)(2,1)} %copy-done.8) | copy-start | bytes 1572868
  161.6 12.4 %copy-start.21 = (f32[128,2048]{1,0:T(8,128)S(1)}, f32[128,2048]{1,0:T(8,128)}, u32[]{:S(2)}) copy-start(f32[128,2048]{1,0:T(8,128)} %copy-done.20) | copy-start | bytes 3145732
Sparse Core Ops, SparseCore 0:
  12.8 82.9 all-gather.4
  159.4 101.7 reduce-scatter.1

commit v2 on v1

v2 whole, which is shorter than its diff:
```python
import jax
import jax.numpy as jnp
from jax import lax
from jax.experimental import pallas as pl
from jax.experimental.pallas import tpu as pltpu
from jax.sharding import PartitionSpec as P

D = 8192
HEAD_DIM = 128
HEADS_AT_ONCE = 4
EPSILON = 1e-05
F32 = jnp.float32
BF16 = jnp.bfloat16
VMEM_LIMIT = 58 << 20
ALL = slice(None)
A_OUT0, B_OUT0, A_QUERY1, B_OUT1, B_QUERY1, A_OUT1 = range(6)
TERM_A_QUERY, TERM_B_QUERY, TERM_A_OUT, TERM_B_OUT = 0, 2, 4, 6


def from_behind(value, axis, steps):
    count = lax.axis_size(axis)
    pairs = [(source, (source + steps) % count) for source in range(count)]
    return lax.ppermute(value, axis, pairs)


def dot(left, right):
    return jnp.dot(left, right, preferred_element_type=F32)


def dot_rows(left, right):
    return lax.dot_general(left, right, (((0,), (0,)), ((), ())), preferred_element_type=F32)


def dot_cols(left, right):
    return lax.dot_general(left, right, (((1,), (1,)), ((), ())), preferred_element_type=F32)


def row_sum(value):
    return jnp.sum(value, axis=1, keepdims=True)


def shape(dims, dtype):
    return jax.ShapeDtypeStruct(dims, dtype)


class Arriving:
    def __init__(self, copy, ref):
        self.copy, self.ref, self.waited = copy, ref, False
        self.shape = ref.shape

    def wait(self):
        if not self.waited:
            self.copy.wait()
            self.waited = True

    def __getitem__(self, at):
        self.wait()
        return self.ref[at]


class Leaving:
    def __init__(self, copy, ref):
        self.copy, self.ref, self.sent = copy, ref, False
        self.shape = ref.shape

    def send(self):
        if not self.sent:
            self.copy.start()
            self.sent = True

    def __setitem__(self, at, value):
        self.ref[at] = value

    def __getitem__(self, at):
        return self.ref[at]


def sliced(dims, at):
    at = at + (ALL,) * (len(dims) - len(at))
    result = []
    for size, entry in zip(dims, at, strict=True):
        if isinstance(entry, slice):
            result.append(len(range(*entry.indices(size))))
    return tuple(result)


def kernel_call(body, ins, outs, flops, alias=None):
    hbm, vmem = pl.BlockSpec(memory_space=pltpu.HBM), pl.BlockSpec(memory_space=pltpu.VMEM)
    scratch, in_count, out_count = [], len(ins), len(outs)
    for index, item in enumerate(ins):
        if isinstance(item, tuple) and index != alias:
            scratch += [pltpu.VMEM(sliced(item[0].shape, at), item[0].dtype) for at in item[1]]
    first_out = len(scratch)
    for item in outs:
        if isinstance(item, tuple):
            scratch += [pltpu.VMEM(sliced(item[0].shape, at), item[0].dtype) for at in item[1]]
    buffers = len(scratch)

    def run(*refs):
        in_refs, out_refs = refs[:in_count], refs[in_count : in_count + out_count]
        places = refs[in_count + out_count :]
        marks = places[buffers] if buffers else None
        used, given, arriving, leaving = 0, [], [], []
        for index, (ref, item) in enumerate(zip(in_refs, ins, strict=True)):
            if index == alias:
                continue
            if not isinstance(item, tuple):
                given.append(ref)
                continue
            for at in item[1]:
                copy = pltpu.make_async_copy(ref.at[at], places[used], marks.at[used])
                copy.start()
                arriving.append(Arriving(copy, places[used]))
                given.append(arriving[-1])
                used += 1
        assert used == first_out
        for ref, item in zip(out_refs, outs, strict=True):
            if not isinstance(item, tuple):
                given.append(ref)
                continue
            for at in item[1]:
                copy = pltpu.make_async_copy(places[used], ref.at[at], marks.at[used])
                leaving.append(Leaving(copy, places[used]))
                given.append(leaving[-1])
                used += 1
        body(*given)
        for item in leaving:
            item.send()
        for item in arriving:
            item.wait()
        for item in leaving:
            item.copy.wait()

    arrays = [item[0] if isinstance(item, tuple) else item for item in ins]
    shapes = [item[0] if isinstance(item, tuple) else item for item in outs]
    size = sum(x.size * x.dtype.itemsize for x in (*arrays, *shapes))
    return pl.pallas_call(
        run,
        out_shape=shapes,
        in_specs=[hbm if isinstance(item, tuple) else vmem for item in ins],
        out_specs=[hbm if isinstance(item, tuple) else vmem for item in outs],
        scratch_shapes=scratch + ([pltpu.SemaphoreType.DMA((buffers,))] if buffers else []),
        input_output_aliases={} if alias is None else {alias: 0},
        compiler_params=pltpu.CompilerParams(vmem_limit_bytes=VMEM_LIMIT),
        cost_estimate=pl.CostEstimate(flops=int(flops), bytes_accessed=size, transcendentals=0),
    )(*arrays)


def whole(value):
    return (value, [(ALL,) * len(value.shape)])


def read_down(ref):
    return ref[...].reshape(-1, 128)


def read_up(ref):
    count, length, _ = ref.shape
    rows = 128 // count
    columns = []
    for pair in range(length // (2 * rows)):
        slab = ref[:, pair * 2 * rows : (pair + 1) * 2 * rows, :].astype(F32)
        for half in range(2):
            columns.append(
                slab[:, half * rows : (half + 1) * rows, :].reshape(128, 128).astype(BF16)
            )
    return jnp.concatenate(columns, axis=1)


def write_down(ref, value):
    ref[...] = value.astype(BF16).reshape(ref.shape)


def write_up(ref, value):
    count, length, _ = ref.shape
    rows = 128 // count
    for pair in range(length // (2 * rows)):
        halves = [
            value[:, (2 * pair + half) * 128 : (2 * pair + half + 1) * 128].reshape(
                count, rows, 128
            )
            for half in range(2)
        ]
        ref[:, pair * 2 * rows : (pair + 1) * 2 * rows, :] = jnp.concatenate(
            halves, axis=1
        ).astype(BF16)


def pack_body(*refs):
    sources, ups, targets = refs[:3], refs[3:6], refs[6:12]
    for ref, place in zip(sources, (A_OUT0, A_QUERY1, A_OUT1), strict=True):
        targets[place][...] = ref[...]
    for ref, place in zip(ups, (B_OUT0, B_OUT1, B_QUERY1), strict=True):
        rows, width = ref.shape
        value = ref[...].astype(F32)
        for pair in range(width // 256):
            halves = [
                value[:, (2 * pair + half) * 128 : (2 * pair + half + 1) * 128]
                for half in range(2)
            ]
            targets[place][pair * 2 * rows : (pair + 1) * 2 * rows, :] = jnp.concatenate(
                halves, axis=0
            ).astype(BF16)


def unpack_body(came, a_query_ref, b_query_ref, a_out_ref, b_out_ref):
    for layer in range(2):
        for ref, place in ((a_query_ref, TERM_A_QUERY), (a_out_ref, TERM_A_OUT)):
            ref[layer] = came[place + layer].astype(F32)
        for ref, place in ((b_query_ref, TERM_B_QUERY), (b_out_ref, TERM_B_OUT)):
            rows, width = ref.shape[1:]
            value = came[place + layer].astype(F32)
            for tile in range(width // 128):
                ref[layer, :, tile * 128 : (tile + 1) * 128] = value[
                    tile * rows : (tile + 1) * rows
                ]


def first_body(hidden_ref, gain_ref, parent_ref, down_ref, sent_ref, bias_ref):
    lane = lax.broadcasted_iota(jnp.int32, (128, 128), 1)
    line = lax.broadcasted_iota(jnp.int32, (128, 128), 0)
    linked = (lane == line) | (jnp.broadcast_to(parent_ref[...], (128, 128)) == line)
    reached = jnp.where(linked, 1.0, 0.0).astype(BF16)
    for _ in range(7):
        reached = jnp.minimum(dot(reached, reached), 1.0).astype(BF16)
    bias_ref[...] = jnp.where(jnp.transpose(reached.astype(F32)) > 0.5, 0.0, -1e30)
    hidden = hidden_ref[...].astype(F32)
    projected = dot((hidden * gain_ref[...]).astype(BF16), down_ref[...])
    squares = lax.dot_general(
        jnp.ones((8, hidden.shape[1]), F32),
        hidden * hidden,
        (((1,), (1,)), ((), ())),
        preferred_element_type=F32,
        precision=lax.Precision.HIGHEST,
    )
    for peer in range(sent_ref.shape[0]):
        sent_ref[peer, :128, :] = projected
        sent_ref[peer, 128:, :] = squares


def to_column(row):
    lane = lax.broadcasted_iota(jnp.int32, (128, 128), 1)
    line = lax.broadcasted_iota(jnp.int32, (128, 128), 0)
    return row_sum(jnp.where(lane == line, jnp.broadcast_to(row, (128, 128)), 0.0))


def total(ref, start=0):
    value = ref[0, start : start + 128, :].astype(F32)
    for peer in range(1, ref.shape[0]):
        value = value + ref[peer, start : start + 128, :].astype(F32)
    return value


def head_blocks(query_ref, key_ref):
    heads = query_ref.shape[-1] // HEAD_DIM
    groups = key_ref.shape[-1] // HEAD_DIM
    share = heads // groups
    return [
        (head, slice((head // share) * HEAD_DIM, (head // share + 1) * HEAD_DIM))
        for head in range(0, heads, HEADS_AT_ONCE)
    ]


def stacked(value, head):
    return jnp.concatenate(
        [
            value[:, (head + k) * HEAD_DIM : (head + k + 1) * HEAD_DIM]
            for k in range(HEADS_AT_ONCE)
        ],
        axis=0,
    )


def spread(ref, head, value):
    for k in range(HEADS_AT_ONCE):
        ref[:, (head + k) * HEAD_DIM : (head + k + 1) * HEAD_DIM] = value[k * 128 : (k + 1) * 128]


def softmax_of(queries, keys, bias):
    scores = dot_cols(queries, keys) * HEAD_DIM ** (-0.5) + bias
    weights = jnp.exp(scores - jnp.max(scores, axis=1, keepdims=True))
    return weights * (1.0 / row_sum(weights))


def score_back(back_attended, probability, keys, values):
    back_probability = dot_cols(back_attended, values)
    back_scores = probability * (back_probability - row_sum(probability * back_probability))
    return (dot(back_scores.astype(BF16), keys) * HEAD_DIM ** (-0.5)).astype(BF16)


def forward0_body(
    came_ref, up_ref, bias_ref, query_ref, key_ref, value_ref, attended_ref, probability_ref,
    rank_ref, small_ref,
):
    projected = total(came_ref)
    squares = came_ref[0, 128:129, :]
    for peer in range(1, came_ref.shape[0]):
        squares = squares + came_ref[peer, 128:129, :]
    squares = to_column(squares)
    scale = lax.rsqrt(squares / D + EPSILON)
    rank_query = (scale * projected).astype(BF16)
    rank_ref[...] = rank_query
    small_ref[0] = projected
    small_ref[1] = jnp.broadcast_to(scale, (128, 128))
    small_ref[2] = jnp.broadcast_to(squares, (128, 128))
    rank_ref.send()
    small_ref.send()
    bias = jnp.concatenate([bias_ref[...]] * HEADS_AT_ONCE, axis=0)
    queries = (query_ref[...].astype(F32) + dot(rank_query, up_ref[...])).astype(BF16)
    for head, shared in head_blocks(query_ref, key_ref):
        probability = softmax_of(stacked(queries, head), key_ref[:, shared], bias)
        probability_ref[head * 128 : (head + HEADS_AT_ONCE) * 128, :] = probability
        spread(
            attended_ref, head, dot(probability.astype(BF16), value_ref[:, shared]).astype(BF16)
        )


def second_body(
    attended_ref, down_output_ref, hidden_ref, up0_ref, down1_ref, cot_ref, up1_ref, gain_ref,
    sent_ref, kept_ref,
):
    sent_ref[:128, :] = dot(attended_ref[...], read_down(down_output_ref)).astype(BF16)
    hidden, gain = hidden_ref[...], gain_ref[...]
    up0 = read_up(up0_ref)
    sent_ref[512:640, :] = dot_cols(hidden, up0).astype(BF16)
    sent_ref[640:, :] = dot_cols(up0, up0).astype(BF16)
    down1 = read_down(down1_ref)
    sent_ref[128:256, :] = dot((hidden.astype(F32) * gain).astype(BF16), down1).astype(BF16)
    sent_ref[256:384, :] = dot((up0.astype(F32) * gain).astype(BF16), down1).astype(BF16)
    cot = cot_ref[...]
    sent_ref[384:512, :] = dot_cols(cot, read_up(up1_ref)).astype(BF16)
    kept_ref[...] = dot_cols(cot, up0).astype(BF16)


def layer1_body(
    came_ref, small0_ref, query_ref, up_ref, key_ref, value_ref, bias_ref, down_ref, kept_ref,
    sent_ref, attended_ref, back_query_ref, ranks_ref, small_ref,
):
    rank_output0 = total(came_ref).astype(BF16)
    cross = total(came_ref, 256)
    projected = total(came_ref, 128) + dot(rank_output0, cross.astype(BF16))
    back_rank_output = total(came_ref, 384).astype(BF16)
    hidden_up = total(came_ref, 512)
    gram = total(came_ref, 640)
    gram_high = gram.astype(BF16)
    gram_low = (gram - gram_high.astype(F32)).astype(BF16)
    output_gram = dot(rank_output0, gram_high) + dot(rank_output0, gram_low)
    squares = small0_ref[2, :, :1] + row_sum(
        rank_output0.astype(F32) * (2.0 * hidden_up + output_gram)
    )
    scale = lax.rsqrt(jnp.maximum(squares, 0.0) / D + EPSILON)
    rank_query = (scale * projected).astype(BF16)
    ranks_ref[0] = rank_output0
    ranks_ref[1] = rank_query
    ranks_ref[2] = back_rank_output
    ranks_ref.send()
    small_ref[0] = projected
    small_ref[1] = jnp.broadcast_to(scale, (128, 128))
    small_ref[2] = cross
    small_ref[3] = hidden_up + output_gram
    small_ref.send()
    bias = jnp.concatenate([bias_ref[...]] * HEADS_AT_ONCE, axis=0)
    up_query = read_up(up_ref)
    queries = (query_ref[...].astype(F32) + dot(rank_query, up_query)).astype(BF16)
    down_output = read_down(down_ref)
    back_attended = dot_cols(back_rank_output, down_output).astype(BF16)
    for head, shared in head_blocks(query_ref, key_ref):
        keys, values = key_ref[:, shared], value_ref[:, shared]
        probability = softmax_of(stacked(queries, head), keys, bias)
        spread(attended_ref, head, dot(probability.astype(BF16), values).astype(BF16))
        spread(
            back_query_ref, head, score_back(stacked(back_attended, head), probability, keys, values)
        )
    attended_ref.send()
    back_query_ref.send()
    rank_output = dot(attended_ref[...], down_output).astype(BF16)
    back_rank = dot_cols(back_query_ref[...], up_query).astype(BF16)
    for peer in range(sent_ref.shape[0]):
        sent_ref[peer, :128, :] = rank_output
        sent_ref[peer, 128:256, :] = back_rank
        sent_ref[peer, 256:, :] = kept_ref[...]


def backward0_body(
    came_ref, small_ref, down_ref, key_ref, value_ref, probability_ref, up_ref,
    sent_ref, back_query_ref, ranks_ref, pull_ref,
):
    back_rank1 = total(came_ref, 128).astype(BF16)
    scale = small_ref[1, :, :1]
    along = row_sum(back_rank1.astype(F32) * small_ref[0]) / D
    pull = scale * scale * scale * along
    back_output = (
        total(came_ref, 256)
        + scale * dot_cols(back_rank1, small_ref[2].astype(BF16))
        - pull * small_ref[3]
    ).astype(BF16)
    ranks_ref[0] = total(came_ref).astype(BF16)
    ranks_ref[1] = back_rank1
    ranks_ref[2] = back_output
    ranks_ref.send()
    pull_ref[...] = jnp.broadcast_to(pull, (128, 128))
    pull_ref.send()
    back_attended = dot_cols(back_output, read_down(down_ref)).astype(BF16)
    for head, shared in head_blocks(back_query_ref, key_ref):
        spread(
            back_query_ref,
            head,
            score_back(
                stacked(back_attended, head),
                probability_ref[head * 128 : (head + HEADS_AT_ONCE) * 128, :],
                key_ref[:, shared],
                value_ref[:, shared],
            ),
        )
    back_query_ref.send()
    back_rank = dot_cols(back_query_ref[...], up_ref[...]).astype(BF16)
    for peer in range(sent_ref.shape[0]):
        sent_ref[peer] = back_rank


def terms_body(
    ranks1_ref, ranks2_ref, small_ref, pull_ref, gain_ref, cot_ref, hidden_ref, up0_ref, down1_ref,
    up1_ref, attended0_ref, attended1_ref, rank0_ref, back_query0_ref, back_query1_ref,
    a_query1, b_query0, b_query1, a_out0, a_out1, b_out0, b_out1, out_ref, gradient_ref,
):
    rank_output0, rank_query1, back_output1 = ranks1_ref[0], ranks1_ref[1], ranks1_ref[2]
    rank_output1, back_rank1, back_output0 = ranks2_ref[0], ranks2_ref[1], ranks2_ref[2]
    cot = cot_ref[...]
    write_up(b_out1, dot_rows(rank_output1, cot))
    b_out1.send()
    gain, scale, pull = gain_ref[...], small_ref[1, :, :1], pull_ref[:, :1]
    hidden = hidden_ref[...].astype(F32) + dot(rank_output0, read_up(up0_ref))
    write_down(a_query1, dot_rows((hidden * scale * gain).astype(BF16), back_rank1))
    a_query1.send()
    gained = gain * dot_cols(back_rank1, read_down(down1_ref))
    gradient = cot.astype(F32) + scale * gained - hidden * pull
    gradient_ref[...] = gradient
    gradient_ref.send()
    write_up(b_out0, dot_rows(rank_output0, gradient.astype(BF16)))
    b_out0.send()
    out_ref[...] = (hidden + dot(rank_output1, read_up(up1_ref))).astype(BF16)
    out_ref.send()
    write_down(a_out0, dot_rows(attended0_ref[...], back_output0))
    a_out0.send()
    write_down(a_out1, dot_rows(attended1_ref[...], back_output1))
    a_out1.send()
    write_up(b_query1, dot_rows(rank_query1, back_query1_ref[...]))
    b_query1.send()
    write_up(b_query0, dot_rows(rank0_ref[...], back_query0_ref[...]))


def last_term_body(came_ref, small_ref, gain_ref, hidden_ref, a_query0):
    normed = (hidden_ref[...].astype(F32) * small_ref[1, :, :1] * gain_ref[...]).astype(BF16)
    write_down(a_query0, dot_rows(normed, total(came_ref).astype(BF16)))


def cot_body(came_ref, small_ref, gain_ref, down_ref, hidden_ref, gradient_ref, cot_ref):
    back_rank = total(came_ref).astype(BF16)
    scale = small_ref[1, :, :1]
    along = row_sum(back_rank.astype(F32) * small_ref[0]) / D
    gained = gain_ref[...] * dot_cols(back_rank, down_ref[...])
    cot_ref[...] = (
        gradient_ref[...]
        + scale * gained
        - hidden_ref[...].astype(F32) * (scale * scale * scale * along)
    ).astype(BF16)


def swap(value, axis):
    return lax.all_to_all(value, axis, 0, 0, tiled=True)


def on_device(
    arrived, cot_later, q_base, k_base, v_base, gains, parents, a_query, b_query, a_out, b_out
):
    ways = lax.axis_size("tensor")
    count = lax.axis_size("dp")
    rows, width = b_query.shape[1], arrived.shape[1]
    length = rows * width // 128
    heads = width // HEAD_DIM
    block = whole(shape((128, width), BF16))
    layer0, layer1 = [(0,)], [(1,)]
    gain0, gain1 = (gains, [(slice(0, 1),)]), (gains, [(slice(1, 2),)])
    factor = [(ALL, member) for member in range(6)]

    (shard,) = kernel_call(
        pack_body,
        [
            (a_out, layer0), (a_query, layer1), (a_out, layer1),
            (b_out, layer0), (b_out, layer1), (b_query, layer1),
        ],
        [(shape((6, length, 128), BF16), [(member,) for member in range(6)])],
        0,
    )
    stack = lax.all_gather(shard, "dp", axis=0, tiled=False)
    hidden = from_behind(arrived, "section", 1)
    cot = from_behind(cot_later, "section", -1)
    down0 = lax.all_gather(a_query[0], "dp", axis=0, tiled=True)
    sent, bias = kernel_call(
        first_body,
        [whole(hidden), gain0, parents.reshape(1, 128), down0],
        [shape((ways, 136, 128), F32), shape((128, 128), F32)],
        1e8,
    )
    came = swap(sent, "tensor")
    up_block, _ = lax.optimization_barrier((b_query[0], sent))
    up0 = lax.all_gather(up_block, "dp", axis=0, tiled=True)
    attended0, probability, rank_query0, small0 = kernel_call(
        forward0_body,
        [came, up0, bias, (q_base, layer0), (k_base, layer0), (v_base, layer0)],
        [
            block,
            whole(shape((heads * 128, 128), F32)),
            whole(shape((128, 128), BF16)),
            whole(shape((3, 128, 128), F32)),
        ],
        4e8,
    )
    sent, kept = kernel_call(
        second_body,
        [
            whole(attended0), (stack, [factor[A_OUT0]]), whole(hidden),
            (stack, [factor[B_OUT0], factor[A_QUERY1]]), whole(cot), (stack, [factor[B_OUT1]]),
            gain1,
        ],
        [shape((768, 128), BF16), shape((128, 128), BF16)],
        5e8,
    )
    came = lax.all_gather(sent, "tensor", axis=0, tiled=False)
    sent, attended1, back_query1, ranks1, small1 = kernel_call(
        layer1_body,
        [
            came, whole(small0), (q_base, layer1), (stack, [factor[B_QUERY1]]), (k_base, layer1),
            (v_base, layer1), bias, (stack, [factor[A_OUT1]]), kept,
        ],
        [
            shape((ways, 384, 128), BF16),
            block,
            block,
            whole(shape((3, 128, 128), BF16)),
            whole(shape((4, 128, 128), F32)),
        ],
        8e8,
    )
    came = swap(sent, "tensor")
    sent, back_query0, ranks2, pull = kernel_call(
        backward0_body,
        [
            came, whole(small1), (stack, [factor[A_OUT0]]), (k_base, layer0), (v_base, layer0),
            whole(probability), whole(up0),
        ],
        [
            shape((ways, 128, 128), BF16),
            block,
            whole(shape((3, 128, 128), BF16)),
            whole(shape((128, 128), F32)),
        ],
        4e8,
    )
    came = swap(sent, "tensor")
    term_shape = shape((count, 8, length, 128), BF16)
    terms, section_out, gradient = kernel_call(
        terms_body,
        [
            whole(ranks1), whole(ranks2), whole(small1), whole(pull), gain1, whole(cot),
            whole(hidden), (stack, [factor[B_OUT0], factor[A_QUERY1], factor[B_OUT1]]),
            whole(attended0), whole(attended1), whole(rank_query0), whole(back_query0),
            whole(back_query1),
        ],
        [
            (
                term_shape,
                [
                    (ALL, member)
                    for member in (
                        TERM_A_QUERY + 1, TERM_B_QUERY, TERM_B_QUERY + 1, TERM_A_OUT,
                        TERM_A_OUT + 1, TERM_B_OUT, TERM_B_OUT + 1,
                    )
                ],
            ),
            block,
            whole(shape((128, width), F32)),
        ],
        1e9,
    )
    (terms,) = kernel_call(
        last_term_body,
        [came, whole(small0), gain0, whole(hidden), whole(terms)],
        [(term_shape, [(ALL, TERM_A_QUERY)])],
        1e8,
        alias=4,
    )
    reduced = lax.psum_scatter(terms, "dp", scatter_dimension=0, tiled=False)
    (cot_send,) = kernel_call(
        cot_body,
        [came, whole(small0), gain0, whole(down0), whole(hidden), whole(gradient)],
        [block],
        1e8,
    )
    grads = kernel_call(
        unpack_body,
        [whole(reduced)],
        [
            whole(shape((2, length, 128), F32)),
            whole(shape((2, rows, width), F32)),
            whole(shape((2, length, 128), F32)),
            whole(shape((2, rows, width), F32)),
        ],
        0,
    )
    return (section_out, cot_send, *grads)


def solution(mesh):
    in_specs = (
        P(("section", "dp"), "tensor"),
        P(("section", "dp"), "tensor"),
        P(None, ("section", "dp"), "tensor"),
        P(None, ("section", "dp"), "tensor"),
        P(None, ("section", "dp"), "tensor"),
        P("section", "tensor"),
        P(("section", "dp")),
        P("section", ("tensor", "dp"), None),
        P("section", "dp", "tensor"),
        P("section", ("tensor", "dp"), None),
        P("section", "dp", "tensor"),
    )
    out_specs = (
        P(("section", "dp"), "tensor"),
        P(("section", "dp"), "tensor"),
        P("section", ("tensor", "dp"), None),
        P("section", "dp", "tensor"),
        P("section", ("tensor", "dp"), None),
        P("section", "dp", "tensor"),
    )
    return jax.shard_map(
        on_device, mesh=mesh, in_specs=in_specs, out_specs=out_specs, check_vma=False
    )
```

time: 273 us -> 249 us (0.912)
  the two profiles are of different devices: /device:TPU:32 before, /device:TPU:10 now
where the time goes in v2:
time: 249 us; the launch traced here: 248 us
  blocking collectives  103 us (41%)
  waiting for transfers between devices  75.5 us (30%)
  Pallas kernels  40.7 us (16%)
  between operations  14.2 us (6%)
  starting transfers between devices  11 us (4%)
  local copies, waits for them, and re-layouts  4.5 us (2%)
    reduce_scatter x1, waiting for transfers between devices, on_device(): reduced = lax.psum_scatter(terms, 'dp', scatter_dimension=0, tiled=False)  75.4 us
    all_gather x1, blocking collectives, on_device(): down0 = lax.all_gather(a_query[0], 'dp', axis=0, tiled=True)  42.2 us
    pallas_call x10, Pallas kernels, kernel_call(): pl.pallas_call(run, out_shape=shapes, in_specs=[hbm if isinstance(item, t...  40.7 us
    all_gather x1, blocking collectives, on_device(): up0 = lax.all_gather(up_block, 'dp', axis=0, tiled=True)  34.8 us
    all_gather x1, blocking collectives, on_device(): came = lax.all_gather(sent, 'tensor', axis=0, tiled=False)  14.7 us
    all_to_all x1, blocking collectives, swap(): return lax.all_to_all(value, axis, 0, 0, tiled=True)  10.9 us
    all_to_all x2, starting transfers between devices, swap(): return lax.all_to_all(value, axis, 0, 0, tiled=True)  9.25 us
  transfers between devices with their start and end apart: 6, of which 1 were waited for; matrix products, arithmetic and copies ran while one was open for 1% of the time, Pallas kernels for 7%

profile of v2, /device:TPU:10, one launch (start us, length us, event | category | flops | bytes accessed | tf_op | source)
XLA Modules:
  0.0 248.5 jit_solution(17569895654785796012)
XLA Ops:
  7.2 0.0 all-gather.5.cloned.1.call-start
  7.2 1.7 shard_map.156
  8.9 0.0 all-gather.5.cloned.1.call-update
  8.9 0.0 collective-permute-start
  8.9 1.7 collective-permute-start.1
  10.7 0.8 slice.6
  11.4 0.8 slice_bitcast_fusion
  12.2 42.2 %all-gather = bf16[1,2048,128]{2,1,0:T(8,128)(2,1)} all-gather(bf16[1,128,128]{2,1,0:T(8,128)(2,1)S(1)} %slice.6), channel_id=2, replica_groups=mesh['section'=8,'dp'=16,'tensor'=4] {'dp'}, dimensions={1}, use_global_device_ids=true | all-gather | bytes 557056 | tf_op jit(solution)/shard_map/all_gather | solution.py:498
  54.4 0.0 collective-permute-done.refs_0_.refs_2_.refs_6_.refs_4_.refs_3_
  54.4 0.0 copy-start
  54.4 0.9 copy-done
  55.3 4.0 %shard_map.154 = (f32[4,136,128]{2,1,0:T(8,128)}, f32[128,128]{1,0:T(8,128)}) custom-call(bf16[128,2048]{1,0:T(8,128)(2,1)} %copy-done, f32[2,2048]{1,0:T(2,128)} %refs_2_.7, s32[1,128]{1,0:T(1,128)} %bitcast.18, bf16[2048,128]{1,0:T(8,128)(2,1)} %bitcast.14), custom_call_target="tpu_custom_call" | custom-call | flops 100000000 | bytes 1409536 | tf_op jit(solution)/shard_map/pallas_call | solution.py:137
  59.3 4.5 %all-to-all-start = ((f32[4,136,128]{2,1,0:T(8,128)}), f32[4,136,128]{2,1,0:T(8,128)S(1)}, u32[]{:S(2)}, u32[]{:S(2)}) async-start(f32[4,136,128]{2,1,0:T(8,128)} %get-tuple-element.31), calls=%async_computation | async-start | bytes 557056 | tf_op jit(solution)/shard_map/all_to_all | solution.py:470
  63.8 34.8 %all_gather.19.refs_1_.refs_6_ = bf16[128,2048]{1,0:T(8,128)(2,1)} all-gather(bf16[8,2048]{1,0:T(8,128)(2,1)S(1)} %slice_bitcast_fusion), channel_id=1, replica_groups=mesh['section'=8,'dp'=16,'tensor'=4] {'dp'}, dimensions={0}, use_global_device_ids=true | all-gather | bytes 557056 | tf_op jit(solution)/shard_map/all_gather | solution.py:507
  98.6 0.0 all-to-all-done.refs_0_
  98.6 0.0 copy-start.3
  98.6 0.7 copy-done.3
  99.3 4.9 %shard_map.155 = (bf16[128,2048]{1,0:T(8,128)(2,1)}, f32[2048,128]{1,0:T(8,128)}, bf16[128,128]{1,0:T(8,128)(2,1)}, f32[3,128,128]{2,1,0:T(8,128)}) custom-call(f32[4,136,128]{2,1,0:T(8,128)} %copy-done.3, bf16[128,2048]{1,0:T(8,128)(2,1)} %all_gather.19.refs_1_.refs_6_, f32[128,128]{1,0:T(8,128)} %get-tuple-element.33.refs_2_.refs_6_, ...), custom_call_target="tpu_custom_call" | custom-call | flops 400000000 | bytes 3981312 | tf_op jit(solution)/shard_map/pallas_call | solution.py:137
  104.2 0.0 collective-permute-done.1.refs_4_.refs_5_
  104.2 0.0 copy-start.1
  104.2 0.0 all-gather.5.cloned.1.call-done
  104.3 0.8 copy-done.1
  105.0 4.0 %shard_map.157 = (bf16[768,128]{1,0:T(8,128)(2,1)}, bf16[128,128]{1,0:T(8,128)(2,1)}) custom-call(bf16[128,2048]{1,0:T(8,128)(2,1)} %get-tuple-element.34.refs_0_.refs_8_, bf16[16,6,128,128]{3,2,1,0:T(8,128)(2,1)} %bitcast.7, bf16[128,2048]{1,0:T(8,128)(2,1)} %copy-done, bf16[16,6,128,128]{3,2,1,0:T(8,128)(2,1)} %bitcast.8, bf16[128,2048]{1,0:T(8,128)(2,1)} %copy-done.1, ...), custom_call_target="tpu_custom_call" | custom-call | flops 500000000 | bytes 11255808 | tf_op jit(solution)/shard_map/pallas_call | solution.py:137
  109.0 14.7 %all-gather.2 = bf16[3072,128]{1,0:T(8,128)(2,1)} all-gather(bf16[768,128]{1,0:T(8,128)(2,1)} %get-tuple-element.35), channel_id=4, replica_groups=mesh['section'=8,'dp'=16,'tensor'=4] {'tensor'}, dimensions={0}, use_global_device_ids=true | all-gather | bytes 983040 | tf_op jit(solution)/shard_map/all_gather | solution.py:529
  123.7 6.3 %shard_map.158 = (bf16[4,384,128]{2,1,0:T(8,128)(2,1)}, bf16[128,2048]{1,0:T(8,128)(2,1)}, bf16[128,2048]{1,0:T(8,128)(2,1)}, bf16[3,128,128]{2,1,0:T(8,128)(2,1)}, f32[4,128,128]{2,1,0:T(8,128)}) custom-call(bf16[4,768,128]{2,1,0:T(8,128)(2,1)} %bitcast.16, f32[3,128,128]{2,1,0:T(8,128)} %get-tuple-element.36.refs_1_, bf16[2,128,2048]{2,1,0:T(8,128)(2,1)} %refs_2_.5, ...), custom_call_target="tpu_custom_call" | custom-call | flops 800000000 | bytes 10485760 | tf_op jit(solution)/shard_map/pallas_call | solution.py:137
  130.0 10.9 %all_to_all.15.refs_0_ = bf16[4,384,128]{2,1,0:T(8,128)(2,1)} all-to-all(bf16[4,384,128]{2,1,0:T(8,128)(2,1)} %get-tuple-element.39), channel_id=1, replica_groups=mesh['section'=8,'dp'=16,'tensor'=4] {'tensor'}, dimensions={0} | all-to-all | bytes 786432 | tf_op jit(solution)/shard_map/all_to_all | solution.py:470
  141.0 5.0 %shard_map.159 = (bf16[4,128,128]{2,1,0:T(8,128)(2,1)}, bf16[128,2048]{1,0:T(8,128)(2,1)}, bf16[3,128,128]{2,1,0:T(8,128)(2,1)}, f32[128,128]{1,0:T(8,128)}) custom-call(bf16[4,384,128]{2,1,0:T(8,128)(2,1)} %all_to_all.15.refs_0_, f32[4,128,128]{2,1,0:T(8,128)} %get-tuple-element.40.refs_1_.refs_2_, bf16[16,6,128,128]{3,2,1,0:T(8,128)(2,1)} %bitcast.12, ...), custom_call_target="tpu_custom_call" | custom-call | flops 400000000 | bytes 6455296 | tf_op jit(solution)/shard_map/pallas_call | solution.py:137
  145.9 4.8 %all-to-all-start.2 = ((bf16[4,128,128]{2,1,0:T(8,128)(2,1)}), bf16[4,128,128]{2,1,0:T(8,128)(2,1)S(1)}, u32[]{:S(2)}, u32[]{:S(2)}) async-start(bf16[4,128,128]{2,1,0:T(8,128)(2,1)} %get-tuple-element.49), calls=%async_computation.2 | async-start | bytes 262144 | tf_op jit(solution)/shard_map/all_to_all | solution.py:470
  150.7 0.0 reduce-scatter.2.cloned.1.call-start
  150.7 5.8 %shard_map.160 = (bf16[16,8,128,128]{3,2,1,0:T(8,128)(2,1)}, bf16[128,2048]{1,0:T(8,128)(2,1)}, f32[128,2048]{1,0:T(8,128)}) custom-call(bf16[3,128,128]{2,1,0:T(8,128)(2,1)} %get-tuple-element.38.refs_0_, bf16[3,128,128]{2,1,0:T(8,128)(2,1)} %get-tuple-element.42.refs_1_, f32[4,128,128]{2,1,0:T(8,128)} %get-tuple-element.40.refs_1_.refs_2_, ...), custom_call_target="tpu_custom_call" | custom-call | flops 1000000000 | bytes 12632064 | tf_op jit(solution)/shard_map/pallas_call | solution.py:137
  156.5 0.0 all-to-all-done.2.refs_0_
  156.5 0.0 copy-start.2
  156.5 0.6 copy-done.2
  157.2 3.5 %shard_map.162 = bf16[16,8,128,128]{3,2,1,0:T(8,128)(2,1)} custom-call(bf16[4,128,128]{2,1,0:T(8,128)(2,1)} %copy-done.2, f32[3,128,128]{2,1,0:T(8,128)} %get-tuple-element.36.refs_1_, f32[2,2048]{1,0:T(2,128)} %refs_2_.7, bf16[128,2048]{1,0:T(8,128)(2,1)} %copy-done, bf16[16,8,128,128]{3,2,1,0:T(8,128)(2,1)} %get-tuple-element.51.refs_4_), custom_call_target="tpu_custom_call", output_to_operand_aliasing={{}: (4, {})} | custom-call | flops 100000000 | bytes 9256960 | tf_op jit(solution)/shard_map/pallas_call | solution.py:137
  160.6 0.0 reduce-scatter.2.cloned.1.call-update
  160.6 3.8 %shard_map.161 = bf16[128,2048]{1,0:T(8,128)(2,1)} custom-call(bf16[4,128,128]{2,1,0:T(8,128)(2,1)} %copy-done.2, f32[3,128,128]{2,1,0:T(8,128)} %get-tuple-element.36.refs_1_, f32[2,2048]{1,0:T(2,128)} %refs_2_.7, bf16[2048,128]{1,0:T(8,128)(2,1)} %bitcast.15, bf16[128,2048]{1,0:T(8,128)(2,1)} %copy-done, f32[128,2048]{1,0:T(8,128)} %get-tuple-element.50.refs_5_), custom_call_target="tpu_custom_call" | custom-call | flops 100000000 | bytes 2965504 | tf_op jit(solution)/shard_map/pallas_call | solution.py:137
  164.4 75.4 %reduce-scatter.2.cloned.1.call-done = bf16[1,8,128,128]{3,2,1,0:T(8,128)(2,1)} async-done(((bf16[16,8,128,128]{3,2,1,0:T(8,128)(2,1)}), bf16[1,8,128,128]{3,2,1,0:T(8,128)(2,1)}) %reduce-scatter.2.cloned.1.call-update) | async-done | bytes 262160 | tf_op jit(solution)/shard_map/reduce_scatter | solution.py:593
  239.8 1.8 shard_map.163
Async XLA Ops:
  7.2 97.1 %all-gather.5.cloned.1.call-start = ((), (), s32[]{:S(2)}) async-start(), calls=%async_computation.5 | async-start | bytes 3342336 | tf_op jit(solution)/shard_map/all_gather | solution.py:495
  8.9 45.5 %collective-permute-start = (bf16[128,2048]{1,0:T(8,128)(2,1)}, bf16[128,2048]{1,0:T(8,128)(2,1)S(1)}, u32[]{:S(2)}, u32[]{:S(2)}) collective-permute-start(bf16[128,2048]{1,0:T(8,128)(2,1)} %param.11), channel_id=1, source_target_pairs={{0,64},{64,128},{128,192},{192,256},{256,320},{320,384},{384,448},... | collective-permute-start | bytes 1572872 | tf_op jit(solution)/shard_map/ppermute | solution.py:23
  8.9 95.3 %collective-permute-start.1 = (bf16[128,2048]{1,0:T(8,128)(2,1)}, bf16[128,2048]{1,0:T(8,128)(2,1)S(1)}, u32[]{:S(2)}, u32[]{:S(2)}) collective-permute-start(bf16[128,2048]{1,0:T(8,128)(2,1)} %param.12), channel_id=1, source_target_pairs={{0,448},{64,0},{128,64},{192,128},{256,192},{320,256},{384,320},{4... | collective-permute-start | bytes 1572872 | tf_op jit(solution)/shard_map/ppermute | solution.py:23
  54.4 0.9 copy-start
  59.3 39.3 %all-to-all-start = ((f32[4,136,128]{2,1,0:T(8,128)}), f32[4,136,128]{2,1,0:T(8,128)S(1)}, u32[]{:S(2)}, u32[]{:S(2)}) async-start(f32[4,136,128]{2,1,0:T(8,128)} %get-tuple-element.31), calls=%async_computation | async-start | bytes 557056 | tf_op jit(solution)/shard_map/all_to_all | solution.py:470
  98.6 0.7 copy-start.3
  104.2 0.8 copy-start.1
  145.9 10.6 %all-to-all-start.2 = ((bf16[4,128,128]{2,1,0:T(8,128)(2,1)}), bf16[4,128,128]{2,1,0:T(8,128)(2,1)S(1)}, u32[]{:S(2)}, u32[]{:S(2)}) async-start(bf16[4,128,128]{2,1,0:T(8,128)(2,1)} %get-tuple-element.49), calls=%async_computation.2 | async-start | bytes 262144 | tf_op jit(solution)/shard_map/all_to_all | solution.py:470
  150.7 89.1 %reduce-scatter.2.cloned.1.call-start = ((), (), s32[]{:S(2)}) async-start(), calls=%async_computation.4 | async-start | bytes 4456448 | tf_op jit(solution)/shard_map/reduce_scatter | solution.py:593
  156.5 0.7 copy-start.2
Sparse Core Ops, SparseCore 0:
  10.1 82.9 all-gather.4
  160.8 79.0 reduce-scatter.1

commit v3 on v2

--- a/solution.py
+++ b/solution.py
@@ -13,7 +13,7 @@
 BF16 = jnp.bfloat16
 VMEM_LIMIT = 58 << 20
 ALL = slice(None)
-A_OUT0, B_OUT0, A_QUERY1, B_OUT1, B_QUERY1, A_OUT1 = range(6)
+A_OUT0, B_OUT0, A_QUERY1, B_OUT1, B_QUERY1, A_OUT1, B_QUERY0 = range(7)
 TERM_A_QUERY, TERM_B_QUERY, TERM_A_OUT, TERM_B_OUT = 0, 2, 4, 6
 
 
@@ -59,13 +59,14 @@
 
 
 class Leaving:
-    def __init__(self, copy, ref):
-        self.copy, self.ref, self.sent = copy, ref, False
+    def __init__(self, copies, ref):
+        self.copies, self.ref, self.sent = copies, ref, False
         self.shape = ref.shape
 
     def send(self):
         if not self.sent:
-            self.copy.start()
+            for copy in self.copies:
+                copy.start()
             self.sent = True
 
     def __setitem__(self, at, value):
@@ -85,42 +86,44 @@
 
 
 def kernel_call(body, ins, outs, flops, alias=None):
-    hbm, vmem = pl.BlockSpec(memory_space=pltpu.HBM), pl.BlockSpec(memory_space=pltpu.VMEM)
-    scratch, in_count, out_count = [], len(ins), len(outs)
-    for index, item in enumerate(ins):
-        if isinstance(item, tuple) and index != alias:
-            scratch += [pltpu.VMEM(sliced(item[0].shape, at), item[0].dtype) for at in item[1]]
-    first_out = len(scratch)
-    for item in outs:
-        if isinstance(item, tuple):
-            scratch += [pltpu.VMEM(sliced(item[0].shape, at), item[0].dtype) for at in item[1]]
-    buffers = len(scratch)
+    hbm = pl.BlockSpec(memory_space=pltpu.HBM)
+    scratch, marks_needed, in_count, out_count = [], 0, len(ins), len(outs)
+    for index, (array, slices) in enumerate(ins):
+        if index != alias:
+            scratch += [pltpu.VMEM(sliced(array.shape, at), array.dtype) for at in slices]
+            marks_needed += len(slices)
+    for result, slices in outs:
+        for at in slices:
+            copies = at[0] if isinstance(at[0], tuple) else (at[0],)
+            marks_needed += len(copies)
+            scratch.append(
+                pltpu.VMEM(sliced(result.shape, (copies[0], *at[1:])), result.dtype)
+            )
 
     def run(*refs):
         in_refs, out_refs = refs[:in_count], refs[in_count : in_count + out_count]
-        places = refs[in_count + out_count :]
-        marks = places[buffers] if buffers else None
-        used, given, arriving, leaving = 0, [], [], []
-        for index, (ref, item) in enumerate(zip(in_refs, ins, strict=True)):
+        places, marks = refs[in_count + out_count : -1], refs[-1]
+        used, mark, given, arriving, leaving = 0, 0, [], [], []
+        for index, (ref, (_, slices)) in enumerate(zip(in_refs, ins, strict=True)):
             if index == alias:
                 continue
-            if not isinstance(item, tuple):
-                given.append(ref)
-                continue
-            for at in item[1]:
-                copy = pltpu.make_async_copy(ref.at[at], places[used], marks.at[used])
+            for at in slices:
+                copy = pltpu.make_async_copy(ref.at[at], places[used], marks.at[mark])
                 copy.start()
                 arriving.append(Arriving(copy, places[used]))
                 given.append(arriving[-1])
-                used += 1
-        assert used == first_out
-        for ref, item in zip(out_refs, outs, strict=True):
-            if not isinstance(item, tuple):
-                given.append(ref)
-                continue
-            for at in item[1]:
-                copy = pltpu.make_async_copy(places[used], ref.at[at], marks.at[used])
-                leaving.append(Leaving(copy, places[used]))
+                used, mark = used + 1, mark + 1
+        for ref, (_, slices) in zip(out_refs, outs, strict=True):
+            for at in slices:
+                copies = []
+                for first in at[0] if isinstance(at[0], tuple) else (at[0],):
+                    copies.append(
+                        pltpu.make_async_copy(
+                            places[used], ref.at[(first, *at[1:])], marks.at[mark]
+                        )
+                    )
+                    mark += 1
+                leaving.append(Leaving(copies, places[used]))
                 given.append(leaving[-1])
                 used += 1
         body(*given)
@@ -129,17 +132,17 @@
         for item in arriving:
             item.wait()
         for item in leaving:
-            item.copy.wait()
-
-    arrays = [item[0] if isinstance(item, tuple) else item for item in ins]
-    shapes = [item[0] if isinstance(item, tuple) else item for item in outs]
+            for copy in item.copies:
+                copy.wait()
+
+    arrays, shapes = [array for array, _ in ins], [result for result, _ in outs]
     size = sum(x.size * x.dtype.itemsize for x in (*arrays, *shapes))
     return pl.pallas_call(
         run,
         out_shape=shapes,
-        in_specs=[hbm if isinstance(item, tuple) else vmem for item in ins],
-        out_specs=[hbm if isinstance(item, tuple) else vmem for item in outs],
-        scratch_shapes=scratch + ([pltpu.SemaphoreType.DMA((buffers,))] if buffers else []),
+        in_specs=[hbm] * in_count,
+        out_specs=[hbm] * out_count,
+        scratch_shapes=[*scratch, pltpu.SemaphoreType.DMA((marks_needed,))],
         input_output_aliases={} if alias is None else {alias: 0},
         compiler_params=pltpu.CompilerParams(vmem_limit_bytes=VMEM_LIMIT),
         cost_estimate=pl.CostEstimate(flops=int(flops), bytes_accessed=size, transcendentals=0),
@@ -168,7 +171,12 @@
 
 
 def write_down(ref, value):
-    ref[...] = value.astype(BF16).reshape(ref.shape)
+    value = value.astype(BF16)
+    size = ref.shape[2] * ref.shape[1] // 128
+    for place in range(ref.shape[0]):
+        for part in range(size // 128):
+            at = place * size + part * 128
+            ref[place, part * 128 : (part + 1) * 128, :] = value[:, at : at + 128]
 
 
 def write_up(ref, value):
@@ -187,10 +195,10 @@
 
 
 def pack_body(*refs):
-    sources, ups, targets = refs[:3], refs[3:6], refs[6:12]
+    sources, ups, targets = refs[:3], refs[3:7], refs[7:14]
     for ref, place in zip(sources, (A_OUT0, A_QUERY1, A_OUT1), strict=True):
         targets[place][...] = ref[...]
-    for ref, place in zip(ups, (B_OUT0, B_OUT1, B_QUERY1), strict=True):
+    for ref, place in zip(ups, (B_OUT0, B_OUT1, B_QUERY1, B_QUERY0), strict=True):
         rows, width = ref.shape
         value = ref[...].astype(F32)
         for pair in range(width // 256):
@@ -206,7 +214,10 @@
 def unpack_body(came, a_query_ref, b_query_ref, a_out_ref, b_out_ref):
     for layer in range(2):
         for ref, place in ((a_query_ref, TERM_A_QUERY), (a_out_ref, TERM_A_OUT)):
-            ref[layer] = came[place + layer].astype(F32)
+            value = came[place + layer].astype(F32)
+            for part in range(value.shape[0] // 128):
+                at = slice(part * 128, (part + 1) * 128)
+                ref[layer, at, :] = jnp.transpose(value[at])
         for ref, place in ((b_query_ref, TERM_B_QUERY), (b_out_ref, TERM_B_OUT)):
             rows, width = ref.shape[1:]
             value = came[place + layer].astype(F32)
@@ -233,9 +244,8 @@
         preferred_element_type=F32,
         precision=lax.Precision.HIGHEST,
     )
-    for peer in range(sent_ref.shape[0]):
-        sent_ref[peer, :128, :] = projected
-        sent_ref[peer, 128:, :] = squares
+    sent_ref[:128, :] = projected
+    sent_ref[128:, :] = squares
 
 
 def to_column(row):
@@ -288,9 +298,10 @@
     return (dot(back_scores.astype(BF16), keys) * HEAD_DIM ** (-0.5)).astype(BF16)
 
 
-def forward0_body(
-    came_ref, up_ref, bias_ref, query_ref, key_ref, value_ref, attended_ref, probability_ref,
-    rank_ref, small_ref,
+def layer0_body(
+    came_ref, query_ref, up_query_ref, key_ref, value_ref, bias_ref, hidden_ref, gain_ref,
+    down_output_ref, up0_ref, down1_ref, up1_ref, cot_ref,
+    sent_ref, attended_ref, probability_ref, rank_ref, small_ref, kept_ref,
 ):
     projected = total(came_ref)
     squares = came_ref[0, 128:129, :]
@@ -306,29 +317,24 @@
     rank_ref.send()
     small_ref.send()
     bias = jnp.concatenate([bias_ref[...]] * HEADS_AT_ONCE, axis=0)
-    queries = (query_ref[...].astype(F32) + dot(rank_query, up_ref[...])).astype(BF16)
+    queries = (query_ref[...].astype(F32) + dot(rank_query, read_up(up_query_ref))).astype(BF16)
     for head, shared in head_blocks(query_ref, key_ref):
         probability = softmax_of(stacked(queries, head), key_ref[:, shared], bias)
         probability_ref[head * 128 : (head + HEADS_AT_ONCE) * 128, :] = probability
         spread(
             attended_ref, head, dot(probability.astype(BF16), value_ref[:, shared]).astype(BF16)
         )
-
-
-def second_body(
-    attended_ref, down_output_ref, hidden_ref, up0_ref, down1_ref, cot_ref, up1_ref, gain_ref,
-    sent_ref, kept_ref,
-):
-    sent_ref[:128, :] = dot(attended_ref[...], read_down(down_output_ref)).astype(BF16)
+    probability_ref.send()
+    attended_ref.send()
     hidden, gain = hidden_ref[...], gain_ref[...]
-    up0 = read_up(up0_ref)
+    up0, down1, cot = read_up(up0_ref), read_down(down1_ref), cot_ref[...]
     sent_ref[512:640, :] = dot_cols(hidden, up0).astype(BF16)
     sent_ref[640:, :] = dot_cols(up0, up0).astype(BF16)
-    down1 = read_down(down1_ref)
     sent_ref[128:256, :] = dot((hidden.astype(F32) * gain).astype(BF16), down1).astype(BF16)
     sent_ref[256:384, :] = dot((up0.astype(F32) * gain).astype(BF16), down1).astype(BF16)
-    cot = cot_ref[...]
     sent_ref[384:512, :] = dot_cols(cot, read_up(up1_ref)).astype(BF16)
+    sent_ref[:128, :] = dot(attended_ref[...], read_down(down_output_ref)).astype(BF16)
+    sent_ref.send()
     kept_ref[...] = dot_cols(cot, up0).astype(BF16)
 
 
@@ -375,10 +381,9 @@
     back_query_ref.send()
     rank_output = dot(attended_ref[...], down_output).astype(BF16)
     back_rank = dot_cols(back_query_ref[...], up_query).astype(BF16)
-    for peer in range(sent_ref.shape[0]):
-        sent_ref[peer, :128, :] = rank_output
-        sent_ref[peer, 128:256, :] = back_rank
-        sent_ref[peer, 256:, :] = kept_ref[...]
+    sent_ref[:128, :] = rank_output
+    sent_ref[128:256, :] = back_rank
+    sent_ref[256:, :] = kept_ref[...]
 
 
 def backward0_body(
@@ -413,9 +418,8 @@
             ),
         )
     back_query_ref.send()
-    back_rank = dot_cols(back_query_ref[...], up_ref[...]).astype(BF16)
-    for peer in range(sent_ref.shape[0]):
-        sent_ref[peer] = back_rank
+    back_rank = dot_cols(back_query_ref[...], read_up(up_ref)).astype(BF16)
+    sent_ref[...] = back_rank
 
 
 def terms_body(
@@ -430,7 +434,7 @@
     b_out1.send()
     gain, scale, pull = gain_ref[...], small_ref[1, :, :1], pull_ref[:, :1]
     hidden = hidden_ref[...].astype(F32) + dot(rank_output0, read_up(up0_ref))
-    write_down(a_query1, dot_rows((hidden * scale * gain).astype(BF16), back_rank1))
+    write_down(a_query1, dot_rows(back_rank1, (hidden * scale * gain).astype(BF16)))
     a_query1.send()
     gained = gain * dot_cols(back_rank1, read_down(down1_ref))
     gradient = cot.astype(F32) + scale * gained - hidden * pull
@@ -440,9 +444,9 @@
     b_out0.send()
     out_ref[...] = (hidden + dot(rank_output1, read_up(up1_ref))).astype(BF16)
     out_ref.send()
-    write_down(a_out0, dot_rows(attended0_ref[...], back_output0))
+    write_down(a_out0, dot_rows(back_output0, attended0_ref[...]))
     a_out0.send()
-    write_down(a_out1, dot_rows(attended1_ref[...], back_output1))
+    write_down(a_out1, dot_rows(back_output1, attended1_ref[...]))
     a_out1.send()
     write_up(b_query1, dot_rows(rank_query1, back_query1_ref[...]))
     b_query1.send()
@@ -451,7 +455,7 @@
 
 def last_term_body(came_ref, small_ref, gain_ref, hidden_ref, a_query0):
     normed = (hidden_ref[...].astype(F32) * small_ref[1, :, :1] * gain_ref[...]).astype(BF16)
-    write_down(a_query0, dot_rows(normed, total(came_ref).astype(BF16)))
+    write_down(a_query0, dot_rows(total(came_ref).astype(BF16), normed))
 
 
 def cot_body(came_ref, small_ref, gain_ref, down_ref, hidden_ref, gradient_ref, cot_ref):
@@ -479,65 +483,64 @@
     length = rows * width // 128
     heads = width // HEAD_DIM
     block = whole(shape((128, width), BF16))
+    ranks = whole(shape((3, 128, 128), BF16))
     layer0, layer1 = [(0,)], [(1,)]
     gain0, gain1 = (gains, [(slice(0, 1),)]), (gains, [(slice(1, 2),)])
-    factor = [(ALL, member) for member in range(6)]
+    peers = [(tuple(range(ways)),)]
 
     (shard,) = kernel_call(
         pack_body,
         [
             (a_out, layer0), (a_query, layer1), (a_out, layer1),
-            (b_out, layer0), (b_out, layer1), (b_query, layer1),
-        ],
-        [(shape((6, length, 128), BF16), [(member,) for member in range(6)])],
+            (b_out, layer0), (b_out, layer1), (b_query, layer1), (b_query, layer0),
+        ],
+        [(shape((7, length, 128), BF16), [(member,) for member in range(7)])],
         0,
     )
     stack = lax.all_gather(shard, "dp", axis=0, tiled=False)
+
+    def factor(*members):
+        return (stack, [(ALL, member) for member in members])
+
     hidden = from_behind(arrived, "section", 1)
     cot = from_behind(cot_later, "section", -1)
     down0 = lax.all_gather(a_query[0], "dp", axis=0, tiled=True)
     sent, bias = kernel_call(
         first_body,
-        [whole(hidden), gain0, parents.reshape(1, 128), down0],
-        [shape((ways, 136, 128), F32), shape((128, 128), F32)],
+        [whole(hidden), gain0, whole(parents.reshape(1, 128)), whole(down0)],
+        [(shape((ways, 136, 128), F32), peers), whole(shape((128, 128), F32))],
         1e8,
     )
     came = swap(sent, "tensor")
-    up_block, _ = lax.optimization_barrier((b_query[0], sent))
-    up0 = lax.all_gather(up_block, "dp", axis=0, tiled=True)
-    attended0, probability, rank_query0, small0 = kernel_call(
-        forward0_body,
-        [came, up0, bias, (q_base, layer0), (k_base, layer0), (v_base, layer0)],
-        [
+    sent, attended0, probability, rank_query0, small0, kept = kernel_call(
+        layer0_body,
+        [
+            whole(came), (q_base, layer0), factor(B_QUERY0), (k_base, layer0), (v_base, layer0),
+            whole(bias), whole(hidden), gain1, factor(A_OUT0, B_OUT0, A_QUERY1, B_OUT1),
+            whole(cot),
+        ],
+        [
+            whole(shape((768, 128), BF16)),
             block,
             whole(shape((heads * 128, 128), F32)),
             whole(shape((128, 128), BF16)),
             whole(shape((3, 128, 128), F32)),
-        ],
-        4e8,
-    )
-    sent, kept = kernel_call(
-        second_body,
-        [
-            whole(attended0), (stack, [factor[A_OUT0]]), whole(hidden),
-            (stack, [factor[B_OUT0], factor[A_QUERY1]]), whole(cot), (stack, [factor[B_OUT1]]),
-            gain1,
-        ],
-        [shape((768, 128), BF16), shape((128, 128), BF16)],
-        5e8,
+            whole(shape((128, 128), BF16)),
+        ],
+        9e8,
     )
     came = lax.all_gather(sent, "tensor", axis=0, tiled=False)
     sent, attended1, back_query1, ranks1, small1 = kernel_call(
         layer1_body,
         [
-            came, whole(small0), (q_base, layer1), (stack, [factor[B_QUERY1]]), (k_base, layer1),
-            (v_base, layer1), bias, (stack, [factor[A_OUT1]]), kept,
-        ],
-        [
-            shape((ways, 384, 128), BF16),
+            whole(came), whole(small0), (q_base, layer1), factor(B_QUERY1), (k_base, layer1),
+            (v_base, layer1), whole(bias), factor(A_OUT1), whole(kept),
+        ],
+        [
+            (shape((ways, 384, 128), BF16), peers),
             block,
             block,
-            whole(shape((3, 128, 128), BF16)),
+            ranks,
             whole(shape((4, 128, 128), F32)),
         ],
         8e8,
@@ -546,38 +549,32 @@
     sent, back_query0, ranks2, pull = kernel_call(
         backward0_body,
         [
-            came, whole(small1), (stack, [factor[A_OUT0]]), (k_base, layer0), (v_base, layer0),
-            whole(probability), whole(up0),
-        ],
-        [
-            shape((ways, 128, 128), BF16),
+            whole(came), whole(small1), factor(A_OUT0), (k_base, layer0), (v_base, layer0),
+            whole(probability), factor(B_QUERY0),
+        ],
+        [
+            (shape((ways, 128, 128), BF16), peers),
             block,
-            whole(shape((3, 128, 128), BF16)),
+            ranks,
             whole(shape((128, 128), F32)),
         ],
         4e8,
     )
     came = swap(sent, "tensor")
     term_shape = shape((count, 8, length, 128), BF16)
+    made_first = (
+        TERM_A_QUERY + 1, TERM_B_QUERY, TERM_B_QUERY + 1, TERM_A_OUT, TERM_A_OUT + 1,
+        TERM_B_OUT, TERM_B_OUT + 1,
+    )
     terms, section_out, gradient = kernel_call(
         terms_body,
         [
             whole(ranks1), whole(ranks2), whole(small1), whole(pull), gain1, whole(cot),
-            whole(hidden), (stack, [factor[B_OUT0], factor[A_QUERY1], factor[B_OUT1]]),
-            whole(attended0), whole(attended1), whole(rank_query0), whole(back_query0),
-            whole(back_query1),
-        ],
-        [
-            (
-                term_shape,
-                [
-                    (ALL, member)
-                    for member in (
-                        TERM_A_QUERY + 1, TERM_B_QUERY, TERM_B_QUERY + 1, TERM_A_OUT,
-                        TERM_A_OUT + 1, TERM_B_OUT, TERM_B_OUT + 1,
-                    )
-                ],
-            ),
+            whole(hidden), factor(B_OUT0, A_QUERY1, B_OUT1), whole(attended0), whole(attended1),
+            whole(rank_query0), whole(back_query0), whole(back_query1),
+        ],
+        [
+            (term_shape, [(ALL, member) for member in made_first]),
             block,
             whole(shape((128, width), F32)),
         ],
@@ -585,7 +582,7 @@
     )
     (terms,) = kernel_call(
         last_term_body,
-        [came, whole(small0), gain0, whole(hidden), whole(terms)],
+        [whole(came), whole(small0), gain0, whole(hidden), whole(terms)],
         [(term_shape, [(ALL, TERM_A_QUERY)])],
         1e8,
         alias=4,
@@ -593,7 +590,7 @@
     reduced = lax.psum_scatter(terms, "dp", scatter_dimension=0, tiled=False)
     (cot_send,) = kernel_call(
         cot_body,
-        [came, whole(small0), gain0, whole(down0), whole(hidden), whole(gradient)],
+        [whole(came), whole(small0), gain0, whole(down0), whole(hidden), whole(gradient)],
         [block],
         1e8,
     )

time: 249 us -> 233 us (0.936)
  the two profiles are of different devices: /device:TPU:10 before, /device:TPU:2 now
where the time goes in v3:
time: 233 us
  waiting for transfers between devices  104 us (45%)
  blocking collectives  69.4 us (30%)
  Pallas kernels  32.6 us (14%)
  between operations  14.1 us (6%)
  starting transfers between devices  9.94 us (4%)
    reduce_scatter x1, waiting for transfers between devices, on_device(): reduced = lax.psum_scatter(terms, 'dp', scatter_dimension=0, tiled=False)  74.5 us
    all_gather x1, blocking collectives, on_device(): down0 = lax.all_gather(a_query[0], 'dp', axis=0, tiled=True)  42.9 us
    pallas_call x9, Pallas kernels, kernel_call(): pl.pallas_call(run, out_shape=shapes, in_specs=[hbm] * in_count, out_spec...  32.6 us
    all_gather x1, waiting for transfers between devices, on_device(): stack = lax.all_gather(shard, 'dp', axis=0, tiled=False)  22.7 us
    all_gather x1, blocking collectives, on_device(): came = lax.all_gather(sent, 'tensor', axis=0, tiled=False)  14.7 us
    all_to_all x1, blocking collectives, swap(): return lax.all_to_all(value, axis, 0, 0, tiled=True)  11.7 us
    all_to_all x2, starting transfers between devices, swap(): return lax.all_to_all(value, axis, 0, 0, tiled=True)  7.93 us
    all_to_all x2, waiting for transfers between devices, swap(): return lax.all_to_all(value, axis, 0, 0, tiled=True)  7.08 us
  transfers between devices with their start and end apart: 6, of which 4 were waited for; matrix products, arithmetic and copies ran while one was open for 0% of the time, Pallas kernels for 5%

profile of v3, /device:TPU:2, one launch (start us, length us, event | category | flops | bytes accessed | tf_op | source)
XLA Modules:
  0.0 232.6 jit_solution(9504447281347122747)
XLA Ops:
  7.2 0.0 all-gather.5.cloned.1.call-start
  7.2 1.7 shard_map.155
  8.9 0.0 all-gather.5.cloned.1.call-update
  8.9 0.0 collective-permute-start
  9.0 1.7 collective-permute-start.1
  10.7 0.8 slice.3
  11.5 42.9 %all-gather = bf16[1,2048,128]{2,1,0:T(8,128)(2,1)} all-gather(bf16[1,128,128]{2,1,0:T(8,128)(2,1)S(1)} %slice.3), channel_id=2, replica_groups=mesh['section'=8,'dp'=16,'tensor'=4] {'dp'}, dimensions={1}, use_global_device_ids=true | all-gather | bytes 557056 | tf_op jit(solution)/shard_map/all_gather | solution.py:507
  54.4 0.0 collective-permute-done.refs_0_.refs_6_.refs_4_.refs_3_
  54.4 0.0 copy-start
  54.4 0.8 copy-done
  55.2 4.0 %shard_map.154 = (f32[4,136,128]{2,1,0:T(8,128)}, f32[128,128]{1,0:T(8,128)}) custom-call(bf16[128,2048]{1,0:T(8,128)(2,1)} %copy-done, f32[2,2048]{1,0:T(2,128)} %refs_2_.7, s32[1,128]{1,0:T(1,128)} %bitcast.16, bf16[2048,128]{1,0:T(8,128)(2,1)} %bitcast.12), custom_call_target="tpu_custom_call" | custom-call | flops 100000000 | bytes 1409536 | tf_op jit(solution)/shard_map/pallas_call | solution.py:140
  59.2 4.6 %all-to-all-start = ((f32[4,136,128]{2,1,0:T(8,128)}), f32[4,136,128]{2,1,0:T(8,128)S(1)}, u32[]{:S(2)}, u32[]{:S(2)}) async-start(f32[4,136,128]{2,1,0:T(8,128)} %get-tuple-element.30), calls=%async_computation | async-start | bytes 557056 | tf_op jit(solution)/shard_map/all_to_all | solution.py:474
  63.8 0.0 collective-permute-done.1.refs_9_.refs_5_
  63.8 0.0 copy-start.1
  63.8 6.8 %all-to-all-done.refs_0_ = f32[4,136,128]{2,1,0:T(8,128)S(1)} async-done(((f32[4,136,128]{2,1,0:T(8,128)}), f32[4,136,128]{2,1,0:T(8,128)S(1)}, u32[]{:S(2)}, u32[]{:S(2)}) %all-to-all-start) | async-done | bytes 278560 | tf_op jit(solution)/shard_map/all_to_all | solution.py:474
  70.5 0.0 copy-start.3
  70.5 22.7 %all-gather.5.cloned.1.call-done = bf16[112,128,128]{2,1,0:T(8,128)(2,1)} async-done(((bf16[7,128,128]{2,1,0:T(8,128)(2,1)}), bf16[112,128,128]{2,1,0:T(8,128)(2,1)}) %all-gather.5.cloned.1.call-update) | async-done | bytes 3670032 | tf_op jit(solution)/shard_map/all_gather | solution.py:500
  93.2 0.0 copy-done.1
  93.2 0.0 copy-done.3
  93.2 5.5 %shard_map.156 = (bf16[768,128]{1,0:T(8,128)(2,1)}, bf16[128,2048]{1,0:T(8,128)(2,1)}, f32[2048,128]{1,0:T(8,128)}, bf16[128,128]{1,0:T(8,128)(2,1)}, f32[3,128,128]{2,1,0:T(8,128)}, /*index=5*/bf16[128,128]{1,0:T(8,128)(2,1)}) custom-call(f32[4,136,128]{2,1,0:T(8,128)} %copy-done.3, bf16[2,128,2048]{2,1,0:T(8,128)(2,1)} %refs_2_.5, ...), custom_call_target="tpu_custom_call" | custom-call | flops 900000000 | bytes 12091392 | tf_op jit(solution)/shard_map/pallas_call | solution.py:140
  98.7 14.7 %all-gather.2 = bf16[3072,128]{1,0:T(8,128)(2,1)} all-gather(bf16[768,128]{1,0:T(8,128)(2,1)} %get-tuple-element.32), channel_id=4, replica_groups=mesh['section'=8,'dp'=16,'tensor'=4] {'tensor'}, dimensions={0}, use_global_device_ids=true | all-gather | bytes 983040 | tf_op jit(solution)/shard_map/all_gather | solution.py:532
  113.4 4.9 %shard_map.157 = (bf16[4,384,128]{2,1,0:T(8,128)(2,1)}, bf16[128,2048]{1,0:T(8,128)(2,1)}, bf16[128,2048]{1,0:T(8,128)(2,1)}, bf16[3,128,128]{2,1,0:T(8,128)(2,1)}, f32[4,128,128]{2,1,0:T(8,128)}) custom-call(bf16[4,768,128]{2,1,0:T(8,128)(2,1)} %bitcast.14, f32[3,128,128]{2,1,0:T(8,128)} %get-tuple-element.33.refs_1_, bf16[2,128,2048]{2,1,0:T(8,128)(2,1)} %refs_2_.5, ...), custom_call_target="tpu_custom_call" | custom-call | flops 800000000 | bytes 11534336 | tf_op jit(solution)/shard_map/pallas_call | solution.py:140
  118.3 11.7 %all_to_all.15.refs_0_ = bf16[4,384,128]{2,1,0:T(8,128)(2,1)} all-to-all(bf16[4,384,128]{2,1,0:T(8,128)(2,1)} %get-tuple-element.36), channel_id=1, replica_groups=mesh['section'=8,'dp'=16,'tensor'=4] {'tensor'}, dimensions={0} | all-to-all | bytes 786432 | tf_op jit(solution)/shard_map/all_to_all | solution.py:474
  130.0 3.8 %shard_map.158 = (bf16[4,128,128]{2,1,0:T(8,128)(2,1)}, bf16[128,2048]{1,0:T(8,128)(2,1)}, bf16[3,128,128]{2,1,0:T(8,128)(2,1)}, f32[128,128]{1,0:T(8,128)}) custom-call(bf16[4,384,128]{2,1,0:T(8,128)(2,1)} %all_to_all.15.refs_0_, f32[4,128,128]{2,1,0:T(8,128)} %get-tuple-element.37.refs_1_.refs_2_, bf16[16,7,128,128]{3,2,1,0:T(8,128)(2,1)} %bitcast.9, ...), custom_call_target="tpu_custom_call" | custom-call | flops 400000000 | bytes 10125312 | tf_op jit(solution)/shard_map/pallas_call | solution.py:140
  133.8 3.3 %all-to-all-start.2 = ((bf16[4,128,128]{2,1,0:T(8,128)(2,1)}), bf16[4,128,128]{2,1,0:T(8,128)(2,1)S(1)}, u32[]{:S(2)}, u32[]{:S(2)}) async-start(bf16[4,128,128]{2,1,0:T(8,128)(2,1)} %get-tuple-element.47), calls=%async_computation.2 | async-start | bytes 262144 | tf_op jit(solution)/shard_map/all_to_all | solution.py:474
  137.1 0.2 reduce-scatter.2.cloned.1.call-start
  137.3 5.4 %shard_map.159 = (bf16[16,8,128,128]{3,2,1,0:T(8,128)(2,1)}, bf16[128,2048]{1,0:T(8,128)(2,1)}, f32[128,2048]{1,0:T(8,128)}) custom-call(bf16[3,128,128]{2,1,0:T(8,128)(2,1)} %get-tuple-element.35.refs_0_, bf16[3,128,128]{2,1,0:T(8,128)(2,1)} %get-tuple-element.39.refs_1_, f32[4,128,128]{2,1,0:T(8,128)} %get-tuple-element.37.refs_1_.refs_2_, ...), custom_call_target="tpu_custom_call" | custom-call | flops 1000000000 | bytes 13156352 | tf_op jit(solution)/shard_map/pallas_call | solution.py:140
  142.7 0.3 all-to-all-done.2.refs_0_
  143.1 0.0 copy-start.2
  143.1 0.7 copy-done.2
  143.7 2.7 %shard_map.161 = bf16[16,8,128,128]{3,2,1,0:T(8,128)(2,1)} custom-call(bf16[4,128,128]{2,1,0:T(8,128)(2,1)} %copy-done.2, f32[3,128,128]{2,1,0:T(8,128)} %get-tuple-element.33.refs_1_, f32[2,2048]{1,0:T(2,128)} %refs_2_.7, bf16[128,2048]{1,0:T(8,128)(2,1)} %copy-done, bf16[16,8,128,128]{3,2,1,0:T(8,128)(2,1)} %get-tuple-element.49.refs_4_), custom_call_target="tpu_custom_call", output_to_operand_aliasing={{}: (4, {})} | custom-call | flops 100000000 | bytes 9256960 | tf_op jit(solution)/shard_map/pallas_call | solution.py:140
  146.4 0.0 reduce-scatter.2.cloned.1.call-update
  146.4 2.9 %shard_map.160 = bf16[128,2048]{1,0:T(8,128)(2,1)} custom-call(bf16[4,128,128]{2,1,0:T(8,128)(2,1)} %copy-done.2, f32[3,128,128]{2,1,0:T(8,128)} %get-tuple-element.33.refs_1_, f32[2,2048]{1,0:T(2,128)} %refs_2_.7, bf16[2048,128]{1,0:T(8,128)(2,1)} %bitcast.13, bf16[128,2048]{1,0:T(8,128)(2,1)} %copy-done, f32[128,2048]{1,0:T(8,128)} %get-tuple-element.48.refs_5_), custom_call_target="tpu_custom_call" | custom-call | flops 100000000 | bytes 2965504 | tf_op jit(solution)/shard_map/pallas_call | solution.py:140
  149.4 74.5 %reduce-scatter.2.cloned.1.call-done = bf16[1,8,128,128]{3,2,1,0:T(8,128)(2,1)} async-done(((bf16[16,8,128,128]{3,2,1,0:T(8,128)(2,1)}), bf16[1,8,128,128]{3,2,1,0:T(8,128)(2,1)}) %reduce-scatter.2.cloned.1.call-update) | async-done | bytes 262160 | tf_op jit(solution)/shard_map/reduce_scatter | solution.py:590
  223.9 1.9 shard_map.162
Async XLA Ops:
  7.2 86.0 %all-gather.5.cloned.1.call-start = ((), (), s32[]{:S(2)}) async-start(), calls=%async_computation.5 | async-start | bytes 3899392 | tf_op jit(solution)/shard_map/all_gather | solution.py:500
  8.9 45.4 %collective-permute-start = (bf16[128,2048]{1,0:T(8,128)(2,1)}, bf16[128,2048]{1,0:T(8,128)(2,1)S(1)}, u32[]{:S(2)}, u32[]{:S(2)}) collective-permute-start(bf16[128,2048]{1,0:T(8,128)(2,1)} %param.11), channel_id=1, source_target_pairs={{0,64},{64,128},{128,192},{192,256},{256,320},{320,384},{384,448},... | collective-permute-start | bytes 1572872 | tf_op jit(solution)/shard_map/ppermute | solution.py:23
  9.0 54.8 %collective-permute-start.1 = (bf16[128,2048]{1,0:T(8,128)(2,1)}, bf16[128,2048]{1,0:T(8,128)(2,1)S(1)}, u32[]{:S(2)}, u32[]{:S(2)}) collective-permute-start(bf16[128,2048]{1,0:T(8,128)(2,1)} %param.12), channel_id=1, source_target_pairs={{0,448},{64,0},{128,64},{192,128},{256,192},{320,256},{384,320},{4... | collective-permute-start | bytes 1572872 | tf_op jit(solution)/shard_map/ppermute | solution.py:23
  54.4 0.8 copy-start
  59.2 11.4 %all-to-all-start = ((f32[4,136,128]{2,1,0:T(8,128)}), f32[4,136,128]{2,1,0:T(8,128)S(1)}, u32[]{:S(2)}, u32[]{:S(2)}) async-start(f32[4,136,128]{2,1,0:T(8,128)} %get-tuple-element.30), calls=%async_computation | async-start | bytes 557056 | tf_op jit(solution)/shard_map/all_to_all | solution.py:474
  63.8 29.4 %copy-start.1 = (bf16[128,2048]{1,0:T(8,128)(2,1)}, bf16[128,2048]{1,0:T(8,128)(2,1)S(1)}, u32[]{:S(2)}) copy-start(bf16[128,2048]{1,0:T(8,128)(2,1)S(1)} %collective-permute-done.1.refs_9_.refs_5_) | copy-start | bytes 1572868
  70.5 22.7 %copy-start.3 = (f32[4,136,128]{2,1,0:T(8,128)}, f32[4,136,128]{2,1,0:T(8,128)S(1)}, u32[]{:S(2)}) copy-start(f32[4,136,128]{2,1,0:T(8,128)S(1)} %all-to-all-done.refs_0_) | copy-start | bytes 835588
  133.8 9.3 %all-to-all-start.2 = ((bf16[4,128,128]{2,1,0:T(8,128)(2,1)}), bf16[4,128,128]{2,1,0:T(8,128)(2,1)S(1)}, u32[]{:S(2)}, u32[]{:S(2)}) async-start(bf16[4,128,128]{2,1,0:T(8,128)(2,1)} %get-tuple-element.47), calls=%async_computation.2 | async-start | bytes 262144 | tf_op jit(solution)/shard_map/all_to_all | solution.py:474
  137.1 86.8 %reduce-scatter.2.cloned.1.call-start = ((), (), s32[]{:S(2)}) async-start(), calls=%async_computation.4 | async-start | bytes 4456448 | tf_op jit(solution)/shard_map/reduce_scatter | solution.py:590
  143.1 0.7 copy-start.2
Sparse Core Ops, SparseCore 0:
  10.1 83.0 all-gather.4
  146.5 77.2 reduce-scatter.1

commit v4 on v3

--- a/solution.py
+++ b/solution.py
@@ -11,7 +11,7 @@
 EPSILON = 1e-05
 F32 = jnp.float32
 BF16 = jnp.bfloat16
-VMEM_LIMIT = 58 << 20
+VMEM_LIMIT = 20 << 20
 ALL = slice(None)
 A_OUT0, B_OUT0, A_QUERY1, B_OUT1, B_QUERY1, A_OUT1, B_QUERY0 = range(7)
 TERM_A_QUERY, TERM_B_QUERY, TERM_A_OUT, TERM_B_OUT = 0, 2, 4, 6
@@ -68,6 +68,21 @@
             for copy in self.copies:
                 copy.start()
             self.sent = True
+
+    def __setitem__(self, at, value):
+        self.ref[at] = value
+
+    def __getitem__(self, at):
+        return self.ref[at]
+
+
+class Staying:
+    def __init__(self, ref):
+        self.ref = ref
+        self.shape = ref.shape
+
+    def send(self):
+        pass
 
     def __setitem__(self, at, value):
         self.ref[at] = value
@@ -85,36 +100,48 @@
     return tuple(result)
 
 
+class Near:
+    def __init__(self, array, *slices):
+        self.array, self.slices = array, slices
+
+
 def kernel_call(body, ins, outs, flops, alias=None):
-    hbm = pl.BlockSpec(memory_space=pltpu.HBM)
+    hbm, vmem = pl.BlockSpec(memory_space=pltpu.HBM), pl.BlockSpec(memory_space=pltpu.VMEM)
     scratch, marks_needed, in_count, out_count = [], 0, len(ins), len(outs)
-    for index, (array, slices) in enumerate(ins):
-        if index != alias:
-            scratch += [pltpu.VMEM(sliced(array.shape, at), array.dtype) for at in slices]
-            marks_needed += len(slices)
-    for result, slices in outs:
-        for at in slices:
-            copies = at[0] if isinstance(at[0], tuple) else (at[0],)
-            marks_needed += len(copies)
-            scratch.append(
-                pltpu.VMEM(sliced(result.shape, (copies[0], *at[1:])), result.dtype)
-            )
+    for index, item in enumerate(ins):
+        if index != alias and not isinstance(item, Near):
+            scratch += [pltpu.VMEM(sliced(item[0].shape, at), item[0].dtype) for at in item[1]]
+            marks_needed += len(item[1])
+    for item in outs:
+        if not isinstance(item, Near):
+            for at in item[1]:
+                copies = at[0] if isinstance(at[0], tuple) else (at[0],)
+                marks_needed += len(copies)
+                scratch.append(
+                    pltpu.VMEM(sliced(item[0].shape, (copies[0], *at[1:])), item[0].dtype)
+                )
 
     def run(*refs):
         in_refs, out_refs = refs[:in_count], refs[in_count : in_count + out_count]
         places, marks = refs[in_count + out_count : -1], refs[-1]
         used, mark, given, arriving, leaving = 0, 0, [], [], []
-        for index, (ref, (_, slices)) in enumerate(zip(in_refs, ins, strict=True)):
+        for index, (ref, item) in enumerate(zip(in_refs, ins, strict=True)):
             if index == alias:
                 continue
-            for at in slices:
+            if isinstance(item, Near):
+                given += [ref.at[at] for at in item.slices] if item.slices else [ref]
+                continue
+            for at in item[1]:
                 copy = pltpu.make_async_copy(ref.at[at], places[used], marks.at[mark])
                 copy.start()
                 arriving.append(Arriving(copy, places[used]))
                 given.append(arriving[-1])
                 used, mark = used + 1, mark + 1
-        for ref, (_, slices) in zip(out_refs, outs, strict=True):
-            for at in slices:
+        for ref, item in zip(out_refs, outs, strict=True):
+            if isinstance(item, Near):
+                given.append(Staying(ref))
+                continue
+            for at in item[1]:
                 copies = []
                 for first in at[0] if isinstance(at[0], tuple) else (at[0],):
                     copies.append(
@@ -135,18 +162,29 @@
             for copy in item.copies:
                 copy.wait()
 
-    arrays, shapes = [array for array, _ in ins], [result for result, _ in outs]
+    arrays = [item.array if isinstance(item, Near) else item[0] for item in ins]
+    shapes = [item.array if isinstance(item, Near) else item[0] for item in outs]
     size = sum(x.size * x.dtype.itemsize for x in (*arrays, *shapes))
     return pl.pallas_call(
         run,
-        out_shape=shapes,
-        in_specs=[hbm] * in_count,
-        out_specs=[hbm] * out_count,
-        scratch_shapes=[*scratch, pltpu.SemaphoreType.DMA((marks_needed,))],
+        out_shape=[
+            result if isinstance(item, Near) else pltpu.HBM(result.shape, result.dtype)
+            for result, item in zip(shapes, outs, strict=True)
+        ],
+        in_specs=[vmem if isinstance(item, Near) else hbm for item in ins],
+        out_specs=[vmem if isinstance(item, Near) else hbm for item in outs],
+        scratch_shapes=[*scratch, pltpu.SemaphoreType.DMA((max(marks_needed, 1),))],
         input_output_aliases={} if alias is None else {alias: 0},
         compiler_params=pltpu.CompilerParams(vmem_limit_bytes=VMEM_LIMIT),
         cost_estimate=pl.CostEstimate(flops=int(flops), bytes_accessed=size, transcendentals=0),
-    )(*arrays)
+    )(
+        *(
+            array
+            if isinstance(item, Near)
+            else pltpu.with_memory_space_constraint(array, pltpu.HBM)
+            for array, item in zip(arrays, ins, strict=True)
+        )
+    )
 
 
 def whole(value):
@@ -301,7 +339,7 @@
 def layer0_body(
     came_ref, query_ref, up_query_ref, key_ref, value_ref, bias_ref, hidden_ref, gain_ref,
     down_output_ref, up0_ref, down1_ref, up1_ref, cot_ref,
-    sent_ref, attended_ref, probability_ref, rank_ref, small_ref, kept_ref,
+    sent_ref, attended_ref, probability_ref, rank_ref, small_ref, kept_ref, far_small_ref,
 ):
     projected = total(came_ref)
     squares = came_ref[0, 128:129, :]
@@ -314,8 +352,10 @@
     small_ref[0] = projected
     small_ref[1] = jnp.broadcast_to(scale, (128, 128))
     small_ref[2] = jnp.broadcast_to(squares, (128, 128))
+    far_small_ref[0] = projected
+    far_small_ref[1] = jnp.broadcast_to(scale, (128, 128))
     rank_ref.send()
-    small_ref.send()
+    far_small_ref.send()
     bias = jnp.concatenate([bias_ref[...]] * HEADS_AT_ONCE, axis=0)
     queries = (query_ref[...].astype(F32) + dot(rank_query, read_up(up_query_ref))).astype(BF16)
     for head, shared in head_blocks(query_ref, key_ref):
@@ -381,9 +421,11 @@
     back_query_ref.send()
     rank_output = dot(attended_ref[...], down_output).astype(BF16)
     back_rank = dot_cols(back_query_ref[...], up_query).astype(BF16)
-    sent_ref[:128, :] = rank_output
-    sent_ref[128:256, :] = back_rank
-    sent_ref[256:, :] = kept_ref[...]
+    kept = kept_ref[...]
+    for peer in range(sent_ref.shape[0]):
+        sent_ref[peer, :128, :] = rank_output
+        sent_ref[peer, 128:256, :] = back_rank
+        sent_ref[peer, 256:, :] = kept
 
 
 def backward0_body(
@@ -453,13 +495,16 @@
     write_up(b_query0, dot_rows(rank0_ref[...], back_query0_ref[...]))
 
 
-def last_term_body(came_ref, small_ref, gain_ref, hidden_ref, a_query0):
+def last_term_body(came_ref, small_ref, gain_ref, hidden_ref, a_query0, back_rank_ref):
+    back_rank = total(came_ref).astype(BF16)
+    back_rank_ref[...] = back_rank
+    back_rank_ref.send()
     normed = (hidden_ref[...].astype(F32) * small_ref[1, :, :1] * gain_ref[...]).astype(BF16)
-    write_down(a_query0, dot_rows(total(came_ref).astype(BF16), normed))
-
-
-def cot_body(came_ref, small_ref, gain_ref, down_ref, hidden_ref, gradient_ref, cot_ref):
-    back_rank = total(came_ref).astype(BF16)
+    write_down(a_query0, dot_rows(back_rank, normed))
+
+
+def cot_body(back_rank_ref, small_ref, gain_ref, down_ref, hidden_ref, gradient_ref, cot_ref):
+    back_rank = back_rank_ref[...]
     scale = small_ref[1, :, :1]
     along = row_sum(back_rank.astype(F32) * small_ref[0]) / D
     gained = gain_ref[...] * dot_cols(back_rank, down_ref[...])
@@ -483,7 +528,6 @@
     length = rows * width // 128
     heads = width // HEAD_DIM
     block = whole(shape((128, width), BF16))
-    ranks = whole(shape((3, 128, 128), BF16))
     layer0, layer1 = [(0,)], [(1,)]
     gain0, gain1 = (gains, [(slice(0, 1),)]), (gains, [(slice(1, 2),)])
     peers = [(tuple(range(ways)),)]
@@ -512,7 +556,7 @@
         1e8,
     )
     came = swap(sent, "tensor")
-    sent, attended0, probability, rank_query0, small0, kept = kernel_call(
+    sent, attended0, probability, rank_query0, small0, kept, far_small0 = kernel_call(
         layer0_body,
         [
             whole(came), (q_base, layer0), factor(B_QUERY0), (k_base, layer0), (v_base, layer0),
@@ -520,28 +564,34 @@
             whole(cot),
         ],
         [
-            whole(shape((768, 128), BF16)),
-            block,
-            whole(shape((heads * 128, 128), F32)),
-            whole(shape((128, 128), BF16)),
-            whole(shape((3, 128, 128), F32)),
-            whole(shape((128, 128), BF16)),
+            Near(shape((768, 128), BF16)),
+            Near(block[0]),
+            Near(shape((heads * 128, 128), F32)),
+            Near(shape((128, 128), BF16)),
+            Near(shape((3, 128, 128), F32)),
+            Near(shape((128, 128), BF16)),
+            whole(shape((2, 128, 128), F32)),
         ],
         9e8,
     )
     came = lax.all_gather(sent, "tensor", axis=0, tiled=False)
+
+    def near_factor(*members):
+        return Near(stack, *[(ALL, member) for member in members])
+
+    near_gain0, near_gain1 = Near(gains, (slice(0, 1),)), Near(gains, (slice(1, 2),))
     sent, attended1, back_query1, ranks1, small1 = kernel_call(
         layer1_body,
         [
-            whole(came), whole(small0), (q_base, layer1), factor(B_QUERY1), (k_base, layer1),
-            (v_base, layer1), whole(bias), factor(A_OUT1), whole(kept),
-        ],
-        [
-            (shape((ways, 384, 128), BF16), peers),
-            block,
-            block,
-            ranks,
-            whole(shape((4, 128, 128), F32)),
+            Near(came), Near(small0), Near(q_base, (1,)), near_factor(B_QUERY1),
+            Near(k_base, (1,)), Near(v_base, (1,)), Near(bias), near_factor(A_OUT1), Near(kept),
+        ],
+        [
+            Near(shape((ways, 384, 128), BF16)),
+            Near(block[0]),
+            Near(block[0]),
+            Near(shape((3, 128, 128), BF16)),
+            Near(shape((4, 128, 128), F32)),
         ],
         8e8,
     )
@@ -549,14 +599,14 @@
     sent, back_query0, ranks2, pull = kernel_call(
         backward0_body,
         [
-            whole(came), whole(small1), factor(A_OUT0), (k_base, layer0), (v_base, layer0),
-            whole(probability), factor(B_QUERY0),
+            Near(came), Near(small1), near_factor(A_OUT0), Near(k_base, (0,)), Near(v_base, (0,)),
+            Near(probability), near_factor(B_QUERY0),
         ],
         [
             (shape((ways, 128, 128), BF16), peers),
             block,
-            ranks,
-            whole(shape((128, 128), F32)),
+            Near(shape((3, 128, 128), BF16)),
+            Near(shape((128, 128), F32)),
         ],
         4e8,
     )
@@ -569,9 +619,9 @@
     terms, section_out, gradient = kernel_call(
         terms_body,
         [
-            whole(ranks1), whole(ranks2), whole(small1), whole(pull), gain1, whole(cot),
-            whole(hidden), factor(B_OUT0, A_QUERY1, B_OUT1), whole(attended0), whole(attended1),
-            whole(rank_query0), whole(back_query0), whole(back_query1),
+            Near(ranks1), Near(ranks2), Near(small1), Near(pull), near_gain1, Near(cot),
+            Near(hidden), factor(B_OUT0, A_QUERY1, B_OUT1), Near(attended0), Near(attended1),
+            Near(rank_query0), whole(back_query0), Near(back_query1),
         ],
         [
             (term_shape, [(ALL, member) for member in made_first]),
@@ -580,17 +630,20 @@
         ],
         1e9,
     )
-    (terms,) = kernel_call(
+    terms, back_rank0 = kernel_call(
         last_term_body,
-        [whole(came), whole(small0), gain0, whole(hidden), whole(terms)],
-        [(term_shape, [(ALL, TERM_A_QUERY)])],
+        [Near(came), Near(small0), near_gain0, Near(hidden), whole(terms)],
+        [(term_shape, [(ALL, TERM_A_QUERY)]), whole(shape((128, 128), BF16))],
         1e8,
         alias=4,
     )
     reduced = lax.psum_scatter(terms, "dp", scatter_dimension=0, tiled=False)
     (cot_send,) = kernel_call(
         cot_body,
-        [whole(came), whole(small0), gain0, whole(down0), whole(hidden), whole(gradient)],
+        [
+            whole(back_rank0), whole(far_small0), gain0, whole(down0), whole(hidden),
+            whole(gradient),
+        ],
         [block],
         1e8,
     )

time: 233 us -> 223 us (0.957)
  Pallas kernels: 32.6 us -> 25.3 us
    pallas_call x9, Pallas kernels: 32.6 us -> 25.3 us  [kernel_call(): pl.pallas_call(run, out_shape=[result if isinstance(item, Near) else pltp...]
where the time goes in v4:
time: 223 us; the launch traced here: 222 us
  waiting for transfers between devices  103 us (46%)
  blocking collectives  67.9 us (30%)
  Pallas kernels  25.3 us (11%)
  between operations  14.2 us (6%)
  starting transfers between devices  10 us (4%)
    reduce_scatter x1, waiting for transfers between devices, on_device(): reduced = lax.psum_scatter(terms, 'dp', scatter_dimension=0, tiled=False)  72.5 us
    all_gather x1, blocking collectives, on_device(): down0 = lax.all_gather(a_query[0], 'dp', axis=0, tiled=True)  42.7 us
    pallas_call x9, Pallas kernels, kernel_call(): pl.pallas_call(run, out_shape=[result if isinstance(item, Near) else pltp...  25.3 us
    all_gather x1, waiting for transfers between devices, on_device(): stack = lax.all_gather(shard, 'dp', axis=0, tiled=False)  22.6 us
    all_gather x1, blocking collectives, on_device(): came = lax.all_gather(sent, 'tensor', axis=0, tiled=False)  14.5 us
    all_to_all x1, blocking collectives, swap(): return lax.all_to_all(value, axis, 0, 0, tiled=True)  10.7 us
    all_to_all x2, starting transfers between devices, swap(): return lax.all_to_all(value, axis, 0, 0, tiled=True)  8.17 us
    all_to_all x2, waiting for transfers between devices, swap(): return lax.all_to_all(value, axis, 0, 0, tiled=True)  8.16 us
  transfers between devices with their start and end apart: 6, of which 4 were waited for; matrix products, arithmetic and copies ran while one was open for 0% of the time, Pallas kernels for 5%

profile of v4, /device:TPU:2, one launch (start us, length us, event | category | flops | bytes accessed | tf_op | source)
XLA Modules:
  0.0 222.3 jit_solution(8782521476706547840)
XLA Ops:
  7.2 0.0 all-gather.5.cloned.1.call-start
  7.2 1.7 shard_map.155
  8.9 0.0 all-gather.5.cloned.1.call-update
  8.9 0.0 collective-permute-start
  9.0 1.7 collective-permute-start.1
  10.7 0.8 slice.3
  11.5 42.7 %all-gather = bf16[1,2048,128]{2,1,0:T(8,128)(2,1)} all-gather(bf16[1,128,128]{2,1,0:T(8,128)(2,1)S(1)} %slice.3), channel_id=2, replica_groups=mesh['section'=8,'dp'=16,'tensor'=4] {'dp'}, dimensions={1}, use_global_device_ids=true | all-gather | bytes 557056 | tf_op jit(solution)/shard_map/all_gather | solution.py:551
  54.2 0.0 collective-permute-done.refs_0_.refs_6_.refs_3_.refs_4_
  54.2 0.0 copy-start.1
  54.2 0.8 copy-done.1
  55.0 3.9 %shard_map.154 = (f32[4,136,128]{2,1,0:T(8,128)}, f32[128,128]{1,0:T(8,128)}) custom-call(bf16[128,2048]{1,0:T(8,128)(2,1)} %copy-done.1, f32[2,2048]{1,0:T(2,128)} %refs_2_.7, s32[1,128]{1,0:T(1,128)} %bitcast.16, bf16[2048,128]{1,0:T(8,128)(2,1)} %bitcast.13), custom_call_target="tpu_custom_call" | custom-call | flops 100000000 | bytes 1409536 | tf_op jit(solution)/shard_map/pallas_call | solution.py:168
  58.9 4.8 %all-to-all-start = ((f32[4,136,128]{2,1,0:T(8,128)}), f32[4,136,128]{2,1,0:T(8,128)S(1)}, u32[]{:S(2)}, u32[]{:S(2)}) async-start(f32[4,136,128]{2,1,0:T(8,128)} %get-tuple-element.33), calls=%async_computation | async-start | bytes 557056 | tf_op jit(solution)/shard_map/all_to_all | solution.py:519
  63.8 0.0 collective-permute-done.1.refs_9_.refs_5_
  63.8 0.0 copy-start.4
  63.8 6.8 %all-to-all-done.refs_0_ = f32[4,136,128]{2,1,0:T(8,128)S(1)} async-done(((f32[4,136,128]{2,1,0:T(8,128)}), f32[4,136,128]{2,1,0:T(8,128)S(1)}, u32[]{:S(2)}, u32[]{:S(2)}) %all-to-all-start) | async-done | bytes 278560 | tf_op jit(solution)/shard_map/all_to_all | solution.py:519
  70.5 0.0 copy-start.10
  70.5 22.6 %all-gather.5.cloned.1.call-done = bf16[112,128,128]{2,1,0:T(8,128)(2,1)} async-done(((bf16[7,128,128]{2,1,0:T(8,128)(2,1)}), bf16[112,128,128]{2,1,0:T(8,128)(2,1)}) %all-gather.5.cloned.1.call-update) | async-done | bytes 3670032 | tf_op jit(solution)/shard_map/all_gather | solution.py:544
  93.2 0.0 copy-done.4
  93.2 0.0 copy-done.10
  93.2 0.0 copy-start
  93.2 0.0 copy-start.3
  93.2 0.0 copy-start.6
  93.2 0.0 copy-start.7
  93.2 0.0 copy-start.9
  93.2 4.9 %shard_map.156 = (bf16[768,128]{1,0:T(8,128)(2,1)S(1)}, bf16[128,2048]{1,0:T(8,128)(2,1)S(1)}, f32[2048,128]{1,0:T(8,128)S(1)}, bf16[128,128]{1,0:T(8,128)(2,1)S...) custom-call(f32[4,136,128]{2,1,0:T(8,128)} %copy-done.10, ...), custom_call_target="tpu_custom_call" | custom-call | flops 900000000 | bytes 12222464 | tf_op jit(solution)/shard_map/pallas_call | solution.py:168
  98.1 14.5 %all-gather.2 = bf16[3072,128]{1,0:T(8,128)(2,1)S(1)} all-gather(bf16[768,128]{1,0:T(8,128)(2,1)S(1)} %get-tuple-element.35), channel_id=4, replica_groups=mesh['section'=8,'dp'=16,'tensor'=4] {'tensor'}, dimensions={0}, use_global_device_ids=true | all-gather | bytes 983040 | tf_op jit(solution)/shard_map/all_gather | solution.py:577
  112.6 0.0 copy-done
  112.6 0.0 copy-done.3
  112.6 0.0 copy-done.6
  112.6 0.0 copy-done.7
  112.6 0.0 copy-done.9
  112.7 2.3 %shard_map.157 = (bf16[4,384,128]{2,1,0:T(8,128)(2,1)S(1)}, bf16[128,2048]{1,0:T(8,128)(2,1)S(1)}, bf16[128,2048]{1,0:T(8,128)(2,1)S(1)}, bf16[3,128,128]{2,1,0:T(8,128)(2,1)S(1)}, f32[4,128,128]{2,1,0:T(8,128)S(1)}) custom-call(bf16[4,768,128]{2,1,0:T(8,128)(2,1)S(1)} %bitcast.12, f32[3,128,128]{2,1,0:T(8,128)S(1)} %get-tuple-element.36.refs_1_, ...), custom_call_target="tpu_custom_call" | custom-call | flops 800000000 | bytes 11534336 | tf_op jit(solution)/shard_map/pallas_call | solution.py:168
  114.9 10.7 %all_to_all.15.refs_0_ = bf16[4,384,128]{2,1,0:T(8,128)(2,1)S(1)} all-to-all(bf16[4,384,128]{2,1,0:T(8,128)(2,1)S(1)} %get-tuple-element.39), channel_id=1, replica_groups=mesh['section'=8,'dp'=16,'tensor'=4] {'tensor'}, dimensions={0} | all-to-all | bytes 786432 | tf_op jit(solution)/shard_map/all_to_all | solution.py:519
  125.6 0.0 copy-start.2
  125.6 0.0 copy-start.5
  125.6 2.1 shard_map.158
  127.7 3.3 %all-to-all-start.2 = ((bf16[4,128,128]{2,1,0:T(8,128)(2,1)}), bf16[4,128,128]{2,1,0:T(8,128)(2,1)S(1)}, u32[]{:S(2)}, u32[]{:S(2)}) async-start(bf16[4,128,128]{2,1,0:T(8,128)(2,1)} %get-tuple-element.50), calls=%async_computation.2 | async-start | bytes 262144 | tf_op jit(solution)/shard_map/all_to_all | solution.py:519
  131.0 0.0 reduce-scatter.2.cloned.1.call-start
  131.1 0.0 copy-done.2
  131.1 0.0 copy-done.5
  131.1 0.0 copy-done.8
  131.1 4.5 %shard_map.159 = (bf16[16,8,128,128]{3,2,1,0:T(8,128)(2,1)}, bf16[128,2048]{1,0:T(8,128)(2,1)}, f32[128,2048]{1,0:T(8,128)}) custom-call(bf16[3,128,128]{2,1,0:T(8,128)(2,1)S(1)} %get-tuple-element.38.refs_0_, bf16[3,128,128]{2,1,0:T(8,128)(2,1)S(1)} %get-tuple-element.42.refs_1_, f32[4,128,128]{2,1,0:T(8,128)S(1)} %get-tuple-element.40.refs_1_.refs_2_, ...), custom_call_target="tpu_custom_call" | custom-call | flops 1000000000 | bytes 13156352 | tf_op jit(solution)/shard_map/pallas_call | solution.py:168
  135.6 1.4 all-to-all-done.2.refs_0_
  137.0 1.2 shard_map.160
  138.2 0.0 reduce-scatter.2.cloned.1.call-update
  138.2 2.8 %shard_map.161 = bf16[128,2048]{1,0:T(8,128)(2,1)} custom-call(bf16[128,128]{1,0:T(8,128)(2,1)} %get-tuple-element.52.refs_0_, f32[2,128,128]{2,1,0:T(8,128)} %get-tuple-element.53.refs_1_, f32[2,2048]{1,0:T(2,128)} %refs_2_.7, bf16[2048,128]{1,0:T(8,128)(2,1)} %bitcast.14, bf16[128,2048]{1,0:T(8,128)(2,1)} %copy-done.1, f32[128,2048]{1,0:T(8,128)} %get-tuple-element.54.refs_5_), custom_call_target="tpu_custom_call" | custom-call | flops 100000000 | bytes 2801664 | tf_op jit(solution)/shard_map/pallas_call | solution.py:168
  141.1 72.5 %reduce-scatter.2.cloned.1.call-done = bf16[1,8,128,128]{3,2,1,0:T(8,128)(2,1)} async-done(((bf16[16,8,128,128]{3,2,1,0:T(8,128)(2,1)}), bf16[1,8,128,128]{3,2,1,0:T(8,128)(2,1)}) %reduce-scatter.2.cloned.1.call-update) | async-done | bytes 262160 | tf_op jit(solution)/shard_map/reduce_scatter | solution.py:640
  213.6 1.9 shard_map.162
  (1 shorter events, 0.0 us)
Async XLA Ops:
  7.2 86.0 %all-gather.5.cloned.1.call-start = ((), (), s32[]{:S(2)}) async-start(), calls=%async_computation.5 | async-start | bytes 3899392 | tf_op jit(solution)/shard_map/all_gather | solution.py:544
  8.9 45.2 %collective-permute-start = (bf16[128,2048]{1,0:T(8,128)(2,1)}, bf16[128,2048]{1,0:T(8,128)(2,1)S(1)}, u32[]{:S(2)}, u32[]{:S(2)}) collective-permute-start(bf16[128,2048]{1,0:T(8,128)(2,1)} %param.11), channel_id=1, source_target_pairs={{0,64},{64,128},{128,192},{192,256},{256,320},{320,384},{384,448},... | collective-permute-start | bytes 1572872 | tf_op jit(solution)/shard_map/ppermute | solution.py:23
  9.0 54.8 %collective-permute-start.1 = (bf16[128,2048]{1,0:T(8,128)(2,1)}, bf16[128,2048]{1,0:T(8,128)(2,1)S(1)}, u32[]{:S(2)}, u32[]{:S(2)}) collective-permute-start(bf16[128,2048]{1,0:T(8,128)(2,1)} %param.12), channel_id=1, source_target_pairs={{0,448},{64,0},{128,64},{192,128},{256,192},{320,256},{384,320},{4... | collective-permute-start | bytes 1572872 | tf_op jit(solution)/shard_map/ppermute | solution.py:23
  54.2 0.8 copy-start.1
  58.9 11.6 %all-to-all-start = ((f32[4,136,128]{2,1,0:T(8,128)}), f32[4,136,128]{2,1,0:T(8,128)S(1)}, u32[]{:S(2)}, u32[]{:S(2)}) async-start(f32[4,136,128]{2,1,0:T(8,128)} %get-tuple-element.33), calls=%async_computation | async-start | bytes 557056 | tf_op jit(solution)/shard_map/all_to_all | solution.py:519
  63.8 29.4 %copy-start.4 = (bf16[128,2048]{1,0:T(8,128)(2,1)}, bf16[128,2048]{1,0:T(8,128)(2,1)S(1)}, u32[]{:S(2)}) copy-start(bf16[128,2048]{1,0:T(8,128)(2,1)S(1)} %collective-permute-done.1.refs_9_.refs_5_) | copy-start | bytes 1572868
  70.5 22.7 %copy-start.10 = (f32[4,136,128]{2,1,0:T(8,128)}, f32[4,136,128]{2,1,0:T(8,128)S(1)}, u32[]{:S(2)}) copy-start(f32[4,136,128]{2,1,0:T(8,128)S(1)} %all-to-all-done.refs_0_) | copy-start | bytes 835588
  93.2 19.4 %copy-start = (bf16[112,128,128]{2,1,0:T(8,128)(2,1)S(1)}, bf16[112,128,128]{2,1,0:T(8,128)(2,1)}, u32[]{:S(2)}) copy-start(bf16[112,128,128]{2,1,0:T(8,128)(2,1)} %all-gather.5.cloned.1.call-done) | copy-start | bytes 11010052
  93.2 19.4 %copy-start.3 = (bf16[2,128,2048]{2,1,0:T(8,128)(2,1)S(1)}, bf16[2,128,2048]{2,1,0:T(8,128)(2,1)}, u32[]{:S(2)}) copy-start(bf16[2,128,2048]{2,1,0:T(8,128)(2,1)} %refs_2_.5) | copy-start | bytes 3145732
  93.2 19.4 %copy-start.6 = (bf16[2,128,256]{2,1,0:T(8,128)(2,1)S(1)}, bf16[2,128,256]{2,1,0:T(8,128)(2,1)}, u32[]{:S(2)}) copy-start(bf16[2,128,256]{2,1,0:T(8,128)(2,1)} %refs_3_.5) | copy-start | bytes 393220
  93.2 19.4 %copy-start.7 = (bf16[2,128,256]{2,1,0:T(8,128)(2,1)S(1)}, bf16[2,128,256]{2,1,0:T(8,128)(2,1)}, u32[]{:S(2)}) copy-start(bf16[2,128,256]{2,1,0:T(8,128)(2,1)} %refs_4_.8) | copy-start | bytes 393220
  93.2 19.4 %copy-start.9 = (f32[128,128]{1,0:T(8,128)S(1)}, f32[128,128]{1,0:T(8,128)}, u32[]{:S(2)}) copy-start(f32[128,128]{1,0:T(8,128)} %get-tuple-element.34.refs_5_.refs_6_) | copy-start | bytes 196612
  125.6 5.5 %copy-start.2 = (bf16[128,2048]{1,0:T(8,128)(2,1)S(1)}, bf16[128,2048]{1,0:T(8,128)(2,1)}, u32[]{:S(2)}) copy-start(bf16[128,2048]{1,0:T(8,128)(2,1)} %copy-done.1) | copy-start | bytes 1572868
  125.6 5.5 %copy-start.5 = (bf16[128,2048]{1,0:T(8,128)(2,1)S(1)}, bf16[128,2048]{1,0:T(8,128)(2,1)}, u32[]{:S(2)}) copy-start(bf16[128,2048]{1,0:T(8,128)(2,1)} %copy-done.4) | copy-start | bytes 1572868
  125.6 5.5 %copy-start.8 = (f32[2,2048]{1,0:T(2,128)S(1)}, f32[2,2048]{1,0:T(2,128)}, u32[]{:S(2)}) copy-start(f32[2,2048]{1,0:T(2,128)} %refs_2_.7) | copy-start | bytes 49156
  127.7 9.3 %all-to-all-start.2 = ((bf16[4,128,128]{2,1,0:T(8,128)(2,1)}), bf16[4,128,128]{2,1,0:T(8,128)(2,1)S(1)}, u32[]{:S(2)}, u32[]{:S(2)}) async-start(bf16[4,128,128]{2,1,0:T(8,128)(2,1)} %get-tuple-element.50), calls=%async_computation.2 | async-start | bytes 262144 | tf_op jit(solution)/shard_map/all_to_all | solution.py:519
  131.0 82.6 %reduce-scatter.2.cloned.1.call-start = ((), (), s32[]{:S(2)}) async-start(), calls=%async_computation.4 | async-start | bytes 4456448 | tf_op jit(solution)/shard_map/reduce_scatter | solution.py:640
Sparse Core Ops, SparseCore 0:
  10.1 83.0 all-gather.4
  138.4 75.1 reduce-scatter.1

commit v5 on v4

--- a/solution.py
+++ b/solution.py
@@ -13,7 +13,11 @@
 BF16 = jnp.bfloat16
 VMEM_LIMIT = 20 << 20
 ALL = slice(None)
-A_OUT0, B_OUT0, A_QUERY1, B_OUT1, B_QUERY1, A_OUT1, B_QUERY0 = range(7)
+(A_QUERY0, A_QUERY1, A_OUT0, A_OUT1, B_QUERY0, B_QUERY1, B_OUT0, B_OUT1) = range(8)
+PROJECTED0, PROJECTED1, CROSS, BACK_OUTPUT1, HIDDEN_UP, GRAM, BACK_OUTPUT0, SQUARES = range(
+    0, 1024, 128
+)
+SCALE_UP = 65536.0
 TERM_A_QUERY, TERM_B_QUERY, TERM_A_OUT, TERM_B_OUT = 0, 2, 4, 6
 
 
@@ -139,7 +143,7 @@
                 used, mark = used + 1, mark + 1
         for ref, item in zip(out_refs, outs, strict=True):
             if isinstance(item, Near):
-                given.append(Staying(ref))
+                given += [Staying(ref.at[at]) for at in item.slices] or [Staying(ref)]
                 continue
             for at in item[1]:
                 copies = []
@@ -232,11 +236,18 @@
         ).astype(BF16)
 
 
-def pack_body(*refs):
-    sources, ups, targets = refs[:3], refs[3:7], refs[7:14]
-    for ref, place in zip(sources, (A_OUT0, A_QUERY1, A_OUT1), strict=True):
-        targets[place][...] = ref[...]
-    for ref, place in zip(ups, (B_OUT0, B_OUT1, B_QUERY1, B_QUERY0), strict=True):
+def pack_body(parent_ref, *refs):
+    downs, ups, targets, bias_ref = refs[:4], refs[4:8], refs[8:16], refs[16]
+    lane = lax.broadcasted_iota(jnp.int32, (128, 128), 1)
+    line = lax.broadcasted_iota(jnp.int32, (128, 128), 0)
+    linked = (lane == line) | (jnp.broadcast_to(parent_ref[...], (128, 128)) == line)
+    reached = jnp.where(linked, 1.0, 0.0).astype(BF16)
+    for _ in range(7):
+        reached = jnp.minimum(dot(reached, reached), 1.0).astype(BF16)
+    bias_ref[...] = jnp.where(jnp.transpose(reached.astype(F32)) > 0.5, 0.0, -1e30)
+    for ref, target in zip(downs, targets[:4], strict=True):
+        target[...] = ref[...]
+    for ref, target in zip(ups, targets[4:], strict=True):
         rows, width = ref.shape
         value = ref[...].astype(F32)
         for pair in range(width // 256):
@@ -244,7 +255,7 @@
                 value[:, (2 * pair + half) * 128 : (2 * pair + half + 1) * 128]
                 for half in range(2)
             ]
-            targets[place][pair * 2 * rows : (pair + 1) * 2 * rows, :] = jnp.concatenate(
+            target[pair * 2 * rows : (pair + 1) * 2 * rows, :] = jnp.concatenate(
                 halves, axis=0
             ).astype(BF16)
 
@@ -265,25 +276,37 @@
                 ]
 
 
-def first_body(hidden_ref, gain_ref, parent_ref, down_ref, sent_ref, bias_ref):
-    lane = lax.broadcasted_iota(jnp.int32, (128, 128), 1)
-    line = lax.broadcasted_iota(jnp.int32, (128, 128), 0)
-    linked = (lane == line) | (jnp.broadcast_to(parent_ref[...], (128, 128)) == line)
-    reached = jnp.where(linked, 1.0, 0.0).astype(BF16)
-    for _ in range(7):
-        reached = jnp.minimum(dot(reached, reached), 1.0).astype(BF16)
-    bias_ref[...] = jnp.where(jnp.transpose(reached.astype(F32)) > 0.5, 0.0, -1e30)
-    hidden = hidden_ref[...].astype(F32)
-    projected = dot((hidden * gain_ref[...]).astype(BF16), down_ref[...])
+def first_body(
+    hidden_ref, cot_ref, gain0_ref, gain1_ref, down0_ref, down1_ref, up0_ref, up1_ref, sent_ref
+):
+    def send(start, value):
+        value = value.astype(BF16)
+        for peer in range(sent_ref.shape[0]):
+            sent_ref[peer, start : start + value.shape[0], :] = value
+
+    hidden, gain1 = hidden_ref[...], gain1_ref[...]
+    wide = hidden.astype(F32)
+    down1, up0, cot = read_down(down1_ref), read_up(up0_ref), cot_ref[...]
+    send(PROJECTED0, dot((wide * gain0_ref[...]).astype(BF16), read_down(down0_ref)))
+    send(PROJECTED1, dot((wide * gain1).astype(BF16), down1))
+    send(CROSS, dot((up0.astype(F32) * gain1).astype(BF16), down1))
+    send(BACK_OUTPUT1, dot_cols(cot, read_up(up1_ref)))
+    send(HIDDEN_UP, dot_cols(hidden, up0))
+    send(GRAM, dot_cols(up0, up0))
+    send(BACK_OUTPUT0, dot_cols(cot, up0))
     squares = lax.dot_general(
-        jnp.ones((8, hidden.shape[1]), F32),
-        hidden * hidden,
+        jnp.ones((16, hidden.shape[1]), F32),
+        wide * wide,
         (((1,), (1,)), ((), ())),
         preferred_element_type=F32,
         precision=lax.Precision.HIGHEST,
     )
-    sent_ref[:128, :] = projected
-    sent_ref[128:, :] = squares
+    high = squares.astype(BF16)
+    rest = squares - high.astype(F32)
+    middle = rest.astype(BF16)
+    send(SQUARES, high)
+    send(SQUARES + 16, middle)
+    send(SQUARES + 32, rest - middle.astype(F32))
 
 
 def to_column(row):
@@ -292,10 +315,10 @@
     return row_sum(jnp.where(lane == line, jnp.broadcast_to(row, (128, 128)), 0.0))
 
 
-def total(ref, start=0):
-    value = ref[0, start : start + 128, :].astype(F32)
+def total(ref, start=0, rows=128):
+    value = ref[0, start : start + rows, :].astype(F32)
     for peer in range(1, ref.shape[0]):
-        value = value + ref[peer, start : start + 128, :].astype(F32)
+        value = value + ref[peer, start : start + rows, :].astype(F32)
     return value
 
 
@@ -337,15 +360,17 @@
 
 
 def layer0_body(
-    came_ref, query_ref, up_query_ref, key_ref, value_ref, bias_ref, hidden_ref, gain_ref,
-    down_output_ref, up0_ref, down1_ref, up1_ref, cot_ref,
-    sent_ref, attended_ref, probability_ref, rank_ref, small_ref, kept_ref, far_small_ref,
+    came_ref, query_ref, up_query_ref, key_ref, value_ref, bias_ref, down_output_ref,
+    sent_ref, attended_ref, probability_ref, rank_ref, small_ref, far_small_ref,
 ):
-    projected = total(came_ref)
-    squares = came_ref[0, 128:129, :]
-    for peer in range(1, came_ref.shape[0]):
-        squares = squares + came_ref[peer, 128:129, :]
-    squares = to_column(squares)
+    projected = total(came_ref, PROJECTED0)
+    squares = to_column(
+        (
+            total(came_ref, SQUARES, 16)
+            + total(came_ref, SQUARES + 16, 16)
+            + total(came_ref, SQUARES + 32, 16)
+        )[:1]
+    )
     scale = lax.rsqrt(squares / D + EPSILON)
     rank_query = (scale * projected).astype(BF16)
     rank_ref[...] = rank_query
@@ -366,28 +391,21 @@
         )
     probability_ref.send()
     attended_ref.send()
-    hidden, gain = hidden_ref[...], gain_ref[...]
-    up0, down1, cot = read_up(up0_ref), read_down(down1_ref), cot_ref[...]
-    sent_ref[512:640, :] = dot_cols(hidden, up0).astype(BF16)
-    sent_ref[640:, :] = dot_cols(up0, up0).astype(BF16)
-    sent_ref[128:256, :] = dot((hidden.astype(F32) * gain).astype(BF16), down1).astype(BF16)
-    sent_ref[256:384, :] = dot((up0.astype(F32) * gain).astype(BF16), down1).astype(BF16)
-    sent_ref[384:512, :] = dot_cols(cot, read_up(up1_ref)).astype(BF16)
-    sent_ref[:128, :] = dot(attended_ref[...], read_down(down_output_ref)).astype(BF16)
-    sent_ref.send()
-    kept_ref[...] = dot_cols(cot, up0).astype(BF16)
+    rank_output = dot(attended_ref[...], read_down(down_output_ref)).astype(BF16)
+    for peer in range(sent_ref.shape[0]):
+        sent_ref[peer] = rank_output
 
 
 def layer1_body(
-    came_ref, small0_ref, query_ref, up_ref, key_ref, value_ref, bias_ref, down_ref, kept_ref,
-    sent_ref, attended_ref, back_query_ref, ranks_ref, small_ref,
+    came_ref, first_ref, small0_ref, query_ref, up_ref, key_ref, value_ref, bias_ref, down_ref,
+    sent_ref, attended_ref, back_query_ref, ranks_ref, small_ref, scale_ref,
 ):
     rank_output0 = total(came_ref).astype(BF16)
-    cross = total(came_ref, 256)
-    projected = total(came_ref, 128) + dot(rank_output0, cross.astype(BF16))
-    back_rank_output = total(came_ref, 384).astype(BF16)
-    hidden_up = total(came_ref, 512)
-    gram = total(came_ref, 640)
+    cross = total(first_ref, CROSS)
+    projected = total(first_ref, PROJECTED1) + dot(rank_output0, cross.astype(BF16))
+    back_rank_output = total(first_ref, BACK_OUTPUT1).astype(BF16)
+    hidden_up = total(first_ref, HIDDEN_UP)
+    gram = total(first_ref, GRAM)
     gram_high = gram.astype(BF16)
     gram_low = (gram - gram_high.astype(F32)).astype(BF16)
     output_gram = dot(rank_output0, gram_high) + dot(rank_output0, gram_low)
@@ -404,7 +422,8 @@
     small_ref[1] = jnp.broadcast_to(scale, (128, 128))
     small_ref[2] = cross
     small_ref[3] = hidden_up + output_gram
-    small_ref.send()
+    scale_ref[...] = jnp.broadcast_to(scale, (128, 128))
+    scale_ref.send()
     bias = jnp.concatenate([bias_ref[...]] * HEADS_AT_ONCE, axis=0)
     up_query = read_up(up_ref)
     queries = (query_ref[...].astype(F32) + dot(rank_query, up_query)).astype(BF16)
@@ -421,15 +440,13 @@
     back_query_ref.send()
     rank_output = dot(attended_ref[...], down_output).astype(BF16)
     back_rank = dot_cols(back_query_ref[...], up_query).astype(BF16)
-    kept = kept_ref[...]
     for peer in range(sent_ref.shape[0]):
         sent_ref[peer, :128, :] = rank_output
-        sent_ref[peer, 128:256, :] = back_rank
-        sent_ref[peer, 256:, :] = kept
+        sent_ref[peer, 128:, :] = back_rank
 
 
 def backward0_body(
-    came_ref, small_ref, down_ref, key_ref, value_ref, probability_ref, up_ref,
+    came_ref, first_ref, small_ref, down_ref, key_ref, value_ref, probability_ref, up_ref,
     sent_ref, back_query_ref, ranks_ref, pull_ref,
 ):
     back_rank1 = total(came_ref, 128).astype(BF16)
@@ -437,7 +454,7 @@
     along = row_sum(back_rank1.astype(F32) * small_ref[0]) / D
     pull = scale * scale * scale * along
     back_output = (
-        total(came_ref, 256)
+        total(first_ref, BACK_OUTPUT0)
         + scale * dot_cols(back_rank1, small_ref[2].astype(BF16))
         - pull * small_ref[3]
     ).astype(BF16)
@@ -465,17 +482,20 @@
 
 
 def terms_body(
-    ranks1_ref, ranks2_ref, small_ref, pull_ref, gain_ref, cot_ref, hidden_ref, up0_ref, down1_ref,
-    up1_ref, attended0_ref, attended1_ref, rank0_ref, back_query0_ref, back_query1_ref,
-    a_query1, b_query0, b_query1, a_out0, a_out1, b_out0, b_out1, out_ref, gradient_ref,
+    ranks1_ref, ranks2_ref, scale_ref, pull_ref, gain_ref, cot_ref, hidden_ref, up0_ref, down1_ref,
+    up1_ref, attended0_ref, attended1_ref, rank0_ref, back_query0_ref, back_query1_ref, small0_ref,
+    gain0_ref, a_query1, b_query0, b_query1, a_out0, a_out1, b_out0, b_out1, out_ref, gradient_ref,
+    normed0_ref,
 ):
     rank_output0, rank_query1, back_output1 = ranks1_ref[0], ranks1_ref[1], ranks1_ref[2]
     rank_output1, back_rank1, back_output0 = ranks2_ref[0], ranks2_ref[1], ranks2_ref[2]
     cot = cot_ref[...]
     write_up(b_out1, dot_rows(rank_output1, cot))
     b_out1.send()
-    gain, scale, pull = gain_ref[...], small_ref[1, :, :1], pull_ref[:, :1]
-    hidden = hidden_ref[...].astype(F32) + dot(rank_output0, read_up(up0_ref))
+    gain, scale, pull = gain_ref[...], scale_ref[:, :1], pull_ref[:, :1]
+    hidden = hidden_ref[...].astype(F32)
+    normed0_ref[...] = (hidden * small0_ref[1, :, :1] * gain0_ref[...]).astype(BF16)
+    hidden = hidden + dot(rank_output0, read_up(up0_ref))
     write_down(a_query1, dot_rows(back_rank1, (hidden * scale * gain).astype(BF16)))
     a_query1.send()
     gained = gain * dot_cols(back_rank1, read_down(down1_ref))
@@ -495,19 +515,18 @@
     write_up(b_query0, dot_rows(rank0_ref[...], back_query0_ref[...]))
 
 
-def last_term_body(came_ref, small_ref, gain_ref, hidden_ref, a_query0, back_rank_ref):
+def last_term_body(came_ref, normed_ref, a_query0, back_rank_ref):
     back_rank = total(came_ref).astype(BF16)
     back_rank_ref[...] = back_rank
     back_rank_ref.send()
-    normed = (hidden_ref[...].astype(F32) * small_ref[1, :, :1] * gain_ref[...]).astype(BF16)
-    write_down(a_query0, dot_rows(back_rank, normed))
+    write_down(a_query0, dot_rows(back_rank, normed_ref[...]))
 
 
 def cot_body(back_rank_ref, small_ref, gain_ref, down_ref, hidden_ref, gradient_ref, cot_ref):
     back_rank = back_rank_ref[...]
     scale = small_ref[1, :, :1]
     along = row_sum(back_rank.astype(F32) * small_ref[0]) / D
-    gained = gain_ref[...] * dot_cols(back_rank, down_ref[...])
+    gained = gain_ref[...] * dot_cols(back_rank, read_down(down_ref))
     cot_ref[...] = (
         gradient_ref[...]
         + scale * gained
@@ -532,66 +551,71 @@
     gain0, gain1 = (gains, [(slice(0, 1),)]), (gains, [(slice(1, 2),)])
     peers = [(tuple(range(ways)),)]
 
-    (shard,) = kernel_call(
+    shard, bias = kernel_call(
         pack_body,
         [
-            (a_out, layer0), (a_query, layer1), (a_out, layer1),
-            (b_out, layer0), (b_out, layer1), (b_query, layer1), (b_query, layer0),
-        ],
-        [(shape((7, length, 128), BF16), [(member,) for member in range(7)])],
+            whole(parents.reshape(1, 128)),
+            *[(array, [(0,), (1,)]) for array in (a_query, a_out, b_query, b_out)],
+        ],
+        [
+            Near(shape((8, length, 128), BF16), *[(member,) for member in range(8)]),
+            whole(shape((128, 128), F32)),
+        ],
         0,
     )
+    shard = (shard.astype(F32) * SCALE_UP).astype(jnp.float16)
     stack = lax.all_gather(shard, "dp", axis=0, tiled=False)
+    stack = (stack.astype(F32) * (1.0 / SCALE_UP)).astype(BF16)
 
     def factor(*members):
         return (stack, [(ALL, member) for member in members])
 
+    def near_factor(*members):
+        return Near(stack, *[(ALL, member) for member in members])
+
     hidden = from_behind(arrived, "section", 1)
     cot = from_behind(cot_later, "section", -1)
-    down0 = lax.all_gather(a_query[0], "dp", axis=0, tiled=True)
-    sent, bias = kernel_call(
+    near_gain0, near_gain1 = Near(gains, (slice(0, 1),)), Near(gains, (slice(1, 2),))
+    (sent,) = kernel_call(
         first_body,
-        [whole(hidden), gain0, whole(parents.reshape(1, 128)), whole(down0)],
-        [(shape((ways, 136, 128), F32), peers), whole(shape((128, 128), F32))],
-        1e8,
+        [
+            Near(hidden), Near(cot), near_gain0, near_gain1,
+            near_factor(A_QUERY0, A_QUERY1, B_OUT0, B_OUT1),
+        ],
+        [Near(shape((ways, SQUARES + 48, 128), BF16))],
+        6e8,
+    )
+    first = swap(sent, "tensor")
+    sent, attended0, probability, rank_query0, small0, far_small0 = kernel_call(
+        layer0_body,
+        [
+            Near(first), Near(q_base, (0,)), near_factor(B_QUERY0), Near(k_base, (0,)),
+            Near(v_base, (0,)), Near(bias), near_factor(A_OUT0),
+        ],
+        [
+            Near(shape((ways, 128, 128), BF16)),
+            block,
+            Near(shape((heads * 128, 128), F32)),
+            whole(shape((128, 128), BF16)),
+            Near(shape((3, 128, 128), F32)),
+            whole(shape((2, 128, 128), F32)),
+        ],
+        9e8,
     )
     came = swap(sent, "tensor")
-    sent, attended0, probability, rank_query0, small0, kept, far_small0 = kernel_call(
-        layer0_body,
-        [
-            whole(came), (q_base, layer0), factor(B_QUERY0), (k_base, layer0), (v_base, layer0),
-            whole(bias), whole(hidden), gain1, factor(A_OUT0, B_OUT0, A_QUERY1, B_OUT1),
-            whole(cot),
-        ],
-        [
-            Near(shape((768, 128), BF16)),
-            Near(block[0]),
-            Near(shape((heads * 128, 128), F32)),
-            Near(shape((128, 128), BF16)),
-            Near(shape((3, 128, 128), F32)),
-            Near(shape((128, 128), BF16)),
-            whole(shape((2, 128, 128), F32)),
-        ],
-        9e8,
-    )
-    came = lax.all_gather(sent, "tensor", axis=0, tiled=False)
-
-    def near_factor(*members):
-        return Near(stack, *[(ALL, member) for member in members])
-
-    near_gain0, near_gain1 = Near(gains, (slice(0, 1),)), Near(gains, (slice(1, 2),))
-    sent, attended1, back_query1, ranks1, small1 = kernel_call(
+    sent, attended1, back_query1, ranks1, small1, scale1 = kernel_call(
         layer1_body,
         [
-            Near(came), Near(small0), Near(q_base, (1,)), near_factor(B_QUERY1),
-            Near(k_base, (1,)), Near(v_base, (1,)), Near(bias), near_factor(A_OUT1), Near(kept),
-        ],
-        [
-            Near(shape((ways, 384, 128), BF16)),
-            Near(block[0]),
-            Near(block[0]),
-            Near(shape((3, 128, 128), BF16)),
+            Near(came), Near(first), Near(small0), Near(q_base, (1,)), near_factor(B_QUERY1),
+            Near(k_base, (1,)), Near(v_base, (1,)), Near(bias), near_factor(A_OUT1),
+        ],
+        [
+            Near(shape((ways, 256, 128), BF16)),
+            block,
+            block,
+            whole(shape((3, 128, 128), BF16)),
             Near(shape((4, 128, 128), F32)),
+            whole(shape((128, 128), F32)),
         ],
         8e8,
     )
@@ -599,14 +623,14 @@
     sent, back_query0, ranks2, pull = kernel_call(
         backward0_body,
         [
-            Near(came), Near(small1), near_factor(A_OUT0), Near(k_base, (0,)), Near(v_base, (0,)),
-            Near(probability), near_factor(B_QUERY0),
+            Near(came), Near(first), Near(small1), near_factor(A_OUT0), Near(k_base, (0,)),
+            Near(v_base, (0,)), Near(probability), near_factor(B_QUERY0),
         ],
         [
             (shape((ways, 128, 128), BF16), peers),
             block,
-            Near(shape((3, 128, 128), BF16)),
-            Near(shape((128, 128), F32)),
+            whole(shape((3, 128, 128), BF16)),
+            whole(shape((128, 128), F32)),
         ],
         4e8,
     )
@@ -616,32 +640,33 @@
         TERM_A_QUERY + 1, TERM_B_QUERY, TERM_B_QUERY + 1, TERM_A_OUT, TERM_A_OUT + 1,
         TERM_B_OUT, TERM_B_OUT + 1,
     )
-    terms, section_out, gradient = kernel_call(
+    terms, section_out, gradient, normed0 = kernel_call(
         terms_body,
         [
-            Near(ranks1), Near(ranks2), Near(small1), Near(pull), near_gain1, Near(cot),
-            Near(hidden), factor(B_OUT0, A_QUERY1, B_OUT1), Near(attended0), Near(attended1),
-            Near(rank_query0), whole(back_query0), Near(back_query1),
+            whole(ranks1), whole(ranks2), whole(scale1), whole(pull), gain1, whole(cot),
+            whole(hidden), factor(B_OUT0, A_QUERY1, B_OUT1), whole(attended0), whole(attended1),
+            whole(rank_query0), whole(back_query0), whole(back_query1), whole(far_small0), gain0,
         ],
         [
             (term_shape, [(ALL, member) for member in made_first]),
             block,
             whole(shape((128, width), F32)),
+            Near(block[0]),
         ],
         1e9,
     )
     terms, back_rank0 = kernel_call(
         last_term_body,
-        [Near(came), Near(small0), near_gain0, Near(hidden), whole(terms)],
+        [Near(came), Near(normed0), whole(terms)],
         [(term_shape, [(ALL, TERM_A_QUERY)]), whole(shape((128, 128), BF16))],
         1e8,
-        alias=4,
+        alias=2,
     )
     reduced = lax.psum_scatter(terms, "dp", scatter_dimension=0, tiled=False)
     (cot_send,) = kernel_call(
         cot_body,
         [
-            whole(back_rank0), whole(far_small0), gain0, whole(down0), whole(hidden),
+            whole(back_rank0), whole(far_small0), gain0, factor(A_QUERY0), whole(hidden),
             whole(gradient),
         ],
         [block],

time: 223 us -> 220 us (0.987)
  the two profiles are of different devices: /device:TPU:2 before, /device:TPU:12 now
where the time goes in v5:
time: 220 us
  blocking collectives  98.4 us (45%)
  waiting for transfers between devices  75.1 us (34%)
  Pallas kernels  24 us (11%)
  between operations  14.2 us (6%)
  starting transfers between devices  6.51 us (3%)
    reduce_scatter x1, waiting for transfers between devices, on_device(): reduced = lax.psum_scatter(terms, 'dp', scatter_dimension=0, tiled=False)  75.1 us
    all_gather x1, blocking collectives, on_device(): stack = lax.all_gather(shard, 'dp', axis=0, tiled=False)  66.9 us
    all_to_all x3, blocking collectives, swap(): return lax.all_to_all(value, axis, 0, 0, tiled=True)  31.5 us
    pallas_call x9, Pallas kernels, kernel_call(): pl.pallas_call(run, out_shape=[result if isinstance(item, Near) else pltp...  24 us
    all_to_all x1, starting transfers between devices, swap(): return lax.all_to_all(value, axis, 0, 0, tiled=True)  4.76 us
  transfers between devices with their start and end apart: 4, of which 1 were waited for; matrix products, arithmetic and copies ran while one was open for 1% of the time, Pallas kernels for 5%

profile of v5, /device:TPU:12, one launch (start us, length us, event | category | flops | bytes accessed | tf_op | source)
XLA Modules:
  0.0 219.6 jit_solution(11868351859855139430)
XLA Ops:
  7.2 0.0 collective-permute-start
  7.2 1.7 collective-permute-start.1
  8.9 2.4 %shard_map.154 = (bf16[8,128,128]{2,1,0:T(8,128)(2,1)S(1)}, f32[128,128]{1,0:T(8,128)}) custom-call(s32[1,128]{1,0:T(1,128)} %bitcast.13, bf16[2,128,128]{2,1,0:T(8,128)(2,1)} %refs_1_.2, bf16[2,128,128]{2,1,0:T(8,128)(2,1)} %refs_2_.3, bf16[2,8,2048]{2,1,0:T(8,128)(2,1)} %refs_3_.4, bf16[2,8,2048]{2,1,0:T(8,128)(2,1)} %refs_4_.4), custom_call_target="tpu_custom_call" | custom-call | bytes 590336 | tf_op jit(solution)/shard_map/pallas_call | solution.py:172
  11.4 0.1 multiply_convert_fusion.1
  11.5 66.9 %all-gather.2 = f16[128,128,128]{2,1,0:T(8,128)(2,1)S(1)} all-gather(f16[8,128,128]{2,1,0:T(8,128)(2,1)S(1)} %multiply_convert_fusion.1), channel_id=2, replica_groups=mesh['section'=8,'dp'=16,'tensor'=4] {'dp'}, dimensions={0}, use_global_device_ids=true | all-gather | bytes 4456448 | tf_op jit(solution)/shard_map/all_gather | solution.py:567
  78.3 0.0 copy-start.6
  78.3 1.2 multiply_convert_fusion
  79.6 0.0 copy-start
  79.6 0.0 copy-start.2
  79.6 0.0 copy-start.4
  79.6 0.0 copy-start.5
  79.7 0.0 copy-start.7
  79.7 0.0 collective-permute-done.refs_0_.refs_6_.refs_4_
  79.7 0.0 copy-start.1
  79.7 0.0 collective-permute-done.1.refs_1_.refs_5_
  79.7 0.0 copy-start.3
  79.7 0.0 copy-done.6
  79.7 2.0 shard_map.155
  81.7 13.7 %all_to_all.20.refs_0_.refs_1_ = bf16[4,944,128]{2,1,0:T(8,128)(2,1)S(1)} all-to-all(bf16[4,944,128]{2,1,0:T(8,128)(2,1)S(1)} %shard_map.155), channel_id=1, replica_groups=mesh['section'=8,'dp'=16,'tensor'=4] {'tensor'}, dimensions={0} | all-to-all | bytes 1933312 | tf_op jit(solution)/shard_map/all_to_all | solution.py:538
  95.4 0.0 copy-done.2
  95.4 0.0 copy-done.4
  95.4 0.0 copy-done.5
  95.4 0.0 copy-done.7
  95.4 2.0 shard_map.156
  97.4 0.0 copy-done.1
  97.5 0.0 copy-done.3
  97.5 8.4 %all_to_all.21.refs_0_ = bf16[4,128,128]{2,1,0:T(8,128)(2,1)S(1)} all-to-all(bf16[4,128,128]{2,1,0:T(8,128)(2,1)S(1)} %get-tuple-element.36), channel_id=1, replica_groups=mesh['section'=8,'dp'=16,'tensor'=4] {'tensor'}, dimensions={0} | all-to-all | bytes 262144 | tf_op jit(solution)/shard_map/all_to_all | solution.py:538
  105.8 3.0 %shard_map.157 = (bf16[4,256,128]{2,1,0:T(8,128)(2,1)S(1)}, bf16[128,2048]{1,0:T(8,128)(2,1)}, bf16[128,2048]{1,0:T(8,128)(2,1)}, bf16[3,128,128]{2,1,0:T(8,128)...) custom-call(bf16[4,128,128]{2,1,0:T(8,128)(2,1)S(1)} %all_to_all.21.refs_0_, ...), custom_call_target="tpu_custom_call" | custom-call | flops 800000000 | bytes 12795904 | tf_op jit(solution)/shard_map/pallas_call | solution.py:172
  108.8 9.4 %all_to_all.22.refs_0_ = bf16[4,256,128]{2,1,0:T(8,128)(2,1)S(1)} all-to-all(bf16[4,256,128]{2,1,0:T(8,128)(2,1)S(1)} %get-tuple-element.39), channel_id=1, replica_groups=mesh['section'=8,'dp'=16,'tensor'=4] {'tensor'}, dimensions={0} | all-to-all | bytes 524288 | tf_op jit(solution)/shard_map/all_to_all | solution.py:538
  118.2 0.0 copy-done
  118.3 2.2 shard_map.158
  120.4 4.8 %all-to-all-start.3 = ((bf16[4,128,128]{2,1,0:T(8,128)(2,1)}), bf16[4,128,128]{2,1,0:T(8,128)(2,1)S(1)}, u32[]{:S(2)}, u32[]{:S(2)}) async-start(bf16[4,128,128]{2,1,0:T(8,128)(2,1)} %get-tuple-element.52), calls=%async_computation.3 | async-start | bytes 262144 | tf_op jit(solution)/shard_map/all_to_all | solution.py:538
  125.2 0.0 reduce-scatter.2.cloned.1.call-start
  125.2 6.6 %shard_map.159 = (bf16[16,8,128,128]{3,2,1,0:T(8,128)(2,1)}, bf16[128,2048]{1,0:T(8,128)(2,1)}, f32[128,2048]{1,0:T(8,128)}, bf16[128,2048]{1,0:T(8,128)(2,1)S(1)}) custom-call(bf16[3,128,128]{2,1,0:T(8,128)(2,1)} %get-tuple-element.38.refs_0_, bf16[3,128,128]{2,1,0:T(8,128)(2,1)} %get-tuple-element.42.refs_1_, f32[128,128]{1,0:T(8,128)} %get-tuple-element.43.refs_2_, ...), custom_call_target="tpu_custom_call" | custom-call | flops 1000000000 | bytes 14155776 | tf_op jit(solution)/shard_map/pallas_call | solution.py:172
  131.8 0.0 all-to-all-done.3.refs_0_
  131.8 1.1 shard_map.160
  132.9 0.0 reduce-scatter.2.cloned.1.call-update
  133.0 2.9 %shard_map.161 = bf16[128,2048]{1,0:T(8,128)(2,1)} custom-call(bf16[128,128]{1,0:T(8,128)(2,1)} %get-tuple-element.55.refs_0_, f32[2,128,128]{2,1,0:T(8,128)} %get-tuple-element.50.refs_13_.refs_1_, f32[2,2048]{1,0:T(2,128)} %refs_2_.5, bf16[16,8,128,128]{3,2,1,0:T(8,128)(2,1)} %bitcast.11, bf16[128,2048]{1,0:T(8,128)(2,1)} %copy-done.1, ...), custom_call_target="tpu_custom_call" | custom-call | flops 100000000 | bytes 6471680 | tf_op jit(solution)/shard_map/pallas_call | solution.py:172
  135.8 75.1 %reduce-scatter.2.cloned.1.call-done = bf16[1,8,128,128]{3,2,1,0:T(8,128)(2,1)} async-done(((bf16[16,8,128,128]{3,2,1,0:T(8,128)(2,1)}), bf16[1,8,128,128]{3,2,1,0:T(8,128)(2,1)}) %reduce-scatter.2.cloned.1.call-update) | async-done | bytes 262160 | tf_op jit(solution)/shard_map/reduce_scatter | solution.py:665
  210.9 1.9 shard_map.162
Async XLA Ops:
  7.2 72.5 %collective-permute-start = (bf16[128,2048]{1,0:T(8,128)(2,1)}, bf16[128,2048]{1,0:T(8,128)(2,1)S(1)}, u32[]{:S(2)}, u32[]{:S(2)}) collective-permute-start(bf16[128,2048]{1,0:T(8,128)(2,1)} %param.11), channel_id=1, source_target_pairs={{0,64},{64,128},{128,192},{192,256},{256,320},{320,384},{384,448},... | collective-permute-start | bytes 1572872 | tf_op jit(solution)/shard_map/ppermute | solution.py:27
  7.2 72.5 %collective-permute-start.1 = (bf16[128,2048]{1,0:T(8,128)(2,1)}, bf16[128,2048]{1,0:T(8,128)(2,1)S(1)}, u32[]{:S(2)}, u32[]{:S(2)}) collective-permute-start(bf16[128,2048]{1,0:T(8,128)(2,1)} %param.12), channel_id=1, source_target_pairs={{0,448},{64,0},{128,64},{192,128},{256,192},{320,256},{384,320},{4... | collective-permute-start | bytes 1572872 | tf_op jit(solution)/shard_map/ppermute | solution.py:27
  78.3 1.4 copy-start.6
  79.6 38.6 %copy-start = (bf16[128,128,128]{2,1,0:T(8,128)(2,1)}, bf16[128,128,128]{2,1,0:T(8,128)(2,1)S(1)}, u32[]{:S(2)}) copy-start(bf16[128,128,128]{2,1,0:T(8,128)(2,1)S(1)} %multiply_convert_fusion) | copy-start | bytes 12582916
  79.6 15.8 %copy-start.2 = (bf16[2,128,2048]{2,1,0:T(8,128)(2,1)S(1)}, bf16[2,128,2048]{2,1,0:T(8,128)(2,1)}, u32[]{:S(2)}) copy-start(bf16[2,128,2048]{2,1,0:T(8,128)(2,1)} %refs_3_.7) | copy-start | bytes 3145732
  79.6 15.8 %copy-start.4 = (bf16[2,128,256]{2,1,0:T(8,128)(2,1)S(1)}, bf16[2,128,256]{2,1,0:T(8,128)(2,1)}, u32[]{:S(2)}) copy-start(bf16[2,128,256]{2,1,0:T(8,128)(2,1)} %refs_4_.6) | copy-start | bytes 393220
  79.6 15.8 %copy-start.5 = (bf16[2,128,256]{2,1,0:T(8,128)(2,1)S(1)}, bf16[2,128,256]{2,1,0:T(8,128)(2,1)}, u32[]{:S(2)}) copy-start(bf16[2,128,256]{2,1,0:T(8,128)(2,1)} %refs_5_.3) | copy-start | bytes 393220
  79.7 15.7 %copy-start.7 = (f32[128,128]{1,0:T(8,128)S(1)}, f32[128,128]{1,0:T(8,128)}, u32[]{:S(2)}) copy-start(f32[128,128]{1,0:T(8,128)} %get-tuple-element.35.refs_5_.refs_7_) | copy-start | bytes 196612
  79.7 17.8 %copy-start.1 = (bf16[128,2048]{1,0:T(8,128)(2,1)}, bf16[128,2048]{1,0:T(8,128)(2,1)S(1)}, u32[]{:S(2)}) copy-start(bf16[128,2048]{1,0:T(8,128)(2,1)S(1)} %collective-permute-done.refs_0_.refs_6_.refs_4_) | copy-start | bytes 1572868
  79.7 17.8 %copy-start.3 = (bf16[128,2048]{1,0:T(8,128)(2,1)}, bf16[128,2048]{1,0:T(8,128)(2,1)S(1)}, u32[]{:S(2)}) copy-start(bf16[128,2048]{1,0:T(8,128)(2,1)S(1)} %collective-permute-done.1.refs_1_.refs_5_) | copy-start | bytes 1572868
  120.4 11.4 %all-to-all-start.3 = ((bf16[4,128,128]{2,1,0:T(8,128)(2,1)}), bf16[4,128,128]{2,1,0:T(8,128)(2,1)S(1)}, u32[]{:S(2)}, u32[]{:S(2)}) async-start(bf16[4,128,128]{2,1,0:T(8,128)(2,1)} %get-tuple-element.52), calls=%async_computation.3 | async-start | bytes 262144 | tf_op jit(solution)/shard_map/all_to_all | solution.py:538
  125.2 85.7 %reduce-scatter.2.cloned.1.call-start = ((), (), s32[]{:S(2)}) async-start(), calls=%async_computation.5 | async-start | bytes 4456448 | tf_op jit(solution)/shard_map/reduce_scatter | solution.py:665
Sparse Core Ops, SparseCore 0:
  133.1 77.7 reduce-scatter.1

commit v6 on v5

--- a/solution.py
+++ b/solution.py
@@ -236,15 +236,8 @@
         ).astype(BF16)
 
 
-def pack_body(parent_ref, *refs):
-    downs, ups, targets, bias_ref = refs[:4], refs[4:8], refs[8:16], refs[16]
-    lane = lax.broadcasted_iota(jnp.int32, (128, 128), 1)
-    line = lax.broadcasted_iota(jnp.int32, (128, 128), 0)
-    linked = (lane == line) | (jnp.broadcast_to(parent_ref[...], (128, 128)) == line)
-    reached = jnp.where(linked, 1.0, 0.0).astype(BF16)
-    for _ in range(7):
-        reached = jnp.minimum(dot(reached, reached), 1.0).astype(BF16)
-    bias_ref[...] = jnp.where(jnp.transpose(reached.astype(F32)) > 0.5, 0.0, -1e30)
+def pack_body(*refs):
+    downs, ups, targets = refs[:4], refs[4:8], refs[8:16]
     for ref, target in zip(downs, targets[:4], strict=True):
         target[...] = ref[...]
     for ref, target in zip(ups, targets[4:], strict=True):
@@ -260,25 +253,31 @@
             ).astype(BF16)
 
 
-def unpack_body(came, a_query_ref, b_query_ref, a_out_ref, b_out_ref):
-    for layer in range(2):
-        for ref, place in ((a_query_ref, TERM_A_QUERY), (a_out_ref, TERM_A_OUT)):
-            value = came[place + layer].astype(F32)
+def unpack_body(*refs):
+    for place, (came, ref) in enumerate(zip(refs[:8], refs[8:], strict=True)):
+        value = came[...].astype(F32)
+        if place % 4 < 2:
             for part in range(value.shape[0] // 128):
                 at = slice(part * 128, (part + 1) * 128)
-                ref[layer, at, :] = jnp.transpose(value[at])
-        for ref, place in ((b_query_ref, TERM_B_QUERY), (b_out_ref, TERM_B_OUT)):
-            rows, width = ref.shape[1:]
-            value = came[place + layer].astype(F32)
+                ref[at, :] = jnp.transpose(value[at])
+        else:
+            rows, width = ref.shape
             for tile in range(width // 128):
-                ref[layer, :, tile * 128 : (tile + 1) * 128] = value[
-                    tile * rows : (tile + 1) * rows
-                ]
+                ref[:, tile * 128 : (tile + 1) * 128] = value[tile * rows : (tile + 1) * rows]
+        ref.send()
 
 
 def first_body(
-    hidden_ref, cot_ref, gain0_ref, gain1_ref, down0_ref, down1_ref, up0_ref, up1_ref, sent_ref
+    parent_ref, hidden_ref, cot_ref, gain0_ref, gain1_ref, down0_ref, down1_ref, up0_ref, up1_ref,
+    sent_ref, bias_ref,
 ):
+    lane = lax.broadcasted_iota(jnp.int32, (128, 128), 1)
+    line = lax.broadcasted_iota(jnp.int32, (128, 128), 0)
+    linked = (lane == line) | (jnp.broadcast_to(parent_ref[...], (128, 128)) == line)
+    reached = jnp.where(linked, 1.0, 0.0).astype(BF16)
+    for _ in range(7):
+        reached = jnp.minimum(dot(reached, reached), 1.0).astype(BF16)
+    bias_ref[...] = jnp.where(jnp.transpose(reached.astype(F32)) > 0.5, 0.0, -1e30)
     def send(start, value):
         value = value.astype(BF16)
         for peer in range(sent_ref.shape[0]):
@@ -483,9 +482,8 @@
 
 def terms_body(
     ranks1_ref, ranks2_ref, scale_ref, pull_ref, gain_ref, cot_ref, hidden_ref, up0_ref, down1_ref,
-    up1_ref, attended0_ref, attended1_ref, rank0_ref, back_query0_ref, back_query1_ref, small0_ref,
-    gain0_ref, a_query1, b_query0, b_query1, a_out0, a_out1, b_out0, b_out1, out_ref, gradient_ref,
-    normed0_ref,
+    attended0_ref, attended1_ref, rank0_ref, back_query0_ref, back_query1_ref, small0_ref,
+    gain0_ref, a_query1, b_query0, b_query1, a_out0, a_out1, b_out0, b_out1, normed0_ref,
 ):
     rank_output0, rank_query1, back_output1 = ranks1_ref[0], ranks1_ref[1], ranks1_ref[2]
     rank_output1, back_rank1, back_output0 = ranks2_ref[0], ranks2_ref[1], ranks2_ref[2]
@@ -500,12 +498,8 @@
     a_query1.send()
     gained = gain * dot_cols(back_rank1, read_down(down1_ref))
     gradient = cot.astype(F32) + scale * gained - hidden * pull
-    gradient_ref[...] = gradient
-    gradient_ref.send()
     write_up(b_out0, dot_rows(rank_output0, gradient.astype(BF16)))
     b_out0.send()
-    out_ref[...] = (hidden + dot(rank_output1, read_up(up1_ref))).astype(BF16)
-    out_ref.send()
     write_down(a_out0, dot_rows(back_output0, attended0_ref[...]))
     a_out0.send()
     write_down(a_out1, dot_rows(back_output1, attended1_ref[...]))
@@ -522,15 +516,24 @@
     write_down(a_query0, dot_rows(back_rank, normed_ref[...]))
 
 
-def cot_body(back_rank_ref, small_ref, gain_ref, down_ref, hidden_ref, gradient_ref, cot_ref):
+def rows_body(
+    back_rank_ref, small_ref, gain0_ref, down0_ref, hidden_ref, cot_ref, gain1_ref, scale_ref,
+    pull_ref, ranks1_ref, ranks2_ref, up0_ref, down1_ref, up1_ref, out_ref, cot_send_ref,
+):
+    hidden0 = hidden_ref[...].astype(F32)
+    hidden1 = hidden0 + dot(ranks1_ref[0], read_up(up0_ref))
+    out_ref[...] = (hidden1 + dot(ranks2_ref[0], read_up(up1_ref))).astype(BF16)
+    out_ref.send()
+    gained = gain1_ref[...] * dot_cols(ranks2_ref[1], read_down(down1_ref))
+    gradient = (
+        cot_ref[...].astype(F32) + scale_ref[:, :1] * gained - hidden1 * pull_ref[:, :1]
+    )
     back_rank = back_rank_ref[...]
     scale = small_ref[1, :, :1]
     along = row_sum(back_rank.astype(F32) * small_ref[0]) / D
-    gained = gain_ref[...] * dot_cols(back_rank, read_down(down_ref))
-    cot_ref[...] = (
-        gradient_ref[...]
-        + scale * gained
-        - hidden_ref[...].astype(F32) * (scale * scale * scale * along)
+    gained = gain0_ref[...] * dot_cols(back_rank, read_down(down0_ref))
+    cot_send_ref[...] = (
+        gradient + scale * gained - hidden0 * (scale * scale * scale * along)
     ).astype(BF16)
 
 
@@ -551,16 +554,10 @@
     gain0, gain1 = (gains, [(slice(0, 1),)]), (gains, [(slice(1, 2),)])
     peers = [(tuple(range(ways)),)]
 
-    shard, bias = kernel_call(
+    (shard,) = kernel_call(
         pack_body,
-        [
-            whole(parents.reshape(1, 128)),
-            *[(array, [(0,), (1,)]) for array in (a_query, a_out, b_query, b_out)],
-        ],
-        [
-            Near(shape((8, length, 128), BF16), *[(member,) for member in range(8)]),
-            whole(shape((128, 128), F32)),
-        ],
+        [(array, [(0,), (1,)]) for array in (a_query, a_out, b_query, b_out)],
+        [Near(shape((8, length, 128), BF16), *[(member,) for member in range(8)])],
         0,
     )
     shard = (shard.astype(F32) * SCALE_UP).astype(jnp.float16)
@@ -576,13 +573,13 @@
     hidden = from_behind(arrived, "section", 1)
     cot = from_behind(cot_later, "section", -1)
     near_gain0, near_gain1 = Near(gains, (slice(0, 1),)), Near(gains, (slice(1, 2),))
-    (sent,) = kernel_call(
+    sent, bias = kernel_call(
         first_body,
         [
-            Near(hidden), Near(cot), near_gain0, near_gain1,
+            Near(parents.reshape(1, 128)), Near(hidden), Near(cot), near_gain0, near_gain1,
             near_factor(A_QUERY0, A_QUERY1, B_OUT0, B_OUT1),
         ],
-        [Near(shape((ways, SQUARES + 48, 128), BF16))],
+        [Near(shape((ways, SQUARES + 48, 128), BF16)), Near(shape((128, 128), F32))],
         6e8,
     )
     first = swap(sent, "tensor")
@@ -640,17 +637,15 @@
         TERM_A_QUERY + 1, TERM_B_QUERY, TERM_B_QUERY + 1, TERM_A_OUT, TERM_A_OUT + 1,
         TERM_B_OUT, TERM_B_OUT + 1,
     )
-    terms, section_out, gradient, normed0 = kernel_call(
+    terms, normed0 = kernel_call(
         terms_body,
         [
             whole(ranks1), whole(ranks2), whole(scale1), whole(pull), gain1, whole(cot),
-            whole(hidden), factor(B_OUT0, A_QUERY1, B_OUT1), whole(attended0), whole(attended1),
+            whole(hidden), factor(B_OUT0, A_QUERY1), whole(attended0), whole(attended1),
             whole(rank_query0), whole(back_query0), whole(back_query1), whole(far_small0), gain0,
         ],
         [
             (term_shape, [(ALL, member) for member in made_first]),
-            block,
-            whole(shape((128, width), F32)),
             Near(block[0]),
         ],
         1e9,
@@ -663,24 +658,21 @@
         alias=2,
     )
     reduced = lax.psum_scatter(terms, "dp", scatter_dimension=0, tiled=False)
-    (cot_send,) = kernel_call(
-        cot_body,
+    section_out, cot_send = kernel_call(
+        rows_body,
         [
             whole(back_rank0), whole(far_small0), gain0, factor(A_QUERY0), whole(hidden),
-            whole(gradient),
-        ],
-        [block],
-        1e8,
-    )
+            whole(cot), gain1, whole(scale1), whole(pull), whole(ranks1), whole(ranks2),
+            factor(B_OUT0, A_QUERY1, B_OUT1),
+        ],
+        [block, block],
+        4e8,
+    )
+    down, up = shape((2, length, 128), F32), shape((2, rows, width), F32)
     grads = kernel_call(
         unpack_body,
-        [whole(reduced)],
-        [
-            whole(shape((2, length, 128), F32)),
-            whole(shape((2, rows, width), F32)),
-            whole(shape((2, length, 128), F32)),
-            whole(shape((2, rows, width), F32)),
-        ],
+        [(reduced, [(member,) for member in range(8)])],
+        [(result, [(0,), (1,)]) for result in (down, up, down, up)],
         0,
     )
     return (section_out, cot_send, *grads)

time: 220 us -> 219 us (level)
  the two profiles are of different devices: /device:TPU:12 before, /device:TPU:2 now
where the time goes in v6:
time: 219 us
  blocking collectives  99 us (45%)
  waiting for transfers between devices  74.1 us (34%)
  Pallas kernels  24.5 us (11%)
  between operations  14.3 us (7%)
  starting transfers between devices  5.31 us (2%)
    reduce_scatter x1, waiting for transfers between devices, on_device(): reduced = lax.psum_scatter(terms, 'dp', scatter_dimension=0, tiled=False)  74.1 us
    all_gather x1, blocking collectives, on_device(): stack = lax.all_gather(shard, 'dp', axis=0, tiled=False)  66.9 us
    all_to_all x3, blocking collectives, swap(): return lax.all_to_all(value, axis, 0, 0, tiled=True)  32.1 us
    pallas_call x9, Pallas kernels, kernel_call(): pl.pallas_call(run, out_shape=[result if isinstance(item, Near) else pltp...  24.5 us
  transfers between devices with their start and end apart: 4, of which 1 were waited for; matrix products, arithmetic and copies ran while one was open for 1% of the time, Pallas kernels for 5%

profile of v6, /device:TPU:2, one launch (start us, length us, event | category | flops | bytes accessed | tf_op | source)
XLA Modules:
  0.0 218.5 jit_solution(6247283672923457553)
XLA Ops:
  7.2 0.0 collective-permute-start
  7.2 1.7 collective-permute-start.1
  8.9 0.9 shard_map.154
  9.9 0.1 multiply_convert_fusion.1
  10.0 66.9 %all-gather.2 = f16[128,128,128]{2,1,0:T(8,128)(2,1)S(1)} all-gather(f16[8,128,128]{2,1,0:T(8,128)(2,1)S(1)} %multiply_convert_fusion.1), channel_id=2, replica_groups=mesh['section'=8,'dp'=16,'tensor'=4] {'dp'}, dimensions={0}, use_global_device_ids=true | all-gather | bytes 4456448 | tf_op jit(solution)/shard_map/all_gather | solution.py:564
  76.8 0.0 copy-start.6
  76.8 0.0 copy-start.7
  76.8 1.2 multiply_convert_fusion
  78.1 0.0 copy-start
  78.1 0.0 copy-start.3
  78.1 0.0 copy-start.4
  78.1 0.0 copy-start.5
  78.1 0.0 collective-permute-done.refs_1_.refs_6_.refs_4_
  78.2 0.0 copy-start.1
  78.2 0.0 collective-permute-done.1.refs_2_.refs_5_
  78.2 0.0 copy-start.2
  78.2 0.0 copy-done.6
  78.2 0.0 copy-done.7
  78.2 2.7 %shard_map.155 = (bf16[4,944,128]{2,1,0:T(8,128)(2,1)S(1)}, f32[128,128]{1,0:T(8,128)S(1)}) custom-call(s32[1,128]{1,0:T(1,128)S(1)} %bitcast.13, bf16[128,2048]{1,0:T(8,128)(2,1)S(1)} %collective-permute-done.refs_1_.refs_6_.refs_4_, bf16[128,2048]{1,0:T(8,128)(2,1)S(1)} %collective-permute-done.1.refs_2_.refs_5_, f32[2,2048]{1,0:T(2,128)S(1)} %copy-done.6, ...), custom_call_target="tpu_custom_call" | custom-call | flops 600000000 | bytes 6308352 | tf_op jit(solution)/shard_map/pallas_call | solution.py:172
  81.0 14.7 %all_to_all.20.refs_0_.refs_1_ = bf16[4,944,128]{2,1,0:T(8,128)(2,1)S(1)} all-to-all(bf16[4,944,128]{2,1,0:T(8,128)(2,1)S(1)} %get-tuple-element.34), channel_id=1, replica_groups=mesh['section'=8,'dp'=16,'tensor'=4] {'tensor'}, dimensions={0} | all-to-all | bytes 1933312 | tf_op jit(solution)/shard_map/all_to_all | solution.py:541
  95.7 0.0 copy-done.3
  95.7 0.0 copy-done.4
  95.7 0.0 copy-done.5
  95.7 2.0 shard_map.156
  97.7 0.0 copy-done.1
  97.7 0.0 copy-done.2
  97.7 8.4 %all_to_all.21.refs_0_ = bf16[4,128,128]{2,1,0:T(8,128)(2,1)S(1)} all-to-all(bf16[4,128,128]{2,1,0:T(8,128)(2,1)S(1)} %get-tuple-element.36), channel_id=1, replica_groups=mesh['section'=8,'dp'=16,'tensor'=4] {'tensor'}, dimensions={0} | all-to-all | bytes 262144 | tf_op jit(solution)/shard_map/all_to_all | solution.py:541
  106.1 3.0 %shard_map.157 = (bf16[4,256,128]{2,1,0:T(8,128)(2,1)S(1)}, bf16[128,2048]{1,0:T(8,128)(2,1)}, bf16[128,2048]{1,0:T(8,128)(2,1)}, bf16[3,128,128]{2,1,0:T(8,128)...) custom-call(bf16[4,128,128]{2,1,0:T(8,128)(2,1)S(1)} %all_to_all.21.refs_0_, ...), custom_call_target="tpu_custom_call" | custom-call | flops 800000000 | bytes 12795904 | tf_op jit(solution)/shard_map/pallas_call | solution.py:172
  109.1 9.1 %all_to_all.22.refs_0_ = bf16[4,256,128]{2,1,0:T(8,128)(2,1)S(1)} all-to-all(bf16[4,256,128]{2,1,0:T(8,128)(2,1)S(1)} %get-tuple-element.38), channel_id=1, replica_groups=mesh['section'=8,'dp'=16,'tensor'=4] {'tensor'}, dimensions={0} | all-to-all | bytes 524288 | tf_op jit(solution)/shard_map/all_to_all | solution.py:541
  118.2 0.0 copy-done
  118.2 2.2 shard_map.158
  120.4 3.3 %all-to-all-start.3 = ((bf16[4,128,128]{2,1,0:T(8,128)(2,1)}), bf16[4,128,128]{2,1,0:T(8,128)(2,1)S(1)}, u32[]{:S(2)}, u32[]{:S(2)}) async-start(bf16[4,128,128]{2,1,0:T(8,128)(2,1)} %get-tuple-element.41), calls=%async_computation.3 | async-start | bytes 262144 | tf_op jit(solution)/shard_map/all_to_all | solution.py:541
  123.7 0.2 reduce-scatter.2.cloned.1.call-start
  123.9 5.9 %shard_map.159 = (bf16[16,8,128,128]{3,2,1,0:T(8,128)(2,1)}, bf16[128,2048]{1,0:T(8,128)(2,1)S(1)}) custom-call(bf16[3,128,128]{2,1,0:T(8,128)(2,1)} %get-tuple-element.42.refs_0_.refs_9_, bf16[3,128,128]{2,1,0:T(8,128)(2,1)} %get-tuple-element.43.refs_1_.refs_10_, f32[128,128]{1,0:T(8,128)} %get-tuple-element.44.refs_2_.refs_7_, ...), custom_call_target="tpu_custom_call" | custom-call | flops 1000000000 | bytes 12582912 | tf_op jit(solution)/shard_map/pallas_call | solution.py:172
  129.9 0.0 all-to-all-done.3.refs_0_
  129.9 1.2 shard_map.160
  131.1 0.0 reduce-scatter.2.cloned.1.call-update
  131.1 4.5 %shard_map.161 = (bf16[128,2048]{1,0:T(8,128)(2,1)}, bf16[128,2048]{1,0:T(8,128)(2,1)}) custom-call(bf16[128,128]{1,0:T(8,128)(2,1)} %get-tuple-element.54.refs_0_, f32[2,128,128]{2,1,0:T(8,128)} %get-tuple-element.51.refs_13_.refs_1_, f32[2,2048]{1,0:T(2,128)} %refs_6_.3, bf16[16,8,128,128]{3,2,1,0:T(8,128)(2,1)} %bitcast.11, bf16[128,2048]{1,0:T(8,128)(2,1)} %copy-done.1, ...), custom_call_target="tpu_custom_call" | custom-call | flops 400000000 | bytes 11010048 | tf_op jit(solution)/shard_map/pallas_call | solution.py:172
  135.6 74.1 %reduce-scatter.2.cloned.1.call-done = bf16[1,8,128,128]{3,2,1,0:T(8,128)(2,1)} async-done(((bf16[16,8,128,128]{3,2,1,0:T(8,128)(2,1)}), bf16[1,8,128,128]{3,2,1,0:T(8,128)(2,1)}) %reduce-scatter.2.cloned.1.call-update) | async-done | bytes 262160 | tf_op jit(solution)/shard_map/reduce_scatter | solution.py:660
  209.7 2.0 shard_map.162
Async XLA Ops:
  7.2 71.0 %collective-permute-start = (bf16[128,2048]{1,0:T(8,128)(2,1)}, bf16[128,2048]{1,0:T(8,128)(2,1)S(1)}, u32[]{:S(2)}, u32[]{:S(2)}) collective-permute-start(bf16[128,2048]{1,0:T(8,128)(2,1)} %param.11), channel_id=1, source_target_pairs={{0,64},{64,128},{128,192},{192,256},{256,320},{320,384},{384,448},... | collective-permute-start | bytes 1572872 | tf_op jit(solution)/shard_map/ppermute | solution.py:27
  7.2 71.0 %collective-permute-start.1 = (bf16[128,2048]{1,0:T(8,128)(2,1)}, bf16[128,2048]{1,0:T(8,128)(2,1)S(1)}, u32[]{:S(2)}, u32[]{:S(2)}) collective-permute-start(bf16[128,2048]{1,0:T(8,128)(2,1)} %param.12), channel_id=1, source_target_pairs={{0,448},{64,0},{128,64},{192,128},{256,192},{320,256},{384,320},{4... | collective-permute-start | bytes 1572872 | tf_op jit(solution)/shard_map/ppermute | solution.py:27
  76.8 1.4 copy-start.6
  76.8 1.4 copy-start.7
  78.1 40.1 %copy-start = (bf16[128,128,128]{2,1,0:T(8,128)(2,1)}, bf16[128,128,128]{2,1,0:T(8,128)(2,1)S(1)}, u32[]{:S(2)}) copy-start(bf16[128,128,128]{2,1,0:T(8,128)(2,1)S(1)} %multiply_convert_fusion) | copy-start | bytes 12582916
  78.1 17.6 %copy-start.3 = (bf16[2,128,2048]{2,1,0:T(8,128)(2,1)S(1)}, bf16[2,128,2048]{2,1,0:T(8,128)(2,1)}, u32[]{:S(2)}) copy-start(bf16[2,128,2048]{2,1,0:T(8,128)(2,1)} %refs_3_.7) | copy-start | bytes 3145732
  78.1 17.6 %copy-start.4 = (bf16[2,128,256]{2,1,0:T(8,128)(2,1)S(1)}, bf16[2,128,256]{2,1,0:T(8,128)(2,1)}, u32[]{:S(2)}) copy-start(bf16[2,128,256]{2,1,0:T(8,128)(2,1)} %refs_4_.6) | copy-start | bytes 393220
  78.1 17.6 %copy-start.5 = (bf16[2,128,256]{2,1,0:T(8,128)(2,1)S(1)}, bf16[2,128,256]{2,1,0:T(8,128)(2,1)}, u32[]{:S(2)}) copy-start(bf16[2,128,256]{2,1,0:T(8,128)(2,1)} %refs_5_.3) | copy-start | bytes 393220
  78.2 19.6 %copy-start.1 = (bf16[128,2048]{1,0:T(8,128)(2,1)}, bf16[128,2048]{1,0:T(8,128)(2,1)S(1)}, u32[]{:S(2)}) copy-start(bf16[128,2048]{1,0:T(8,128)(2,1)S(1)} %collective-permute-done.refs_1_.refs_6_.refs_4_) | copy-start | bytes 1572868
  78.2 19.6 %copy-start.2 = (bf16[128,2048]{1,0:T(8,128)(2,1)}, bf16[128,2048]{1,0:T(8,128)(2,1)S(1)}, u32[]{:S(2)}) copy-start(bf16[128,2048]{1,0:T(8,128)(2,1)S(1)} %collective-permute-done.1.refs_2_.refs_5_) | copy-start | bytes 1572868
  120.4 9.5 %all-to-all-start.3 = ((bf16[4,128,128]{2,1,0:T(8,128)(2,1)}), bf16[4,128,128]{2,1,0:T(8,128)(2,1)S(1)}, u32[]{:S(2)}, u32[]{:S(2)}) async-start(bf16[4,128,128]{2,1,0:T(8,128)(2,1)} %get-tuple-element.41), calls=%async_computation.3 | async-start | bytes 262144 | tf_op jit(solution)/shard_map/all_to_all | solution.py:541
  123.7 86.0 %reduce-scatter.2.cloned.1.call-start = ((), (), s32[]{:S(2)}) async-start(), calls=%async_computation.5 | async-start | bytes 4456448 | tf_op jit(solution)/shard_map/reduce_scatter | solution.py:660
Sparse Core Ops, SparseCore 0:
  131.2 78.3 reduce-scatter.1

commit v7 on v6

--- a/solution.py
+++ b/solution.py
@@ -253,18 +253,20 @@
             ).astype(BF16)
 
 
-def unpack_body(*refs):
-    for place, (came, ref) in enumerate(zip(refs[:8], refs[8:], strict=True)):
-        value = came[...].astype(F32)
-        if place % 4 < 2:
+def unpack_body(came, a_query_ref, b_query_ref, a_out_ref, b_out_ref):
+    for layer in range(2):
+        for ref, place in ((a_query_ref, TERM_A_QUERY), (a_out_ref, TERM_A_OUT)):
+            value = came[place + layer].astype(F32)
             for part in range(value.shape[0] // 128):
                 at = slice(part * 128, (part + 1) * 128)
-                ref[at, :] = jnp.transpose(value[at])
-        else:
-            rows, width = ref.shape
+                ref[layer, at, :] = jnp.transpose(value[at])
+        for ref, place in ((b_query_ref, TERM_B_QUERY), (b_out_ref, TERM_B_OUT)):
+            rows, width = ref.shape[1:]
+            value = came[place + layer].astype(F32)
             for tile in range(width // 128):
-                ref[:, tile * 128 : (tile + 1) * 128] = value[tile * rows : (tile + 1) * rows]
-        ref.send()
+                ref[layer, :, tile * 128 : (tile + 1) * 128] = value[
+                    tile * rows : (tile + 1) * rows
+                ]
 
 
 def first_body(
@@ -481,31 +483,32 @@
 
 
 def terms_body(
-    ranks1_ref, ranks2_ref, scale_ref, pull_ref, gain_ref, cot_ref, hidden_ref, up0_ref, down1_ref,
-    attended0_ref, attended1_ref, rank0_ref, back_query0_ref, back_query1_ref, small0_ref,
-    gain0_ref, a_query1, b_query0, b_query1, a_out0, a_out1, b_out0, b_out1, normed0_ref,
+    ranks2_ref, ranks1_ref, scale_ref, pull_ref, small0_ref, rank0_ref, gain0_ref, gain_ref, cot_ref,
+    up0_ref, hidden_ref, down1_ref, back_query1_ref, attended1_ref, attended0_ref, back_query0_ref,
+    a_query1, b_query0, b_query1, a_out0, a_out1, b_out0, b_out1, normed0_ref,
 ):
+    rank_output1, back_rank1, back_output0 = ranks2_ref[0], ranks2_ref[1], ranks2_ref[2]
     rank_output0, rank_query1, back_output1 = ranks1_ref[0], ranks1_ref[1], ranks1_ref[2]
-    rank_output1, back_rank1, back_output0 = ranks2_ref[0], ranks2_ref[1], ranks2_ref[2]
     cot = cot_ref[...]
     write_up(b_out1, dot_rows(rank_output1, cot))
     b_out1.send()
+    write_up(b_query1, dot_rows(rank_query1, back_query1_ref[...]))
+    b_query1.send()
+    write_down(a_out1, dot_rows(back_output1, attended1_ref[...]))
+    a_out1.send()
+    write_down(a_out0, dot_rows(back_output0, attended0_ref[...]))
+    a_out0.send()
+    change = dot(rank_output0, read_up(up0_ref))
     gain, scale, pull = gain_ref[...], scale_ref[:, :1], pull_ref[:, :1]
     hidden = hidden_ref[...].astype(F32)
     normed0_ref[...] = (hidden * small0_ref[1, :, :1] * gain0_ref[...]).astype(BF16)
-    hidden = hidden + dot(rank_output0, read_up(up0_ref))
+    hidden = hidden + change
     write_down(a_query1, dot_rows(back_rank1, (hidden * scale * gain).astype(BF16)))
     a_query1.send()
     gained = gain * dot_cols(back_rank1, read_down(down1_ref))
     gradient = cot.astype(F32) + scale * gained - hidden * pull
     write_up(b_out0, dot_rows(rank_output0, gradient.astype(BF16)))
     b_out0.send()
-    write_down(a_out0, dot_rows(back_output0, attended0_ref[...]))
-    a_out0.send()
-    write_down(a_out1, dot_rows(back_output1, attended1_ref[...]))
-    a_out1.send()
-    write_up(b_query1, dot_rows(rank_query1, back_query1_ref[...]))
-    b_query1.send()
     write_up(b_query0, dot_rows(rank0_ref[...], back_query0_ref[...]))
 
 
@@ -591,7 +594,7 @@
         ],
         [
             Near(shape((ways, 128, 128), BF16)),
-            block,
+            Near(block[0]),
             Near(shape((heads * 128, 128), F32)),
             whole(shape((128, 128), BF16)),
             Near(shape((3, 128, 128), F32)),
@@ -608,8 +611,8 @@
         ],
         [
             Near(shape((ways, 256, 128), BF16)),
-            block,
-            block,
+            Near(block[0]),
+            Near(block[0]),
             whole(shape((3, 128, 128), BF16)),
             Near(shape((4, 128, 128), F32)),
             whole(shape((128, 128), F32)),
@@ -640,9 +643,10 @@
     terms, normed0 = kernel_call(
         terms_body,
         [
-            whole(ranks1), whole(ranks2), whole(scale1), whole(pull), gain1, whole(cot),
-            whole(hidden), factor(B_OUT0, A_QUERY1), whole(attended0), whole(attended1),
-            whole(rank_query0), whole(back_query0), whole(back_query1), whole(far_small0), gain0,
+            whole(ranks2), whole(ranks1), whole(scale1), whole(pull), whole(far_small0),
+            whole(rank_query0), gain0, gain1, Near(cot), factor(B_OUT0), Near(hidden),
+            factor(A_QUERY1), Near(back_query1), Near(attended1), Near(attended0),
+            whole(back_query0),
         ],
         [
             (term_shape, [(ALL, member) for member in made_first]),
@@ -668,11 +672,15 @@
         [block, block],
         4e8,
     )
-    down, up = shape((2, length, 128), F32), shape((2, rows, width), F32)
     grads = kernel_call(
         unpack_body,
-        [(reduced, [(member,) for member in range(8)])],
-        [(result, [(0,), (1,)]) for result in (down, up, down, up)],
+        [whole(reduced)],
+        [
+            whole(shape((2, length, 128), F32)),
+            whole(shape((2, rows, width), F32)),
+            whole(shape((2, length, 128), F32)),
+            whole(shape((2, rows, width), F32)),
+        ],
         0,
     )
     return (section_out, cot_send, *grads)

time: 219 us -> 217 us (level)
  transfers between devices with their start and end apart: 4 -> 4, of which waited for: 1 -> 2; matrix products, arithmetic and copies ran while one was open for 1% -> 1% of each run, Pallas kernels for 5% -> 5%
where the time goes in v7:
time: 217 us
  blocking collectives  99 us (46%)
  waiting for transfers between devices  74.5 us (34%)
  Pallas kernels  22.6 us (10%)
  between operations  14.2 us (7%)
  starting transfers between devices  5.31 us (2%)
    reduce_scatter x1, waiting for transfers between devices, on_device(): reduced = lax.psum_scatter(terms, 'dp', scatter_dimension=0, tiled=False)  73.4 us
    all_gather x1, blocking collectives, on_device(): stack = lax.all_gather(shard, 'dp', axis=0, tiled=False)  66.9 us
    all_to_all x3, blocking collectives, swap(): return lax.all_to_all(value, axis, 0, 0, tiled=True)  32.1 us
    pallas_call x9, Pallas kernels, kernel_call(): pl.pallas_call(run, out_shape=[result if isinstance(item, Near) else pltp...  22.6 us
  transfers between devices with their start and end apart: 4, of which 2 were waited for; matrix products, arithmetic and copies ran while one was open for 1% of the time, Pallas kernels for 5%

profile of v7, /device:TPU:2, one launch (start us, length us, event | category | flops | bytes accessed | tf_op | source)
XLA Modules:
  0.0 217.0 jit_solution(3393671968044049938)
XLA Ops:
  7.2 0.0 collective-permute-start
  7.2 1.7 collective-permute-start.1
  8.9 0.9 shard_map.154
  9.9 0.1 multiply_convert_fusion.1
  10.0 66.9 %all-gather.2 = f16[128,128,128]{2,1,0:T(8,128)(2,1)S(1)} all-gather(f16[8,128,128]{2,1,0:T(8,128)(2,1)S(1)} %multiply_convert_fusion.1), channel_id=2, replica_groups=mesh['section'=8,'dp'=16,'tensor'=4] {'dp'}, dimensions={0}, use_global_device_ids=true | all-gather | bytes 4456448 | tf_op jit(solution)/shard_map/all_gather | solution.py:567
  76.8 0.0 copy-start.6
  76.8 0.0 copy-start.7
  76.8 1.2 multiply_convert_fusion
  78.1 0.0 copy-start
  78.1 0.0 copy-start.3
  78.1 0.0 copy-start.4
  78.1 0.0 copy-start.5
  78.1 0.0 collective-permute-done.refs_1_.refs_10_.refs_4_
  78.2 0.0 copy-start.1
  78.2 0.0 collective-permute-done.1.refs_2_.refs_8_.refs_5_
  78.2 0.0 copy-start.2
  78.2 0.0 copy-done.6
  78.2 0.0 copy-done.7
  78.2 2.7 %shard_map.155 = (bf16[4,944,128]{2,1,0:T(8,128)(2,1)S(1)}, f32[128,128]{1,0:T(8,128)S(1)}) custom-call(s32[1,128]{1,0:T(1,128)S(1)} %bitcast.14, bf16[128,2048]{1,0:T(8,128)(2,1)S(1)} %collective-permute-done.refs_1_.refs_10_.refs_4_, bf16[128,2048]{1,0:T(8,128)(2,1)S(1)} %collective-permute-done.1.refs_2_.refs_8_.refs_5_, f32[2,2048]{1,0:T(2,128)S(1)} %copy-done.6, ...), custom_call_target="tpu_custom_call" | custom-call | flops 600000000 | bytes 6308352 | tf_op jit(solution)/shard_map/pallas_call | solution.py:172
  81.0 14.7 %all_to_all.20.refs_0_.refs_1_ = bf16[4,944,128]{2,1,0:T(8,128)(2,1)S(1)} all-to-all(bf16[4,944,128]{2,1,0:T(8,128)(2,1)S(1)} %get-tuple-element.34), channel_id=1, replica_groups=mesh['section'=8,'dp'=16,'tensor'=4] {'tensor'}, dimensions={0} | all-to-all | bytes 1933312 | tf_op jit(solution)/shard_map/all_to_all | solution.py:544
  95.7 0.0 copy-done.3
  95.7 0.0 copy-done.4
  95.7 0.0 copy-done.5
  95.7 1.9 shard_map.156
  97.6 8.4 %all_to_all.21.refs_0_ = bf16[4,128,128]{2,1,0:T(8,128)(2,1)S(1)} all-to-all(bf16[4,128,128]{2,1,0:T(8,128)(2,1)S(1)} %get-tuple-element.36), channel_id=1, replica_groups=mesh['section'=8,'dp'=16,'tensor'=4] {'tensor'}, dimensions={0} | all-to-all | bytes 262144 | tf_op jit(solution)/shard_map/all_to_all | solution.py:544
  105.9 2.7 %shard_map.157 = (bf16[4,256,128]{2,1,0:T(8,128)(2,1)S(1)}, bf16[128,2048]{1,0:T(8,128)(2,1)S(1)}, bf16[128,2048]{1,0:T(8,128)(2,1)S(1)}, bf16[3,128,128]{2,1,0:...) custom-call(bf16[4,128,128]{2,1,0:T(8,128)(2,1)S(1)} %all_to_all.21.refs_0_, ...), custom_call_target="tpu_custom_call" | custom-call | flops 800000000 | bytes 12795904 | tf_op jit(solution)/shard_map/pallas_call | solution.py:172
  108.7 9.1 %all_to_all.22.refs_0_ = bf16[4,256,128]{2,1,0:T(8,128)(2,1)S(1)} all-to-all(bf16[4,256,128]{2,1,0:T(8,128)(2,1)S(1)} %get-tuple-element.38), channel_id=1, replica_groups=mesh['section'=8,'dp'=16,'tensor'=4] {'tensor'}, dimensions={0} | all-to-all | bytes 524288 | tf_op jit(solution)/shard_map/all_to_all | solution.py:544
  117.7 0.0 copy-done
  117.7 2.2 %shard_map.158 = (bf16[4,128,128]{2,1,0:T(8,128)(2,1)}, bf16[128,2048]{1,0:T(8,128)(2,1)}, bf16[3,128,128]{2,1,0:T(8,128)(2,1)}, f32[128,128]{1,0:T(8,128)}) custom-call(bf16[4,256,128]{2,1,0:T(8,128)(2,1)S(1)} %all_to_all.22.refs_0_, bf16[4,944,128]{2,1,0:T(8,128)(2,1)S(1)} %all_to_all.20.refs_0_.refs_1_, f32[4,128,128]{2,1,0:T(8,128)S(1)} %get-tuple-element.39.refs_2_, ...), custom_call_target="tpu_custom_call" | custom-call | flops 400000000 | bytes 12009472 | tf_op jit(solution)/shard_map/pallas_call | solution.py:172
  119.9 3.3 %all-to-all-start.3 = ((bf16[4,128,128]{2,1,0:T(8,128)(2,1)}), bf16[4,128,128]{2,1,0:T(8,128)(2,1)S(1)}, u32[]{:S(2)}, u32[]{:S(2)}) async-start(bf16[4,128,128]{2,1,0:T(8,128)(2,1)} %get-tuple-element.41), calls=%async_computation.3 | async-start | bytes 262144 | tf_op jit(solution)/shard_map/all_to_all | solution.py:544
  123.3 0.2 reduce-scatter.2.cloned.1.call-start
  123.5 0.0 copy-done.1
  123.5 0.0 copy-done.2
  123.5 4.6 %shard_map.159 = (bf16[16,8,128,128]{3,2,1,0:T(8,128)(2,1)}, bf16[128,2048]{1,0:T(8,128)(2,1)S(1)}) custom-call(bf16[3,128,128]{2,1,0:T(8,128)(2,1)} %get-tuple-element.42.refs_0_.refs_10_, bf16[3,128,128]{2,1,0:T(8,128)(2,1)} %get-tuple-element.43.refs_1_.refs_9_, f32[128,128]{1,0:T(8,128)} %get-tuple-element.44.refs_2_.refs_7_, ...), custom_call_target="tpu_custom_call" | custom-call | flops 1000000000 | bytes 16777216 | tf_op jit(solution)/shard_map/pallas_call | solution.py:172
  128.1 1.1 all-to-all-done.3.refs_0_
  129.2 1.2 shard_map.160
  130.4 0.0 reduce-scatter.2.cloned.1.call-update
  130.4 4.5 %shard_map.161 = (bf16[128,2048]{1,0:T(8,128)(2,1)}, bf16[128,2048]{1,0:T(8,128)(2,1)}) custom-call(bf16[128,128]{1,0:T(8,128)(2,1)} %get-tuple-element.54.refs_0_, f32[2,128,128]{2,1,0:T(8,128)} %get-tuple-element.46.refs_4_.refs_1_, f32[2,2048]{1,0:T(2,128)} %refs_6_.5, bf16[16,8,128,128]{3,2,1,0:T(8,128)(2,1)} %bitcast.12, bf16[128,2048]{1,0:T(8,128)(2,1)} %copy-done.1, ...), custom_call_target="tpu_custom_call" | custom-call | flops 400000000 | bytes 11010048 | tf_op jit(solution)/shard_map/pallas_call | solution.py:172
  134.9 73.4 %reduce-scatter.2.cloned.1.call-done = bf16[1,8,128,128]{3,2,1,0:T(8,128)(2,1)} async-done(((bf16[16,8,128,128]{3,2,1,0:T(8,128)(2,1)}), bf16[1,8,128,128]{3,2,1,0:T(8,128)(2,1)}) %reduce-scatter.2.cloned.1.call-update) | async-done | bytes 262160 | tf_op jit(solution)/shard_map/reduce_scatter | solution.py:664
  208.3 1.9 shard_map.162
Async XLA Ops:
  7.2 71.0 %collective-permute-start = (bf16[128,2048]{1,0:T(8,128)(2,1)}, bf16[128,2048]{1,0:T(8,128)(2,1)S(1)}, u32[]{:S(2)}, u32[]{:S(2)}) collective-permute-start(bf16[128,2048]{1,0:T(8,128)(2,1)} %param.11), channel_id=1, source_target_pairs={{0,64},{64,128},{128,192},{192,256},{256,320},{320,384},{384,448},... | collective-permute-start | bytes 1572872 | tf_op jit(solution)/shard_map/ppermute | solution.py:27
  7.2 71.0 %collective-permute-start.1 = (bf16[128,2048]{1,0:T(8,128)(2,1)}, bf16[128,2048]{1,0:T(8,128)(2,1)S(1)}, u32[]{:S(2)}, u32[]{:S(2)}) collective-permute-start(bf16[128,2048]{1,0:T(8,128)(2,1)} %param.12), channel_id=1, source_target_pairs={{0,448},{64,0},{128,64},{192,128},{256,192},{320,256},{384,320},{4... | collective-permute-start | bytes 1572872 | tf_op jit(solution)/shard_map/ppermute | solution.py:27
  76.8 1.4 copy-start.6
  76.8 1.4 copy-start.7
  78.1 39.7 %copy-start = (bf16[128,128,128]{2,1,0:T(8,128)(2,1)}, bf16[128,128,128]{2,1,0:T(8,128)(2,1)S(1)}, u32[]{:S(2)}) copy-start(bf16[128,128,128]{2,1,0:T(8,128)(2,1)S(1)} %multiply_convert_fusion) | copy-start | bytes 12582916
  78.1 17.6 %copy-start.3 = (bf16[2,128,2048]{2,1,0:T(8,128)(2,1)S(1)}, bf16[2,128,2048]{2,1,0:T(8,128)(2,1)}, u32[]{:S(2)}) copy-start(bf16[2,128,2048]{2,1,0:T(8,128)(2,1)} %refs_3_.7) | copy-start | bytes 3145732
  78.1 17.6 %copy-start.4 = (bf16[2,128,256]{2,1,0:T(8,128)(2,1)S(1)}, bf16[2,128,256]{2,1,0:T(8,128)(2,1)}, u32[]{:S(2)}) copy-start(bf16[2,128,256]{2,1,0:T(8,128)(2,1)} %refs_4_.5) | copy-start | bytes 393220
  78.1 17.6 %copy-start.5 = (bf16[2,128,256]{2,1,0:T(8,128)(2,1)S(1)}, bf16[2,128,256]{2,1,0:T(8,128)(2,1)}, u32[]{:S(2)}) copy-start(bf16[2,128,256]{2,1,0:T(8,128)(2,1)} %refs_5_.3) | copy-start | bytes 393220
  78.2 45.4 %copy-start.1 = (bf16[128,2048]{1,0:T(8,128)(2,1)}, bf16[128,2048]{1,0:T(8,128)(2,1)S(1)}, u32[]{:S(2)}) copy-start(bf16[128,2048]{1,0:T(8,128)(2,1)S(1)} %collective-permute-done.refs_1_.refs_10_.refs_4_) | copy-start | bytes 1572868
  78.2 45.3 %copy-start.2 = (bf16[128,2048]{1,0:T(8,128)(2,1)}, bf16[128,2048]{1,0:T(8,128)(2,1)S(1)}, u32[]{:S(2)}) copy-start(bf16[128,2048]{1,0:T(8,128)(2,1)S(1)} %collective-permute-done.1.refs_2_.refs_8_.refs_5_) | copy-start | bytes 1572868
  119.9 9.3 %all-to-all-start.3 = ((bf16[4,128,128]{2,1,0:T(8,128)(2,1)}), bf16[4,128,128]{2,1,0:T(8,128)(2,1)S(1)}, u32[]{:S(2)}, u32[]{:S(2)}) async-start(bf16[4,128,128]{2,1,0:T(8,128)(2,1)} %get-tuple-element.41), calls=%async_computation.3 | async-start | bytes 262144 | tf_op jit(solution)/shard_map/all_to_all | solution.py:544
  123.3 85.0 %reduce-scatter.2.cloned.1.call-start = ((), (), s32[]{:S(2)}) async-start(), calls=%async_computation.5 | async-start | bytes 4456448 | tf_op jit(solution)/shard_map/reduce_scatter | solution.py:664
Sparse Core Ops, SparseCore 0:
  130.6 77.6 reduce-scatter.1

commit v8 on v7

--- a/solution.py
+++ b/solution.py
@@ -7,7 +7,7 @@
 
 D = 8192
 HEAD_DIM = 128
-HEADS_AT_ONCE = 4
+HEADS_AT_ONCE = 8
 EPSILON = 1e-05
 F32 = jnp.float32
 BF16 = jnp.bfloat16

time: 217 us -> 217 us (level)
  the two profiles are of different devices: /device:TPU:2 before, /device:TPU:12 now
where the time goes in v8:
time: 217 us; the launch traced here: 216 us
  blocking collectives  98.6 us (45%)
  waiting for transfers between devices  73.3 us (34%)
  Pallas kernels  22.4 us (10%)
  between operations  14.2 us (7%)
  starting transfers between devices  6.51 us (3%)
    reduce_scatter x1, waiting for transfers between devices, on_device(): reduced = lax.psum_scatter(terms, 'dp', scatter_dimension=0, tiled=False)  73.3 us
    all_gather x1, blocking collectives, on_device(): stack = lax.all_gather(shard, 'dp', axis=0, tiled=False)  66.9 us
    all_to_all x3, blocking collectives, swap(): return lax.all_to_all(value, axis, 0, 0, tiled=True)  31.7 us
    pallas_call x9, Pallas kernels, kernel_call(): pl.pallas_call(run, out_shape=[result if isinstance(item, Near) else pltp...  22.4 us
    all_to_all x1, starting transfers between devices, swap(): return lax.all_to_all(value, axis, 0, 0, tiled=True)  4.76 us
  transfers between devices with their start and end apart: 4, of which 1 were waited for; matrix products, arithmetic and copies ran while one was open for 1% of the time, Pallas kernels for 5%

profile of v8, /device:TPU:12, one launch (start us, length us, event | category | flops | bytes accessed | tf_op | source)
XLA Modules:
  0.0 216.4 jit_solution(13246479337437326854)
XLA Ops:
  7.2 0.0 collective-permute-start
  7.2 1.7 collective-permute-start.1
  8.9 0.9 shard_map.154
  9.9 0.1 multiply_convert_fusion.1
  10.0 66.9 %all-gather.2 = f16[128,128,128]{2,1,0:T(8,128)(2,1)S(1)} all-gather(f16[8,128,128]{2,1,0:T(8,128)(2,1)S(1)} %multiply_convert_fusion.1), channel_id=2, replica_groups=mesh['section'=8,'dp'=16,'tensor'=4] {'dp'}, dimensions={0}, use_global_device_ids=true | all-gather | bytes 4456448 | tf_op jit(solution)/shard_map/all_gather | solution.py:567
  76.8 0.0 copy-start.6
  76.8 0.0 copy-start.7
  76.8 1.2 multiply_convert_fusion
  78.1 0.0 copy-start
  78.1 0.0 copy-start.3
  78.1 0.0 copy-start.4
  78.1 0.0 copy-start.5
  78.1 0.0 collective-permute-done.refs_1_.refs_10_.refs_4_
  78.2 0.0 copy-start.1
  78.2 0.0 collective-permute-done.1.refs_2_.refs_8_.refs_5_
  78.2 0.0 copy-start.2
  78.2 0.0 copy-done.6
  78.2 0.0 copy-done.7
  78.2 2.7 %shard_map.155 = (bf16[4,944,128]{2,1,0:T(8,128)(2,1)S(1)}, f32[128,128]{1,0:T(8,128)S(1)}) custom-call(s32[1,128]{1,0:T(1,128)S(1)} %bitcast.14, bf16[128,2048]{1,0:T(8,128)(2,1)S(1)} %collective-permute-done.refs_1_.refs_10_.refs_4_, bf16[128,2048]{1,0:T(8,128)(2,1)S(1)} %collective-permute-done.1.refs_2_.refs_8_.refs_5_, f32[2,2048]{1,0:T(2,128)S(1)} %copy-done.6, ...), custom_call_target="tpu_custom_call" | custom-call | flops 600000000 | bytes 6308352 | tf_op jit(solution)/shard_map/pallas_call | solution.py:172
  81.0 13.7 %all_to_all.20.refs_0_.refs_1_ = bf16[4,944,128]{2,1,0:T(8,128)(2,1)S(1)} all-to-all(bf16[4,944,128]{2,1,0:T(8,128)(2,1)S(1)} %get-tuple-element.34), channel_id=1, replica_groups=mesh['section'=8,'dp'=16,'tensor'=4] {'tensor'}, dimensions={0} | all-to-all | bytes 1933312 | tf_op jit(solution)/shard_map/all_to_all | solution.py:544
  94.7 0.0 copy-done.3
  94.7 0.0 copy-done.4
  94.7 0.0 copy-done.5
  94.7 1.9 shard_map.156
  96.6 8.4 %all_to_all.21.refs_0_ = bf16[4,128,128]{2,1,0:T(8,128)(2,1)S(1)} all-to-all(bf16[4,128,128]{2,1,0:T(8,128)(2,1)S(1)} %get-tuple-element.36), channel_id=1, replica_groups=mesh['section'=8,'dp'=16,'tensor'=4] {'tensor'}, dimensions={0} | all-to-all | bytes 262144 | tf_op jit(solution)/shard_map/all_to_all | solution.py:544
  105.0 2.7 %shard_map.157 = (bf16[4,256,128]{2,1,0:T(8,128)(2,1)S(1)}, bf16[128,2048]{1,0:T(8,128)(2,1)S(1)}, bf16[128,2048]{1,0:T(8,128)(2,1)S(1)}, bf16[3,128,128]{2,1,0:...) custom-call(bf16[4,128,128]{2,1,0:T(8,128)(2,1)S(1)} %all_to_all.21.refs_0_, ...), custom_call_target="tpu_custom_call" | custom-call | flops 800000000 | bytes 12795904 | tf_op jit(solution)/shard_map/pallas_call | solution.py:172
  107.7 9.6 %all_to_all.22.refs_0_ = bf16[4,256,128]{2,1,0:T(8,128)(2,1)S(1)} all-to-all(bf16[4,256,128]{2,1,0:T(8,128)(2,1)S(1)} %get-tuple-element.38), channel_id=1, replica_groups=mesh['section'=8,'dp'=16,'tensor'=4] {'tensor'}, dimensions={0} | all-to-all | bytes 524288 | tf_op jit(solution)/shard_map/all_to_all | solution.py:544
  117.3 0.0 copy-done
  117.3 1.9 shard_map.158
  119.2 4.8 %all-to-all-start.3 = ((bf16[4,128,128]{2,1,0:T(8,128)(2,1)}), bf16[4,128,128]{2,1,0:T(8,128)(2,1)S(1)}, u32[]{:S(2)}, u32[]{:S(2)}) async-start(bf16[4,128,128]{2,1,0:T(8,128)(2,1)} %get-tuple-element.41), calls=%async_computation.3 | async-start | bytes 262144 | tf_op jit(solution)/shard_map/all_to_all | solution.py:544
  124.0 0.0 reduce-scatter.2.cloned.1.call-start
  124.0 0.0 copy-done.1
  124.0 0.0 copy-done.2
  124.0 4.6 %shard_map.159 = (bf16[16,8,128,128]{3,2,1,0:T(8,128)(2,1)}, bf16[128,2048]{1,0:T(8,128)(2,1)S(1)}) custom-call(bf16[3,128,128]{2,1,0:T(8,128)(2,1)} %get-tuple-element.42.refs_0_.refs_10_, bf16[3,128,128]{2,1,0:T(8,128)(2,1)} %get-tuple-element.43.refs_1_.refs_9_, f32[128,128]{1,0:T(8,128)} %get-tuple-element.44.refs_2_.refs_7_, ...), custom_call_target="tpu_custom_call" | custom-call | flops 1000000000 | bytes 16777216 | tf_op jit(solution)/shard_map/pallas_call | solution.py:172
  128.6 0.0 all-to-all-done.3.refs_0_
  128.6 1.2 shard_map.160
  129.8 0.0 reduce-scatter.2.cloned.1.call-update
  129.9 4.5 %shard_map.161 = (bf16[128,2048]{1,0:T(8,128)(2,1)}, bf16[128,2048]{1,0:T(8,128)(2,1)}) custom-call(bf16[128,128]{1,0:T(8,128)(2,1)} %get-tuple-element.54.refs_0_, f32[2,128,128]{2,1,0:T(8,128)} %get-tuple-element.46.refs_4_.refs_1_, f32[2,2048]{1,0:T(2,128)} %refs_6_.5, bf16[16,8,128,128]{3,2,1,0:T(8,128)(2,1)} %bitcast.12, bf16[128,2048]{1,0:T(8,128)(2,1)} %copy-done.1, ...), custom_call_target="tpu_custom_call" | custom-call | flops 400000000 | bytes 11010048 | tf_op jit(solution)/shard_map/pallas_call | solution.py:172
  134.3 73.3 %reduce-scatter.2.cloned.1.call-done = bf16[1,8,128,128]{3,2,1,0:T(8,128)(2,1)} async-done(((bf16[16,8,128,128]{3,2,1,0:T(8,128)(2,1)}), bf16[1,8,128,128]{3,2,1,0:T(8,128)(2,1)}) %reduce-scatter.2.cloned.1.call-update) | async-done | bytes 262160 | tf_op jit(solution)/shard_map/reduce_scatter | solution.py:664
  207.7 1.9 shard_map.162
Async XLA Ops:
  7.2 71.0 %collective-permute-start = (bf16[128,2048]{1,0:T(8,128)(2,1)}, bf16[128,2048]{1,0:T(8,128)(2,1)S(1)}, u32[]{:S(2)}, u32[]{:S(2)}) collective-permute-start(bf16[128,2048]{1,0:T(8,128)(2,1)} %param.11), channel_id=1, source_target_pairs={{0,64},{64,128},{128,192},{192,256},{256,320},{320,384},{384,448},... | collective-permute-start | bytes 1572872 | tf_op jit(solution)/shard_map/ppermute | solution.py:27
  7.2 71.0 %collective-permute-start.1 = (bf16[128,2048]{1,0:T(8,128)(2,1)}, bf16[128,2048]{1,0:T(8,128)(2,1)S(1)}, u32[]{:S(2)}, u32[]{:S(2)}) collective-permute-start(bf16[128,2048]{1,0:T(8,128)(2,1)} %param.12), channel_id=1, source_target_pairs={{0,448},{64,0},{128,64},{192,128},{256,192},{320,256},{384,320},{4... | collective-permute-start | bytes 1572872 | tf_op jit(solution)/shard_map/ppermute | solution.py:27
  76.8 1.4 copy-start.6
  76.8 1.4 copy-start.7
  78.1 39.2 %copy-start = (bf16[128,128,128]{2,1,0:T(8,128)(2,1)}, bf16[128,128,128]{2,1,0:T(8,128)(2,1)S(1)}, u32[]{:S(2)}) copy-start(bf16[128,128,128]{2,1,0:T(8,128)(2,1)S(1)} %multiply_convert_fusion) | copy-start | bytes 12582916
  78.1 16.6 %copy-start.3 = (bf16[2,128,2048]{2,1,0:T(8,128)(2,1)S(1)}, bf16[2,128,2048]{2,1,0:T(8,128)(2,1)}, u32[]{:S(2)}) copy-start(bf16[2,128,2048]{2,1,0:T(8,128)(2,1)} %refs_3_.7) | copy-start | bytes 3145732
  78.1 16.5 %copy-start.4 = (bf16[2,128,256]{2,1,0:T(8,128)(2,1)S(1)}, bf16[2,128,256]{2,1,0:T(8,128)(2,1)}, u32[]{:S(2)}) copy-start(bf16[2,128,256]{2,1,0:T(8,128)(2,1)} %refs_4_.5) | copy-start | bytes 393220
  78.1 16.5 %copy-start.5 = (bf16[2,128,256]{2,1,0:T(8,128)(2,1)S(1)}, bf16[2,128,256]{2,1,0:T(8,128)(2,1)}, u32[]{:S(2)}) copy-start(bf16[2,128,256]{2,1,0:T(8,128)(2,1)} %refs_5_.3) | copy-start | bytes 393220
  78.2 45.8 %copy-start.1 = (bf16[128,2048]{1,0:T(8,128)(2,1)}, bf16[128,2048]{1,0:T(8,128)(2,1)S(1)}, u32[]{:S(2)}) copy-start(bf16[128,2048]{1,0:T(8,128)(2,1)S(1)} %collective-permute-done.refs_1_.refs_10_.refs_4_) | copy-start | bytes 1572868
  78.2 45.8 %copy-start.2 = (bf16[128,2048]{1,0:T(8,128)(2,1)}, bf16[128,2048]{1,0:T(8,128)(2,1)S(1)}, u32[]{:S(2)}) copy-start(bf16[128,2048]{1,0:T(8,128)(2,1)S(1)} %collective-permute-done.1.refs_2_.refs_8_.refs_5_) | copy-start | bytes 1572868
  119.2 9.4 %all-to-all-start.3 = ((bf16[4,128,128]{2,1,0:T(8,128)(2,1)}), bf16[4,128,128]{2,1,0:T(8,128)(2,1)S(1)}, u32[]{:S(2)}, u32[]{:S(2)}) async-start(bf16[4,128,128]{2,1,0:T(8,128)(2,1)} %get-tuple-element.41), calls=%async_computation.3 | async-start | bytes 262144 | tf_op jit(solution)/shard_map/all_to_all | solution.py:544
  124.0 83.7 %reduce-scatter.2.cloned.1.call-start = ((), (), s32[]{:S(2)}) async-start(), calls=%async_computation.5 | async-start | bytes 4456448 | tf_op jit(solution)/shard_map/reduce_scatter | solution.py:664
Sparse Core Ops, SparseCore 0:
  130.0 77.6 reduce-scatter.1
